TPU v7x, 32 devices: a whole 2x2x4 slice. The times are simulated.
32 devices in a mesh: req: 16 (over z, x, core), head: 2 (over y).
Axes of the slice: x: 2, y: 2, z: 4, core: 2. Of those that a mesh axis runs over, the one named last changes fastest.
Arguments:
- draft_ids: int32 [256, 16], P('req'), may hold values from 0 to 63999
- worker_slot: int32 [256], P('req'), may hold values from 0 to 255, as said below
- accepted: int32 [256], P('req'), may hold values from 0 to 16
- embedding: bfloat16 [64000, 2048], P('req', 'head'), may hold values from -120 to 120
- w_query: bfloat16 [2048, 2048], P('req', 'head'), may hold values from -0.125 to 0.125
- w_key: bfloat16 [2048, 2048], P('req', 'head'), may hold values from -0.125 to 0.125
- w_value: bfloat16 [2048, 4096], P('req', 'head'), may hold values from -0.125 to 0.125
- w_gate: bfloat16 [2048, 4096], P('req', 'head'), may hold values from -0.125 to 0.125
- old_state: bfloat16 [256, 8, 256, 512], P('req', 'head'), may hold values from -4 to 4
Outputs:
- hidden: bfloat16 [256, 16, 4096], P('req', None, 'head')
- new_state: bfloat16 [256, 8, 256, 512], P('req', 'head')
Inputs may be any that keep to these rules, and one draw needn't show every extreme that they name: worker_slot is a permutation of 0 to 255; request r is handled by worker worker_slot[r] // 16 at position worker_slot[r] % 16; the 16 requests of one owner (aligned blocks of 16) go to 16 different workers.
All inputs are finite; a program needn't handle non-finite values.
Results may differ from a plain program's by a relative error of at most 0.0095.
Values may be sent and summed in bfloat16 or wider, within the bound.
No kernel may reach another device: no remote copies, remote signals or barrier semaphores. Data moves between devices by JAX's collectives and lax.ppermute only.
A program may use at most 192 MiB of HBM per device.

v0:
```python
import jax
import jax.numpy as jnp
from jax import lax
from jax.sharding import PartitionSpec as P


def layer_norm(values):
    center = jnp.mean(values, axis=-1, keepdims=True)
    shifted = values - center
    spread = jnp.mean(shifted * shifted, axis=-1, keepdims=True)
    return shifted * lax.rsqrt(spread + 1e-05)


def add_rows(normed, piece):
    return jnp.dot(normed, piece, preferred_element_type=jnp.float32)


def retention(queries, keys_scaled, values_all, gates_all, start_state, counts_int, head_ids):
    row_count = queries.shape[0]
    draft_len = queries.shape[1]
    heads_dev = start_state.shape[1]
    key_dim = start_state.shape[2]
    value_dim = start_state.shape[3]
    query_heads = queries.reshape(row_count, draft_len, heads_dev, key_dim)
    key_heads = keys_scaled.reshape(row_count, draft_len, heads_dev, key_dim)
    value_heads = values_all.reshape(row_count, draft_len, heads_dev, value_dim)
    gate_heads = gates_all.reshape(row_count, draft_len, heads_dev, value_dim)
    decay_rate = 1.0 - jnp.exp2(-5.0 - head_ids)
    positions = jnp.arange(draft_len, dtype=jnp.float32)
    distance = positions[:, None] - positions[None, :]
    causal = distance >= 0.0
    decay_mask = jnp.where(
        causal[None], jnp.power(decay_rate[:, None, None], jnp.maximum(distance, 0.0)[None]), 0.0
    )
    scores = (
        jnp.einsum("nthk,nshk->nhts", query_heads, key_heads, preferred_element_type=jnp.float32)
        * decay_mask[None]
    )
    weights = scores.astype(jnp.bfloat16)
    inside_terms = jnp.einsum(
        "nhts,nshv->nthv", weights, value_heads, preferred_element_type=jnp.float32
    )
    state_terms = jnp.einsum(
        "nthk,nhkv->nthv", query_heads, start_state, preferred_element_type=jnp.float32
    )
    state_terms = (
        state_terms * jnp.power(decay_rate[None, :], positions[:, None] + 1.0)[None, :, :, None]
    )
    mixture = layer_norm(inside_terms + state_terms)
    hidden = (jax.nn.silu(gate_heads.astype(jnp.float32)) * mixture).astype(jnp.bfloat16)
    hidden = hidden.reshape(row_count, draft_len, heads_dev * value_dim)
    counts = counts_int.astype(jnp.float32)[:, None]
    remaining = jnp.maximum(counts - 1.0 - positions[None, :], 0.0)
    within = positions[None, :] < counts
    scale_rows = jnp.where(
        within[:, :, None], jnp.power(decay_rate[None, None, :], remaining[:, :, None]), 0.0
    )
    kept_keys = (key_heads.astype(jnp.float32) * scale_rows[..., None]).astype(jnp.bfloat16)
    updated = jnp.einsum(
        "nshk,nshv->nhkv", kept_keys, value_heads, preferred_element_type=jnp.float32
    )
    updated = updated + jnp.power(decay_rate[None, :], counts)[
        :, :, None, None
    ] * start_state.astype(jnp.float32)
    return (hidden, updated.astype(jnp.bfloat16))


def per_device(
    draft_ids, worker_slot, accepted, embedding, w_query, w_key, w_value, w_gate, old_state
):
    own_rows = worker_slot.shape[0]
    width_req = lax.axis_size("req")
    my_index = lax.axis_index("req")
    all_ids, all_slots, all_counts = (
        lax.all_gather(draft_ids, "req", axis=0, tiled=True),
        lax.all_gather(worker_slot, "req", axis=0, tiled=True),
        lax.all_gather(accepted, "req", axis=0, tiled=True),
    )
    total_rows = all_slots.shape[0]
    holder = (
        jnp.zeros((total_rows,), jnp.int32)
        .at[all_slots]
        .set(jnp.arange(total_rows, dtype=jnp.int32))
    )
    vocab_rows = embedding.shape[0]
    local_ids = all_ids - my_index * vocab_rows
    inside = (local_ids >= 0) & (local_ids < vocab_rows)
    looked = jnp.take(embedding, jnp.clip(local_ids, 0, vocab_rows - 1), axis=0)
    partial_rows = jnp.where(inside[:, :, None], looked.astype(jnp.float32), 0.0)
    token_cols = lax.psum_scatter(
        partial_rows.astype(jnp.bfloat16), "req", scatter_dimension=0, tiled=True
    )
    tokens = lax.all_gather(token_cols, "head", axis=2, tiled=True)
    draft_len = tokens.shape[1]
    normed = (
        layer_norm(tokens.astype(jnp.float32))
        .astype(jnp.bfloat16)
        .reshape(own_rows * draft_len, tokens.shape[2])
    )

    def add_one(piece):
        return add_rows(normed, piece)

    raw_query = add_one(lax.all_gather(w_query, "req", axis=0, tiled=True))
    raw_key = add_one(lax.all_gather(w_key, "req", axis=0, tiled=True))
    raw_value = add_one(lax.all_gather(w_value, "req", axis=0, tiled=True))
    raw_gate = add_one(lax.all_gather(w_gate, "req", axis=0, tiled=True))
    key_scale = old_state.shape[2] ** (-0.5)
    queries = raw_query.astype(jnp.bfloat16).reshape(own_rows, draft_len, -1)
    keys_scaled = (raw_key * key_scale).astype(jnp.bfloat16).reshape(own_rows, draft_len, -1)
    values_all = raw_value.astype(jnp.bfloat16).reshape(own_rows, draft_len, -1)
    gates_all = raw_gate.astype(jnp.bfloat16).reshape(own_rows, draft_len, -1)
    heads_dev = old_state.shape[1]
    head_ids = (lax.axis_index("head") * heads_dev + jnp.arange(heads_dev, dtype=jnp.int32)).astype(
        jnp.float32
    )
    my_requests = lax.dynamic_slice_in_dim(holder, my_index * own_rows, own_rows)
    source = my_requests // own_rows
    target = worker_slot // own_rows
    to_worker = (
        jnp.zeros((width_req,), jnp.int32).at[target].set(jnp.arange(own_rows, dtype=jnp.int32))
    )
    answer, new_state = retention(
        queries, keys_scaled, values_all, gates_all, old_state, accepted, head_ids
    )
    received = lax.all_to_all(
        jnp.take(answer, to_worker, axis=0), "req", split_axis=0, concat_axis=0, tiled=True
    )
    hidden = jnp.take(received, source, axis=0)
    return (hidden, new_state)


def solution(mesh):
    return jax.shard_map(
        per_device,
        mesh=mesh,
        in_specs=(
            P("req", None),
            P("req"),
            P("req"),
            P("req", "head"),
            P("req", "head"),
            P("req", "head"),
            P("req", "head"),
            P("req", "head"),
            P("req", "head", None, None),
        ),
        out_specs=(P("req", None, "head"), P("req", "head", None, None)),
        check_vma=False,
    )
```

profile of v0, /device:TPU:9, one launch (start us, length us, event | category | flops | bytes accessed | tf_op | source)
XLA Modules:
  0.0 497.8 jit_solution(5932785029727653407)
XLA Ops:
  7.2 19.9 %all_gather.21 = s32[256,16]{1,0:T(8,128)S(1)} all-gather(s32[16,16]{1,0:T(8,128)} %param.11), channel_id=1, replica_groups=mesh['req'=16,'head'=2] {'req'}, dimensions={0}, use_global_device_ids=true | all-gather | bytes 17408 | tf_op jit(solution)/shard_map/all_gather | solution.py:75
  27.7 25.2 %gather_fusion = bf16[4096,1024]{1,0:T(8,128)(2,1)} fusion(bf16[4000,1024]{1,0:T(8,128)(2,1)} %param.14, s32[4096]{0:T(1024)S(1)} %broadcast_clamp_fusion), kind=kCustom, calls=%fused_computation.2 | custom fusion | bytes 16793600 | tf_op jit(solution)/shard_map/jit(_take)/gather | solution.py:88
  52.9 7.9 %select_convert_fusion = bf16[256,16,1024]{2,1,0:T(8,128)(2,1)} fusion(bf16[256,16,1024]{2,1,0:T(8,128)(2,1)} %bitcast.21, pred[256,16]{1,0:T(8,128)(4,1)S(1)} %copy.42, pred[256,16]{1,0:T(8,128)(4,1)S(1)} %copy.41), kind=kLoop, calls=%fused_computation.6 | loop fusion | flops 16777216 | bytes 16785408 | tf_op jit(solution)/shard_map/convert_element_type | solution.py:91
  60.9 104.3 %reduce-scatter.2.cloned.1.call-done = bf16[16,16,1024]{2,1,0:T(8,128)(2,1)} async-done(((bf16[256,16,1024]{2,1,0:T(8,128)(2,1)}), bf16[16,16,1024]{2,1,0:T(8,128)(2,1)}) %reduce-scatter.2.cloned.1.call-update) | async-done | bytes 524304 | tf_op jit(solution)/shard_map/reduce_scatter | solution.py:90
  165.2 0.7 all-gather.12.cloned.1.call-update
  170.0 8.3 %all-reduce = s32[256]{0:T(256)S(1)} all-reduce(s32[256]{0:T(256)S(1)} %dynamic-update-slice), channel_id=1, replica_groups=mesh['req'=16,'head'=2] {'req'}, use_global_device_ids=true, to_apply=%add | all-reduce | flops 256 | bytes 2048
  178.4 1.4 scatter_custom_fusion.1
  180.1 7.6 %all-gather.6.cloned.1.call-done = bf16[16,16,2048]{2,1,0:T(8,128)(2,1)} async-done(((bf16[16,16,1024]{2,1,0:T(8,128)(2,1)}), bf16[16,16,2048]{2,1,0:T(8,128)(2,1)}) %all-gather.6.cloned.1.call-update) | async-done | bytes 1048592 | tf_op jit(solution)/shard_map/all_gather | solution.py:93
  187.7 1.4 convert_reduce_fusion
  189.2 1.6 fusion.3
  190.8 1.6 fusion.4
  192.4 48.7 %all-gather.12.cloned.1.call-done = bf16[2048,1024]{1,0:T(8,128)(2,1)} async-done(((bf16[128,1024]{1,0:T(8,128)(2,1)}), bf16[2048,1024]{1,0:T(8,128)(2,1)}) %all-gather.12.cloned.1.call-update) | async-done | bytes 4194320 | tf_op jit(solution)/shard_map/all_gather | solution.py:104
  241.1 3.4 convolution_convert_fusion.2
  244.9 47.3 %all-gather.14.cloned.1.call-done = bf16[2048,1024]{1,0:T(8,128)(2,1)} async-done(((bf16[128,1024]{1,0:T(8,128)(2,1)}), bf16[2048,1024]{1,0:T(8,128)(2,1)}) %all-gather.14.cloned.1.call-update) | async-done | bytes 4194320 | tf_op jit(solution)/shard_map/all_gather | solution.py:105
  292.2 3.4 fusion.6
  295.6 1.2 reshape_reshape.12
  296.8 9.9 %fusion.15 = f32[16,4,16,512]{3,2,1,0:T(8,128)} fusion(bf16[16,4,256,512]{3,2,1,0:T(8,128)(2,1)} %param.19, bf16[16,16,4,256]{3,2,1,0:T(4,128)(2,1)S(1)} %reshape_reshape.11), kind=kOutput, calls=%fused_computation.34 | convolution fusion | flops 268435456 | bytes 19398656 | tf_op jit(solution)/shard_map/nthk,nhkv->nthv/dot_general | solution.py:43
  306.8 60.3 %all-gather.10.cloned.1.call-done = bf16[2048,2048]{1,0:T(8,128)(2,1)} async-done(((bf16[128,2048]{1,0:T(8,128)(2,1)}), bf16[2048,2048]{1,0:T(8,128)(2,1)}) %all-gather.10.cloned.1.call-update) | async-done | bytes 8388624 | tf_op jit(solution)/shard_map/all_gather | solution.py:106
  367.0 6.7 %convolution_convert_fusion = bf16[256,2048]{1,0:T(8,128)(2,1)} fusion(bf16[256,2048]{1,0:T(8,128)(2,1)S(1)} %bitcast.25, bf16[2048,2048]{1,0:T(8,128)(2,1)} %all-gather.10.cloned.1.call-done), kind=kOutput, calls=%fused_computation.9 | convolution fusion | flops 2148007936 | bytes 10485760 | tf_op jit(solution)/shard_map/dot_general | solution.py:15
  373.7 1.8 reshape_reshape.10
  375.6 2.8 fusion.26
  378.9 63.3 %all-gather.8.cloned.1.call-done = bf16[2048,2048]{1,0:T(8,128)(2,1)} async-done(((bf16[128,2048]{1,0:T(8,128)(2,1)}), bf16[2048,2048]{1,0:T(8,128)(2,1)}) %all-gather.8.cloned.1.call-update) | async-done | bytes 8388624 | tf_op jit(solution)/shard_map/all_gather | solution.py:107
  442.2 7.4 %fusion = f32[256,2048]{1,0:T(8,128)} fusion(bf16[256,2048]{1,0:T(8,128)(2,1)} %bitcast.26, bf16[2048,2048]{1,0:T(8,128)(2,1)} %all-gather.8.cloned.1.call-done), kind=kOutput, calls=%fused_computation.11 | convolution fusion | flops 2148532224 | bytes 11534336 | tf_op jit(solution)/shard_map/dot_general | solution.py:15
  449.6 3.7 reshape.209
  453.3 2.5 fusion.8
  455.8 1.1 copy.54
  456.9 1.8 gather_fusion.1
  458.7 1.1 broadcast_select_fusion.1
  459.8 4.5 all-to-all-start
  464.6 19.5 %add_convert_fusion = bf16[16,4,256,512]{3,2,1,0:T(8,128)(2,1)} fusion(bf16[16,4,256,512]{3,2,1,0:T(8,128)(2,1)} %param.19, f32[16,4]{1,0:T(8,128)S(1)} %copy.53, bf16[16,16,4,512]{3,2,1,0:T(4,128)(2,1)S(1)} %reshape_reshape.10, f32[16,16,4]{1,2,0:T(4,128)S(1)} %power_select_fusion, bf16[16,16,4,256]{3,2,1,0:T(4,128)(2,1)S(1)} %copy-done.1), kind=kOutput, calls=%fused_computation.5 | convolution fusion | flops 302776320 | bytes 35131648 | tf_op jit(solution)/shard_map/nshk,nshv->nhkv/dot_general | solution.py:59
  484.1 5.1 %all-to-all-done = bf16[16,16,2048]{2,1,0:T(8,128)(2,1)S(1)} async-done(((bf16[16,16,2048]{2,1,0:T(8,128)(2,1)}), bf16[16,16,2048]{2,1,0:T(8,128)(2,1)S(1)}, u32[]{:S(2)}, u32[]{:S(2)}) %all-to-all-start) | async-done | bytes 1048608 | tf_op jit(solution)/shard_map/all_to_all | solution.py:126
  489.8 1.1 broadcast_select_fusion
  (62 shorter events, 6.2 us)
Async XLA Ops:
  7.2 158.0 %reduce-scatter.2.cloned.1.call-start = ((), (), s32[]{:S(2)}) async-start(), calls=%async_computation.2 | async-start | bytes 8912896 | tf_op jit(solution)/shard_map/reduce_scatter | solution.py:90
  60.8 106.9 %copy-start.4 = (s32[16]{0:T(128)S(1)}, s32[16]{0:T(128)}, u32[]{:S(2)}) copy-start(s32[16]{0:T(128)} %param.13) | copy-start | bytes 196
  60.8 107.1 %copy-start.3 = (s32[16]{0:T(128)S(1)}, s32[16]{0:T(128)}, u32[]{:S(2)}) copy-start(s32[16]{0:T(128)} %param.12) | copy-start | bytes 196
  60.8 107.7 %copy-start.5 = (u32[32]{0:T(128)S(1)}, u32[32]{0:T(128)}, u32[]{:S(2)}) copy-start(u32[32]{0:T(128)} %constant.98) | copy-start | bytes 388
  60.8 126.9 %all-gather.6.cloned.1.call-start = ((), (), s32[]{:S(2)}) async-start(), calls=%async_computation.3 | async-start | bytes 1572864 | tf_op jit(solution)/shard_map/all_gather | solution.py:93
  165.2 75.9 %all-gather.12.cloned.1.call-start = ((), (), s32[]{:S(2)}) async-start(), calls=%async_computation.6 | async-start | bytes 4456448 | tf_op jit(solution)/shard_map/all_gather | solution.py:104
  165.9 126.3 %all-gather.14.cloned.1.call-start = ((), (), s32[]{:S(2)}) async-start(), calls=%async_computation.7 | async-start | bytes 4456448 | tf_op jit(solution)/shard_map/all_gather | solution.py:105
  166.5 200.6 %all-gather.10.cloned.1.call-start = ((), (), s32[]{:S(2)}) async-start(), calls=%async_computation.5 | async-start | bytes 8912896 | tf_op jit(solution)/shard_map/all_gather | solution.py:106
  167.1 275.2 %all-gather.8.cloned.1.call-start = ((), (), s32[]{:S(2)}) async-start(), calls=%async_computation.4 | async-start | bytes 8912896 | tf_op jit(solution)/shard_map/all_gather | solution.py:107
  192.4 174.6 %copy-start.2 = (bf16[16,16,2048]{2,1,0:T(8,128)(2,1)}, bf16[16,16,2048]{2,1,0:T(8,128)(2,1)S(1)}, u32[]{:S(2)}) copy-start(bf16[16,16,2048]{2,1,0:T(8,128)(2,1)S(1)} %fusion.4) | copy-start | bytes 3145732
  244.9 51.9 %copy-start = (bf16[16,16,4,256]{3,2,1,0:T(4,128)(2,1)}, bf16[16,16,4,256]{3,2,1,0:T(4,128)(2,1)S(1)}, u32[]{:S(2)}) copy-start(bf16[16,16,4,256]{3,2,1,0:T(4,128)(2,1)S(1)} %reshape_reshape.11) | copy-start | bytes 1572868
  455.8 8.8 %copy-start.1 = (bf16[16,16,4,256]{3,2,1,0:T(4,128)(2,1)S(1)}, bf16[16,16,4,256]{3,2,1,0:T(4,128)(2,1)}, u32[]{:S(2)}) copy-start(bf16[16,16,4,256]{3,2,1,0:T(4,128)(2,1)} %reshape_reshape.12) | copy-start | bytes 1572868
  459.8 29.4 %all-to-all-start = ((bf16[16,16,2048]{2,1,0:T(8,128)(2,1)}), bf16[16,16,2048]{2,1,0:T(8,128)(2,1)S(1)}, u32[]{:S(2)}, u32[]{:S(2)}) async-start(bf16[16,16,2048]{2,1,0:T(8,128)(2,1)} %broadcast_select_fusion.1), calls=%async_computation.1 | async-start | bytes 2097152 | tf_op jit(solution)/shard_map/all_to_all | solution.py:126
Sparse Core Ops, SparseCore 0:
  60.9 104.1 reduce-scatter.1
  166.7 21.0 all-gather.5
  189.9 51.1 all-gather.11
  243.1 49.0 all-gather.13
  294.2 72.7 all-gather.9
  369.0 73.1 all-gather.7
where the time goes:
time: 499 us; the launch traced here: 498 us
  waiting for transfers between devices  339 us (68%)
  matrix products  53.1 us (11%)
  local copies, waits for them, and re-layouts  39.3 us (8%)
  blocking collectives  28.2 us (6%)
  other arithmetic  18.4 us (4%)
  between operations  15.1 us (3%)
    reduce_scatter x1, waiting for transfers between devices, per_device(): lax.psum_scatter(partial_rows.astype(jnp.bfloat16), 'req', scatter_dimens...  104 us
    all_gather x1, waiting for transfers between devices, per_device(): raw_gate = add_one(lax.all_gather(w_gate, 'req', axis=0, tiled=True))  63.3 us
    all_gather x1, waiting for transfers between devices, per_device(): raw_value = add_one(lax.all_gather(w_value, 'req', axis=0, tiled=True))  60.3 us
    all_gather x1, waiting for transfers between devices, per_device(): raw_query = add_one(lax.all_gather(w_query, 'req', axis=0, tiled=True))  48.7 us
    all_gather x1, waiting for transfers between devices, per_device(): raw_key = add_one(lax.all_gather(w_key, 'req', axis=0, tiled=True))  47.3 us
    gather x1, local copies, waits for them, and re-layouts, per_device(): looked = jnp.take(embedding, jnp.clip(local_ids, 0, vocab_rows - 1), axis=0)  25.2 us
    dot_general x4, matrix products, add_rows(): return jnp.dot(normed, piece, preferred_element_type=jnp.float32)  20.9 us
    all_gather x1, blocking collectives, per_device(): lax.all_gather(draft_ids, 'req', axis=0, tiled=True)  19.9 us
  transfers between devices with their start and end apart: 7, of which 7 were waited for; matrix products, arithmetic and copies ran while one was open for 12% of the time, Pallas kernels for 0%

commit v1 on v0

v1 whole, which is shorter than its diff:
```python
import jax
import jax.numpy as jnp
from jax import lax
from jax.experimental import pallas as pl
from jax.experimental.pallas import tpu as pltpu
from jax.sharding import PartitionSpec as P

ZLEN = 4


def layer_norm(values):
    center = jnp.mean(values, axis=-1, keepdims=True)
    shifted = values - center
    spread = jnp.mean(shifted * shifted, axis=-1, keepdims=True)
    return shifted * lax.rsqrt(spread + 1e-05)


def retention(queries, keys_scaled, values_all, gates_all, start_state, counts_int, head_ids):
    row_count = queries.shape[0]
    draft_len = queries.shape[1]
    heads_dev = start_state.shape[1]
    key_dim = start_state.shape[2]
    value_dim = start_state.shape[3]
    query_heads = queries.reshape(row_count, draft_len, heads_dev, key_dim)
    key_heads = keys_scaled.reshape(row_count, draft_len, heads_dev, key_dim)
    value_heads = values_all.reshape(row_count, draft_len, heads_dev, value_dim)
    gate_heads = gates_all.reshape(row_count, draft_len, heads_dev, value_dim)
    decay_rate = 1.0 - jnp.exp2(-5.0 - head_ids)
    positions = jnp.arange(draft_len, dtype=jnp.float32)
    distance = positions[:, None] - positions[None, :]
    causal = distance >= 0.0
    decay_mask = jnp.where(
        causal[None], jnp.power(decay_rate[:, None, None], jnp.maximum(distance, 0.0)[None]), 0.0
    )
    scores = (
        jnp.einsum("nthk,nshk->nhts", query_heads, key_heads, preferred_element_type=jnp.float32)
        * decay_mask[None]
    )
    weights = scores.astype(jnp.bfloat16)
    inside_terms = jnp.einsum(
        "nhts,nshv->nthv", weights, value_heads, preferred_element_type=jnp.float32
    )
    state_terms = jnp.einsum(
        "nthk,nhkv->nthv", query_heads, start_state, preferred_element_type=jnp.float32
    )
    state_terms = (
        state_terms * jnp.power(decay_rate[None, :], positions[:, None] + 1.0)[None, :, :, None]
    )
    mixture = layer_norm(inside_terms + state_terms)
    hidden = (jax.nn.silu(gate_heads.astype(jnp.float32)) * mixture).astype(jnp.bfloat16)
    hidden = hidden.reshape(row_count, draft_len, heads_dev * value_dim)
    counts = counts_int.astype(jnp.float32)[:, None]
    remaining = jnp.maximum(counts - 1.0 - positions[None, :], 0.0)
    within = positions[None, :] < counts
    scale_rows = jnp.where(
        within[:, :, None], jnp.power(decay_rate[None, None, :], remaining[:, :, None]), 0.0
    )
    kept_keys = (key_heads.astype(jnp.float32) * scale_rows[..., None]).astype(jnp.bfloat16)
    updated = jnp.einsum(
        "nshk,nshv->nhkv", kept_keys, value_heads, preferred_element_type=jnp.float32
    )
    updated = updated + jnp.power(decay_rate[None, :], counts)[
        :, :, None, None
    ] * start_state.astype(jnp.float32)
    return (hidden, updated.astype(jnp.bfloat16))


def token_rows(draft_ids, worker_slot, embedding):
    width = lax.axis_size("req")
    own_rows, draft_len = draft_ids.shape
    count = own_rows * draft_len
    vocab_rows, cols = embedding.shape
    cap = -(-2 * count // width)
    lanes = -(-(cap + 2) // 128) * 128
    ids = draft_ids.reshape(count)
    holder = ids // vocab_rows
    local = ids - holder * vocab_rows
    order = jnp.arange(count, dtype=jnp.int32)
    same = ids[:, None] == ids[None, :]
    first_at = jnp.min(jnp.where(same, order[None, :], count), axis=1)
    is_first = first_at == order
    peers = is_first[None, :] & (holder[:, None] == holder[None, :])
    rank = jnp.sum((peers & (order[None, :] < first_at[:, None])).astype(jnp.int32), axis=1)
    most = jnp.max(jnp.sum(peers.astype(jnp.int32), axis=1))
    own_rounds = (most + cap - 1) // cap

    def requests(turn):
        spot = jnp.where(is_first & (rank // cap == turn), holder * cap + rank % cap, -1)
        hit = spot[None, :] == jnp.arange(width * cap, dtype=jnp.int32)[:, None]
        return jnp.sum(jnp.where(hit, local[None, :], 0), axis=1).reshape(width, cap)

    def rows_for(wanted):
        picked = jnp.take(embedding, wanted.reshape(width * cap), axis=0, mode="clip")
        got = lax.all_to_all(
            picked.reshape(width, cap, cols), "req", split_axis=0, concat_axis=0, tiled=True
        )
        return jnp.take(got.reshape(width * cap, cols), holder * cap + rank % cap, axis=0, mode="clip")

    target = worker_slot // own_rows
    place = worker_slot - target * own_rows
    to_target = target[None, :] == jnp.arange(width, dtype=jnp.int32)[:, None]
    place_for = jnp.sum(jnp.where(to_target, place[None, :], 0), axis=1)
    table = jnp.concatenate(
        [
            requests(0),
            place_for[:, None],
            jnp.full((width, 1), own_rounds, jnp.int32),
            jnp.zeros((width, lanes - cap - 2), jnp.int32),
        ],
        axis=1,
    )
    heard = lax.all_to_all(table, "req", split_axis=0, concat_axis=0, tiled=True)
    place_of = heard[:, cap]
    rounds = jnp.max(heard[:, cap + 1])
    tokens = rows_for(heard[:, :cap])

    def more(carry):
        return carry[0] < rounds

    def step(carry):
        turn, held = carry
        wanted = lax.all_to_all(
            requests(turn), "req", split_axis=0, concat_axis=0, tiled=True
        )
        fresh = rows_for(wanted)
        return turn + 1, jnp.where((rank // cap == turn)[:, None], fresh, held)

    _, tokens = lax.while_loop(more, step, (jnp.int32(1), tokens))
    return tokens, place_of


def project_kernel(zpos_ref, normed_ref, *refs):
    pieces, out_ref = refs[:-1], refs[-1]
    depth = pieces[0].shape[0]
    total = None
    for step, piece in enumerate(pieces):
        shard = lax.rem(zpos_ref[0] + (len(pieces) - step), len(pieces))
        start = pl.multiple_of(shard * depth, 128)
        term = jnp.dot(
            normed_ref[:, pl.ds(start, depth)], piece[...], preferred_element_type=jnp.float32
        )
        total = term if total is None else total + term
    out_ref[...] = total.astype(out_ref.dtype)


def project(zpos, normed, pieces):
    rows, width = normed.shape[0], pieces[0].shape[1]
    block = 256
    depth = pieces[0].shape[0]
    return pl.pallas_call(
        project_kernel,
        out_shape=jax.ShapeDtypeStruct((rows, width), jnp.bfloat16),
        grid_spec=pltpu.PrefetchScalarGridSpec(
            num_scalar_prefetch=1,
            grid=(rows // block,),
            in_specs=[pl.BlockSpec((block, normed.shape[1]), lambda i, z: (i, 0))]
            + [pl.BlockSpec((depth, width), lambda i, z: (0, 0)) for _ in pieces],
            out_specs=pl.BlockSpec((block, width), lambda i, z: (i, 0)),
        ),
        cost_estimate=pl.CostEstimate(
            flops=2 * rows * width * normed.shape[1],
            bytes_accessed=2 * (rows * normed.shape[1] + normed.shape[1] * width + rows * width),
            transcendentals=0,
        ),
        name="project",
    )(zpos, normed, *pieces)


GROUP = 4


def hidden_kernel(head, key_dim, value_dim, to_ref, rate_ref, mix_ref, state_ref, out_ref):
    draft = mix_ref.shape[1]
    log_rate = rate_ref[head]
    t_pos = lax.broadcasted_iota(jnp.int32, (draft, draft), 0)
    s_pos = lax.broadcasted_iota(jnp.int32, (draft, draft), 1)
    away = (t_pos - s_pos).astype(jnp.float32)
    mask = jnp.where(away >= 0.0, jnp.exp(jnp.maximum(away, 0.0) * log_rate), 0.0)
    after = lax.broadcasted_iota(jnp.int32, (draft, value_dim), 0).astype(jnp.float32) + 1.0
    fade = jnp.exp(after * log_rate)
    base = pl.program_id(0) * GROUP
    for r in range(GROUP):
        query = mix_ref[r, :, :key_dim]
        keys = mix_ref[r, :, key_dim : 2 * key_dim] * jnp.bfloat16(key_dim**-0.5)
        values = mix_ref[r, :, 2 * key_dim : 2 * key_dim + value_dim]
        gate = mix_ref[r, :, 2 * key_dim + value_dim :].astype(jnp.float32)
        scores = lax.dot_general(
            query, keys, (((1,), (1,)), ((), ())), preferred_element_type=jnp.float32
        )
        weights = (scores * mask).astype(jnp.bfloat16)
        inside = jnp.dot(weights, values, preferred_element_type=jnp.float32)
        carried = jnp.dot(query, state_ref[r, 0], preferred_element_type=jnp.float32)
        mixture = layer_norm(inside + carried * fade)
        out_ref[to_ref[base + r]] = (jax.nn.silu(gate) * mixture).astype(jnp.bfloat16)


def hidden_of(head, target, log_rate, mix, state):
    rows, draft, width = mix.shape
    _, _, key_dim, value_dim = state.shape
    return pl.pallas_call(
        lambda *refs: hidden_kernel(head, key_dim, value_dim, *refs),
        out_shape=jax.ShapeDtypeStruct((rows, draft, value_dim), jnp.bfloat16),
        grid_spec=pltpu.PrefetchScalarGridSpec(
            num_scalar_prefetch=2,
            grid=(rows // GROUP,),
            in_specs=[
                pl.BlockSpec((GROUP, draft, width), lambda i, *_: (i, 0, 0)),
                pl.BlockSpec((GROUP, 1, key_dim, value_dim), lambda i, *_: (i, head, 0, 0)),
            ],
            out_specs=pl.BlockSpec((rows, draft, value_dim), lambda i, *_: (0, 0, 0)),
        ),
        cost_estimate=pl.CostEstimate(
            flops=2 * rows * draft * key_dim * value_dim * 8,
            bytes_accessed=2 * rows * (key_dim * value_dim + draft * (width + value_dim)),
            transcendentals=rows * draft * value_dim,
        ),
        name="hidden",
    )(target, log_rate, mix, state)


def update_kernel(head, key_dim, value_dim, held, acc_ref, rate_ref, mix_ref, state_ref, *refs):
    out_ref = refs[-1]
    draft = mix_ref.shape[1]
    log_rate = rate_ref[head]
    spot = lax.broadcasted_iota(jnp.int32, (draft, key_dim), 0)
    base = pl.program_id(0) * GROUP
    for r in range(GROUP):
        taken = acc_ref[base + r]
        left = jnp.maximum(taken - 1 - spot, 0).astype(jnp.float32)
        scale = jnp.where(spot < taken, jnp.exp(left * log_rate), 0.0)
        keys = (mix_ref[r, :, key_dim : 2 * key_dim] * jnp.bfloat16(key_dim**-0.5)).astype(
            jnp.float32
        )
        kept = (keys * scale).astype(jnp.bfloat16)
        values = mix_ref[r, :, 2 * key_dim : 2 * key_dim + value_dim]
        fresh = lax.dot_general(
            kept, values, (((0,), (0,)), ((), ())), preferred_element_type=jnp.float32
        )
        fade = jnp.exp(
            jnp.full((key_dim, value_dim), taken.astype(jnp.float32) * log_rate, jnp.float32)[:8]
        )[:1]
        out_ref[r, 0] = (fresh + fade * state_ref[r, 0].astype(jnp.float32)).astype(jnp.bfloat16)


def update_of(head, accepted, log_rate, mix, state, earlier):
    rows, draft, width = mix.shape
    _, _, key_dim, value_dim = state.shape
    spec = pl.BlockSpec((GROUP, 1, key_dim, value_dim), lambda i, *_: (i, head, 0, 0))
    more = () if earlier is None else (earlier,)
    return pl.pallas_call(
        lambda *refs: update_kernel(head, key_dim, value_dim, bool(more), *refs),
        out_shape=jax.ShapeDtypeStruct(state.shape, jnp.bfloat16),
        grid_spec=pltpu.PrefetchScalarGridSpec(
            num_scalar_prefetch=2,
            grid=(rows // GROUP,),
            in_specs=[pl.BlockSpec((GROUP, draft, width), lambda i, *_: (i, 0, 0)), spec]
            + [pl.BlockSpec(memory_space=pl.ANY) for _ in more],
            out_specs=spec,
        ),
        input_output_aliases={4: 0} if more else {},
        cost_estimate=pl.CostEstimate(
            flops=2 * rows * draft * key_dim * value_dim * 8,
            bytes_accessed=4 * rows * key_dim * value_dim,
            transcendentals=0,
        ),
        name="update",
    )(accepted, log_rate, mix, state, *more)


def settle_kernel(place_ref, *refs):
    parts, out_ref = refs[:-1], refs[-1]
    value_dim = parts[0].shape[2]
    for s in range(parts[0].shape[0]):
        row = place_ref[s]
        for j, part in enumerate(parts):
            out_ref[row, :, j * value_dim : (j + 1) * value_dim] = part[s]


def settle(place_of, parts):
    rows, draft, value_dim = parts[0].shape
    whole = (rows, draft, value_dim * len(parts))
    return pl.pallas_call(
        settle_kernel,
        out_shape=jax.ShapeDtypeStruct(whole, jnp.bfloat16),
        grid_spec=pltpu.PrefetchScalarGridSpec(
            num_scalar_prefetch=1,
            grid=(1,),
            in_specs=[
                pl.BlockSpec(part.shape, lambda i, *_: (0, 0, 0)) for part in parts
            ],
            out_specs=pl.BlockSpec(whole, lambda i, *_: (0, 0, 0)),
        ),
        name="settle",
    )(place_of, *parts)


def canonical(member, pieces):
    pieces = list(pieces)
    bit = 1
    while bit < len(pieces):
        swap = (member & bit) != 0
        pieces = [jnp.where(swap, pieces[k ^ bit], pieces[k]) for k in range(len(pieces))]
        bit *= 2
    return pieces


def swap_perm(group, k):
    return [(z * group + m, z * group + (m ^ k)) for z in range(ZLEN) for m in range(group)]


def ring_perm(group, shift):
    return [
        (z * group + m, ((z + shift) % ZLEN) * group + m) for z in range(ZLEN) for m in range(group)
    ]


def fast_device(
    draft_ids, worker_slot, accepted, embedding, w_query, w_key, w_value, w_gate, old_state
):
    own_rows, draft = draft_ids.shape
    heads = old_state.shape[1]
    key_dim, value_dim = old_state.shape[2:]
    group = lax.axis_size("req") // ZLEN
    member = lax.axis_index("req") % group
    zpos = lax.axis_index("req") // group
    count = own_rows * draft
    share = 2 * (key_dim + value_dim) // group

    gathered = []
    for j in range(heads):
        whole = jnp.concatenate(
            [
                w_query[:, j * key_dim : (j + 1) * key_dim],
                w_key[:, j * key_dim : (j + 1) * key_dim],
                w_value[:, j * value_dim : (j + 1) * value_dim],
                w_gate[:, j * value_dim : (j + 1) * value_dim],
            ],
            axis=1,
        )
        parts = []
        for k in range(group):
            part = lax.dynamic_slice_in_dim(whole, (member ^ k) * share, share, axis=1)
            parts.append(part if k == 0 else lax.ppermute(part, "req", swap_perm(group, k)))
        plane = jnp.concatenate(canonical(member, parts), axis=0)
        one = lax.ppermute(plane, "req", ring_perm(group, 1))
        three = lax.ppermute(plane, "req", ring_perm(group, 3))
        two = lax.ppermute(one, "req", ring_perm(group, 1))
        gathered.append((plane, one, two, three))

    half, place_of = token_rows(draft_ids, worker_slot, embedding)
    other = lax.ppermute(half, "head", [(0, 1), (1, 0)])
    low = lax.axis_index("head") == 0
    tokens = jnp.concatenate([jnp.where(low, half, other), jnp.where(low, other, half)], axis=1)
    normed = layer_norm(tokens.astype(jnp.float32)).astype(jnp.bfloat16)
    bit = 1
    while bit < group:
        there = lax.ppermute(normed, "req", swap_perm(group, bit))
        swap = (member & bit) != 0
        normed = jnp.concatenate(
            [jnp.where(swap, there, normed), jnp.where(swap, normed, there)], axis=0
        )
        bit *= 2

    head_ids = (lax.axis_index("head") * heads + jnp.arange(heads, dtype=jnp.int32)).astype(
        jnp.float32
    )
    log_rate = jnp.log1p(-jnp.exp2(-5.0 - head_ids))
    target = worker_slot // own_rows
    parts_out, new_state = [], None
    for j in range(heads):
        result = project(zpos.reshape(1).astype(jnp.int32), normed, gathered[j])
        parts = []
        for k in range(group):
            part = lax.dynamic_slice_in_dim(result, (member ^ k) * count, count, axis=0)
            parts.append(part if k == 0 else lax.ppermute(part, "req", swap_perm(group, k)))
        mix = jnp.concatenate(canonical(member, parts), axis=1).reshape(own_rows, draft, -1)
        answer = hidden_of(j, target, log_rate, mix, old_state)
        parts_out.append(
            lax.all_to_all(answer, "req", split_axis=0, concat_axis=0, tiled=True)
        )
        new_state = update_of(j, accepted, log_rate, mix, old_state, new_state)
    return settle(place_of, parts_out), new_state


def plain_device(
    draft_ids, worker_slot, accepted, embedding, w_query, w_key, w_value, w_gate, old_state
):
    own_rows, draft = draft_ids.shape
    tables = [
        lax.all_gather(table, "req", axis=0, tiled=True)
        for table in (w_query, w_key, w_value, w_gate)
    ]
    half, place_of = token_rows(draft_ids, worker_slot, embedding)
    tokens = lax.all_gather(half, "head", axis=1, tiled=True)
    normed = layer_norm(tokens.astype(jnp.float32)).astype(jnp.bfloat16)
    raw = [jnp.dot(normed, table, preferred_element_type=jnp.float32) for table in tables]
    raw[1] = raw[1] * old_state.shape[2] ** (-0.5)
    made = [one.astype(jnp.bfloat16).reshape(own_rows, draft, -1) for one in raw]
    heads = old_state.shape[1]
    head_ids = (lax.axis_index("head") * heads + jnp.arange(heads, dtype=jnp.int32)).astype(
        jnp.float32
    )
    answer, new_state = retention(*made, old_state, accepted, head_ids)
    width = lax.axis_size("req")
    target = worker_slot // own_rows
    ahead = jnp.zeros((width,) + answer.shape[1:], answer.dtype).at[target].set(answer)
    received = lax.all_to_all(ahead, "req", split_axis=0, concat_axis=0, tiled=True)
    mine = lax.axis_index("req")
    valid = lax.all_to_all(
        (target[None, :] == jnp.arange(width)[:, None]).any(axis=1).astype(jnp.int32)[:, None],
        "req", split_axis=0, concat_axis=0, tiled=True,
    )[:, 0]
    spot = jnp.where(valid > 0, place_of, own_rows)
    hidden = jnp.zeros_like(answer).at[spot].set(received, mode="drop")
    return hidden, new_state


def solution(mesh):
    width, head_width = mesh.shape["req"], mesh.shape["head"]
    fast = head_width == 2 and width == 16
    return jax.shard_map(
        fast_device if fast else plain_device,
        mesh=mesh,
        in_specs=(
            P("req", None),
            P("req"),
            P("req"),
            P("req", "head"),
            P("req", "head"),
            P("req", "head"),
            P("req", "head"),
            P("req", "head"),
            P("req", "head", None, None),
        ),
        out_specs=(P("req", None, "head"), P("req", "head", None, None)),
        check_vma=False,
    )
```

time: 499 us -> 344 us (0.69)
  waiting for transfers between devices: 339 us -> 143 us
  Pallas kernels: 0 us -> 78.3 us
  starting transfers between devices: 4.72 us -> 59.7 us
  matrix products: 53.1 us -> 0 us
  blocking collectives: 28.2 us -> 11.1 us
  local copies, waits for them, and re-layouts: 39.3 us -> 22.3 us
  between operations: 15.1 us -> 1.8 us
  other arithmetic: 18.4 us -> 24.3 us
    all_gather x5 -> x0, waiting for transfers between devices: 227 us -> none  [the longest x1 63.3 us: per_device(): raw_gate = add_one(lax.all_gather(w_gate, 'req', axis=0, tiled=True))]
    ppermute x0 -> x39, waiting for transfers between devices: none -> 118 us  [the longest x24 44.6 us: fast_device(): lax.ppermute(part, 'req', swap_perm(group, k))]
    reduce_scatter x1 -> x0, waiting for transfers between devices: 104 us -> none  [per_device(): lax.psum_scatter(partial_rows.astype(jnp.bfloat16), 'req', scatter_dimens...]
    pallas_call x0 -> x13, Pallas kernels: none -> 78.3 us  [the longest x4 26.1 us: update_of(): pl.pallas_call(lambda *refs: update_kernel(head, key_dim, value_dim, bool...]
    dot_general x7 -> x0, matrix products: 53.1 us -> none  [the longest x4 20.9 us: add_rows(): return jnp.dot(normed, piece, preferred_element_type=jnp.float32)]
    ppermute x0 -> x39, starting transfers between devices: none -> 33.4 us  [the longest x24 22.5 us: fast_device(): lax.ppermute(part, 'req', swap_perm(group, k))]
    all_to_all x1 -> x5, starting transfers between devices: 4.49 us -> 26.2 us  [the longest x4 20.8 us: fast_device(): lax.all_to_all(answer, 'req', split_axis=0, concat_axis=0, tiled=True)]
    all_gather x1 -> x0, blocking collectives: 19.9 us -> none  [per_device(): lax.all_gather(draft_ids, 'req', axis=0, tiled=True)]
  transfers between devices with their start and end apart: 7 -> 44, of which waited for: 7 -> 13; matrix products, arithmetic and copies ran while one was open for 12% -> 9% of each run, Pallas kernels for 0% -> 22%
where the time goes in v1:
time: 344 us; the launch traced here: 341 us
  waiting for transfers between devices  143 us (42%)
  Pallas kernels  78.3 us (23%)
  starting transfers between devices  59.7 us (17%)
  other arithmetic  24.3 us (7%)
  local copies, waits for them, and re-layouts  22.3 us (6%)
  blocking collectives  11.1 us (3%)
    ppermute x24, waiting for transfers between devices, fast_device(): lax.ppermute(part, 'req', swap_perm(group, k))  44.6 us
    ppermute x4, waiting for transfers between devices, fast_device(): one = lax.ppermute(plane, 'req', ring_perm(group, 1))  36.2 us
    pallas_call x4, Pallas kernels, update_of(): pl.pallas_call(lambda *refs: update_kernel(head, key_dim, value_dim, bool...  26.1 us
    pallas_call x4, Pallas kernels, hidden_of(): pl.pallas_call(lambda *refs: hidden_kernel(head, key_dim, value_dim, *ref...  25.7 us
    ppermute x4, waiting for transfers between devices, fast_device(): two = lax.ppermute(one, 'req', ring_perm(group, 1))  25.3 us
    all_to_all x1, waiting for transfers between devices, rows_for(): lax.all_to_all(picked.reshape(width, cap, cols), 'req', split_axis=0, con...  23.9 us
    pallas_call x4, Pallas kernels, project(): pl.pallas_call(project_kernel, out_shape=jax.ShapeDtypeStruct((rows, widt...  23.6 us
    ppermute x24, starting transfers between devices, fast_device(): lax.ppermute(part, 'req', swap_perm(group, k))  22.5 us
  transfers between devices with their start and end apart: 44, of which 13 were waited for; matrix products, arithmetic and copies ran while one was open for 9% of the time, Pallas kernels for 22%

profile of v1, /device:TPU:9, one launch (start us, length us, event | category | flops | bytes accessed | tf_op | source)
XLA Modules:
  0.0 341.0 jit_solution(9491405098241150929)
XLA Ops:
  4.6 11.1 %all_to_all.66 = s32[16,1,128]{2,1,0:T(1,128)S(1)} all-to-all(s32[16,1,128]{2,1,0:T(1,128)S(1)} %bitcast.56), channel_id=1, replica_groups=mesh['req'=16,'head'=2] {'req'}, dimensions={0} | all-to-all | bytes 16384 | tf_op jit(solution)/shard_map/all_to_all | solution.py:112
  15.7 7.8 %gather_fusion.2 = bf16[512,1024]{1,0:T(8,128)(2,1)} fusion(bf16[4000,1024]{1,0:T(8,128)(2,1)} %param.14, s32[1024]{0:T(1024)S(1)} %pad_clamp_fusion.3), kind=kCustom, calls=%fused_computation.2 | custom fusion | bytes 2099200 | tf_op jit(solution)/shard_map/jit(_take)/gather | solution.py:93
  23.6 5.4 %all-to-all-start.3 = ((bf16[16,32,1024]{2,1,0:T(8,128)(2,1)}), bf16[16,32,1024]{2,1,0:T(8,128)(2,1)S(1)}, u32[]{:S(2)}, u32[]{:S(2)}) async-start(bf16[16,32,1024]{2,1,0:T(8,128)(2,1)} %bitcast.11), calls=%async_computation.3 | async-start | bytes 2097152 | tf_op jit(solution)/shard_map/all_to_all | solution.py:94
  29.9 23.9 %all-to-all-done.3 = bf16[16,32,1024]{2,1,0:T(8,128)(2,1)S(1)} async-done(((bf16[16,32,1024]{2,1,0:T(8,128)(2,1)}), bf16[16,32,1024]{2,1,0:T(8,128)(2,1)S(1)}, u32[]{:S(2)}, u32[]{:S(2)}) %all-to-all-start.3) | async-done | bytes 1048608 | tf_op jit(solution)/shard_map/all_to_all | solution.py:94
  57.7 11.8 %collective-permute-done = bf16[256,1024]{1,0:T(8,128)(2,1)S(1)} collective-permute-done((bf16[256,1024]{1,0:T(8,128)(2,1)S(1)}, bf16[256,1024]{1,0:T(8,128)(2,1)S(1)}, u32[]{:S(2)}, u32[]{:S(2)}) %collective-permute-start) | collective-permute-done | bytes 524320 | tf_op jit(solution)/shard_map/ppermute | solution.py:351
  87.5 42.2 %collective-permute-done.13 = bf16[128,384]{1,0:T(8,128)(2,1)S(1)} collective-permute-done((bf16[128,384]{1,0:T(8,128)(2,1)S(1)}, bf16[128,384]{1,0:T(8,128)(2,1)S(1)}, u32[]{:S(2)}, u32[]{:S(2)}) %collective-permute-start.13) | collective-permute-done | bytes 98336 | tf_op jit(solution)/shard_map/ppermute | solution.py:343
  140.7 6.2 %collective-permute-done.6.refs_1_ = bf16[512,384]{1,0:T(8,128)(2,1)S(1)} collective-permute-done((bf16[512,384]{1,0:T(8,128)(2,1)S(1)}, bf16[512,384]{1,0:T(8,128)(2,1)S(1)}, u32[]{:S(2)}, u32[]{:S(2)}) %collective-permute-start.6) | collective-permute-done | bytes 393248 | tf_op jit(solution)/shard_map/ppermute | solution.py:345
  148.0 2.8 broadcast_select_fusion.2
  150.8 29.9 %collective-permute-done.33.refs_1_ = bf16[512,384]{1,0:T(8,128)(2,1)} collective-permute-done((bf16[512,384]{1,0:T(8,128)(2,1)S(1)}, bf16[512,384]{1,0:T(8,128)(2,1)}, u32[]{:S(2)}, u32[]{:S(2)}) %collective-permute-start.33) | collective-permute-done | bytes 393248 | tf_op jit(solution)/shard_map/ppermute | solution.py:345
  181.8 2.6 pad_maximum_fusion.normed_ref
  185.4 3.7 %collective-permute-done.7.refs_2_ = bf16[512,384]{1,0:T(8,128)(2,1)S(1)} collective-permute-done((bf16[512,384]{1,0:T(8,128)(2,1)S(1)}, bf16[512,384]{1,0:T(8,128)(2,1)S(1)}, u32[]{:S(2)}, u32[]{:S(2)}) %collective-permute-start.7) | collective-permute-done | bytes 393248 | tf_op jit(solution)/shard_map/ppermute | solution.py:347
  189.8 5.9 %project.4 = bf16[1024,384]{1,0:T(8,128)(2,1)} custom-call(s32[1]{0:T(128)} %bitcast.10.zpos_ref, bf16[1024,2048]{1,0:T(8,128)(2,1)} %pad_maximum_fusion.normed_ref, bf16[512,384]{1,0:T(8,128)(2,1)} %copy-done.2, bf16[512,384]{1,0:T(8,128)(2,1)} %copy-done.14, bf16[512,384]{1,0:T(8,128)(2,1)} %copy-done.21, bf16[512,384]{1,0:T(8,128)(2,1)} %copy-done.16), custom_call_target="tpu_custom_call" | custom-call | flops 1610612736 | bytes 6553600 | tf_op jit(solution)/shard_map/project/pallas_call | solution.py:150
  199.2 6.8 %collective-permute-done.16.refs_2_ = bf16[512,384]{1,0:T(8,128)(2,1)} collective-permute-done((bf16[512,384]{1,0:T(8,128)(2,1)}, bf16[512,384]{1,0:T(8,128)(2,1)}, u32[]{:S(2)}, u32[]{:S(2)}) %collective-permute-start.16) | collective-permute-done | bytes 393248 | tf_op jit(solution)/shard_map/ppermute | solution.py:347
  207.5 5.9 %project.5 = bf16[1024,384]{1,0:T(8,128)(2,1)} custom-call(s32[1]{0:T(128)} %bitcast.10.zpos_ref, bf16[1024,2048]{1,0:T(8,128)(2,1)} %pad_maximum_fusion.normed_ref, bf16[512,384]{1,0:T(8,128)(2,1)} %copy-done.4, bf16[512,384]{1,0:T(8,128)(2,1)} %collective-permute-done.15.refs_1_, bf16[512,384]{1,0:T(8,128)(2,1)} %collective-permute-done.16.refs_2_, ...), custom_call_target="tpu_custom_call" | custom-call | flops 1610612736 | bytes 6553600 | tf_op jit(solution)/shard_map/project/pallas_call | solution.py:150
  216.0 6.8 %collective-permute-done.34.refs_2_ = bf16[512,384]{1,0:T(8,128)(2,1)S(1)} collective-permute-done((bf16[512,384]{1,0:T(8,128)(2,1)}, bf16[512,384]{1,0:T(8,128)(2,1)S(1)}, u32[]{:S(2)}, u32[]{:S(2)}) %collective-permute-start.34) | collective-permute-done | bytes 393248 | tf_op jit(solution)/shard_map/ppermute | solution.py:347
  222.8 2.7 collective-permute-start.9
  225.5 5.9 %project.7 = bf16[1024,384]{1,0:T(8,128)(2,1)} custom-call(s32[1]{0:T(128)} %bitcast.10.zpos_ref, bf16[1024,2048]{1,0:T(8,128)(2,1)} %pad_maximum_fusion.normed_ref, bf16[512,384]{1,0:T(8,128)(2,1)} %copy-done.5, bf16[512,384]{1,0:T(8,128)(2,1)} %collective-permute-done.33.refs_1_, bf16[512,384]{1,0:T(8,128)(2,1)} %copy-done.19, bf16[512,384]{1,0:T(8,128)(2,1)} %copy-done.17), custom_call_target="tpu_custom_call" | custom-call | flops 1610612736 | bytes 6553600 | tf_op jit(solution)/shard_map/project/pallas_call | solution.py:150
  231.6 8.0 %collective-permute-done.25.refs_2_ = bf16[512,384]{1,0:T(8,128)(2,1)S(1)} collective-permute-done((bf16[512,384]{1,0:T(8,128)(2,1)S(1)}, bf16[512,384]{1,0:T(8,128)(2,1)S(1)}, u32[]{:S(2)}, u32[]{:S(2)}) %collective-permute-start.25) | collective-permute-done | bytes 393248 | tf_op jit(solution)/shard_map/ppermute | solution.py:347
  240.5 5.9 %project.6 = bf16[1024,384]{1,0:T(8,128)(2,1)} custom-call(s32[1]{0:T(128)} %bitcast.10.zpos_ref, bf16[1024,2048]{1,0:T(8,128)(2,1)} %pad_maximum_fusion.normed_ref, bf16[512,384]{1,0:T(8,128)(2,1)} %copy-done.3, bf16[512,384]{1,0:T(8,128)(2,1)} %copy-done.15, bf16[512,384]{1,0:T(8,128)(2,1)} %copy-done.20, bf16[512,384]{1,0:T(8,128)(2,1)} %copy-done.18), custom_call_target="tpu_custom_call" | custom-call | flops 1610612736 | bytes 6553600 | tf_op jit(solution)/shard_map/project/pallas_call | solution.py:150
  253.7 6.4 %hidden.4 = bf16[16,16,512]{2,1,0:T(8,128)(2,1)} custom-call(s32[16]{0:T(128)} %copy-done.29, f32[4]{0:T(128)} %negate_log-plus-one_fusion.refs_1_, bf16[16,16,1536]{2,1,0:T(8,128)(2,1)} %bitcast.39, bf16[16,4,256,512]{3,2,1,0:T(8,128)(2,1)} %refs_3_.15), custom_call_target="tpu_custom_call" | custom-call | flops 536870912 | bytes 5242880 | tf_op jit(solution)/shard_map/hidden/pallas_call | solution.py:200
  260.1 4.9 %all-to-all-start.4 = ((bf16[16,16,512]{2,1,0:T(8,128)(2,1)}), bf16[16,16,512]{2,1,0:T(8,128)(2,1)S(1)}, u32[]{:S(2)}, u32[]{:S(2)}) async-start(bf16[16,16,512]{2,1,0:T(8,128)(2,1)} %hidden.4), calls=%async_computation.4 | async-start | bytes 524288 | tf_op jit(solution)/shard_map/all_to_all | solution.py:379
  269.8 6.4 %hidden.5 = bf16[16,16,512]{2,1,0:T(8,128)(2,1)} custom-call(s32[16]{0:T(128)} %copy-done.29, f32[4]{0:T(128)} %negate_log-plus-one_fusion.refs_1_, bf16[16,16,1536]{2,1,0:T(8,128)(2,1)} %bitcast.41, bf16[16,4,256,512]{3,2,1,0:T(8,128)(2,1)} %refs_3_.15), custom_call_target="tpu_custom_call" | custom-call | flops 536870912 | bytes 5242880 | tf_op jit(solution)/shard_map/hidden/pallas_call | solution.py:200
  278.0 4.9 %all-to-all-start.5 = ((bf16[16,16,512]{2,1,0:T(8,128)(2,1)}), bf16[16,16,512]{2,1,0:T(8,128)(2,1)S(1)}, u32[]{:S(2)}, u32[]{:S(2)}) async-start(bf16[16,16,512]{2,1,0:T(8,128)(2,1)} %hidden.5), calls=%async_computation.5 | async-start | bytes 524288 | tf_op jit(solution)/shard_map/all_to_all | solution.py:379
  285.1 6.4 %hidden.6 = bf16[16,16,512]{2,1,0:T(8,128)(2,1)} custom-call(s32[16]{0:T(128)} %copy-done.29, f32[4]{0:T(128)} %negate_log-plus-one_fusion.refs_1_, bf16[16,16,1536]{2,1,0:T(8,128)(2,1)} %bitcast.43, bf16[16,4,256,512]{3,2,1,0:T(8,128)(2,1)} %refs_3_.15), custom_call_target="tpu_custom_call" | custom-call | flops 536870912 | bytes 5242880 | tf_op jit(solution)/shard_map/hidden/pallas_call | solution.py:200
  291.6 6.0 %all-to-all-start.6 = ((bf16[16,16,512]{2,1,0:T(8,128)(2,1)}), bf16[16,16,512]{2,1,0:T(8,128)(2,1)S(1)}, u32[]{:S(2)}, u32[]{:S(2)}) async-start(bf16[16,16,512]{2,1,0:T(8,128)(2,1)} %hidden.6), calls=%async_computation.6 | async-start | bytes 524288 | tf_op jit(solution)/shard_map/all_to_all | solution.py:379
  298.8 6.4 %hidden.7 = bf16[16,16,512]{2,1,0:T(8,128)(2,1)} custom-call(s32[16]{0:T(128)} %copy-done.29, f32[4]{0:T(128)} %negate_log-plus-one_fusion.refs_1_, bf16[16,16,1536]{2,1,0:T(8,128)(2,1)} %bitcast.45, bf16[16,4,256,512]{3,2,1,0:T(8,128)(2,1)} %refs_3_.15), custom_call_target="tpu_custom_call" | custom-call | flops 536870912 | bytes 5242880 | tf_op jit(solution)/shard_map/hidden/pallas_call | solution.py:200
  306.3 5.0 %all-to-all-start.7 = ((bf16[16,16,512]{2,1,0:T(8,128)(2,1)}), bf16[16,16,512]{2,1,0:T(8,128)(2,1)S(1)}, u32[]{:S(2)}, u32[]{:S(2)}) async-start(bf16[16,16,512]{2,1,0:T(8,128)(2,1)} %hidden.7), calls=%async_computation.7 | async-start | bytes 524288 | tf_op jit(solution)/shard_map/all_to_all | solution.py:379
  311.3 6.5 %update.4.refs_4_ = bf16[16,4,256,512]{3,2,1,0:T(8,128)(2,1)} custom-call(s32[16]{0:T(128)} %refs_0_.7, f32[4]{0:T(128)} %negate_log-plus-one_fusion.refs_1_, bf16[16,16,1536]{2,1,0:T(8,128)(2,1)} %bitcast.40, bf16[16,4,256,512]{3,2,1,0:T(8,128)(2,1)} %refs_3_.15), custom_call_target="tpu_custom_call" | custom-call | flops 536870912 | bytes 8388608 | tf_op jit(solution)/shard_map/update/pallas_call | solution.py:250
  317.8 6.5 %update.5.refs_4_ = bf16[16,4,256,512]{3,2,1,0:T(8,128)(2,1)} custom-call(s32[16]{0:T(128)} %refs_0_.7, f32[4]{0:T(128)} %negate_log-plus-one_fusion.refs_1_, bf16[16,16,1536]{2,1,0:T(8,128)(2,1)} %bitcast.42, bf16[16,4,256,512]{3,2,1,0:T(8,128)(2,1)} %refs_3_.15, bf16[16,4,256,512]{3,2,1,0:T(8,128)(2,1)} %update.4.refs_4_), custom_call_target="tpu_custom_call", output_to_operand_aliasing={{}: (4, {})} | custom-call | flops 536870912 | bytes 8388608 | tf_op jit(solution)/shard_map/update/pallas_call | solution.py:250
  324.3 6.5 %update.6.refs_4_ = bf16[16,4,256,512]{3,2,1,0:T(8,128)(2,1)} custom-call(s32[16]{0:T(128)} %refs_0_.7, f32[4]{0:T(128)} %negate_log-plus-one_fusion.refs_1_, bf16[16,16,1536]{2,1,0:T(8,128)(2,1)} %bitcast.44, bf16[16,4,256,512]{3,2,1,0:T(8,128)(2,1)} %refs_3_.15, bf16[16,4,256,512]{3,2,1,0:T(8,128)(2,1)} %update.5.refs_4_), custom_call_target="tpu_custom_call", output_to_operand_aliasing={{}: (4, {})} | custom-call | flops 536870912 | bytes 8388608 | tf_op jit(solution)/shard_map/update/pallas_call | solution.py:250
  330.9 6.5 %update.7 = bf16[16,4,256,512]{3,2,1,0:T(8,128)(2,1)} custom-call(s32[16]{0:T(128)} %refs_0_.7, f32[4]{0:T(128)} %negate_log-plus-one_fusion.refs_1_, bf16[16,16,1536]{2,1,0:T(8,128)(2,1)} %bitcast.46, bf16[16,4,256,512]{3,2,1,0:T(8,128)(2,1)} %refs_3_.15, bf16[16,4,256,512]{3,2,1,0:T(8,128)(2,1)} %update.6.refs_4_), custom_call_target="tpu_custom_call", output_to_operand_aliasing={{}: (4, {})} | custom-call | flops 536870912 | bytes 8388608 | tf_op jit(solution)/shard_map/update/pallas_call | solution.py:250
  338.1 2.9 settle.1
  (199 shorter events, 68.3 us)
Async XLA Ops:
  23.6 30.3 %all-to-all-start.3 = ((bf16[16,32,1024]{2,1,0:T(8,128)(2,1)}), bf16[16,32,1024]{2,1,0:T(8,128)(2,1)S(1)}, u32[]{:S(2)}, u32[]{:S(2)}) async-start(bf16[16,32,1024]{2,1,0:T(8,128)(2,1)} %bitcast.11), calls=%async_computation.3 | async-start | bytes 2097152 | tf_op jit(solution)/shard_map/all_to_all | solution.py:94
  80.0 67.5 %collective-permute-start.2 = (bf16[512,2048]{1,0:T(8,128)(2,1)}, bf16[512,2048]{1,0:T(8,128)(2,1)}, u32[]{:S(2)}, u32[]{:S(2)}) collective-permute-start(bf16[512,2048]{1,0:T(8,128)(2,1)} %pad_maximum_fusion.1), channel_id=1, source_target_pairs={{0,4},{2,6},{4,0},{6,2},{8,12},{10,14},{12,8},{14,10},{16,20},{18,... | collective-permute-start | bytes 6291464 | tf_op jit(solution)/shard_map/ppermute | solution.py:357
  83.8 45.8 %collective-permute-start.13 = (bf16[128,384]{1,0:T(8,128)(2,1)S(1)}, bf16[128,384]{1,0:T(8,128)(2,1)S(1)}, u32[]{:S(2)}, u32[]{:S(2)}) collective-permute-start(bf16[128,384]{1,0:T(8,128)(2,1)S(1)} %copy-done.27), channel_id=1, source_target_pairs={{0,4},{2,6},{4,0},{6,2},{8,12},{10,14},{12,8},{14,10},{16,20},{18,... | collective-permute-start | bytes 294920 | tf_op jit(solution)/shard_map/ppermute | solution.py:343
  84.2 47.9 %collective-permute-start.12 = (bf16[128,384]{1,0:T(8,128)(2,1)S(1)}, bf16[128,384]{1,0:T(8,128)(2,1)S(1)}, u32[]{:S(2)}, u32[]{:S(2)}) collective-permute-start(bf16[128,384]{1,0:T(8,128)(2,1)S(1)} %copy-done.26), channel_id=1, source_target_pairs={{0,6},{2,4},{4,2},{6,0},{8,14},{10,12},{12,10},{14,8},{16,22},{18,... | collective-permute-start | bytes 294920 | tf_op jit(solution)/shard_map/ppermute | solution.py:343
  85.9 47.3 %collective-permute-start.23 = (bf16[128,384]{1,0:T(8,128)(2,1)S(1)}, bf16[128,384]{1,0:T(8,128)(2,1)S(1)}, u32[]{:S(2)}, u32[]{:S(2)}) collective-permute-start(bf16[128,384]{1,0:T(8,128)(2,1)S(1)} %get-tuple-element.353), channel_id=1, source_target_pairs={{0,2},{2,0},{4,6},{6,4},{8,10},{10,8},{12,14},{14,12},{16,18},{18,... | collective-permute-start | bytes 294920 | tf_op jit(solution)/shard_map/ppermute | solution.py:343
  87.1 47.5 %collective-permute-start.22 = (bf16[128,384]{1,0:T(8,128)(2,1)S(1)}, bf16[128,384]{1,0:T(8,128)(2,1)S(1)}, u32[]{:S(2)}, u32[]{:S(2)}) collective-permute-start(bf16[128,384]{1,0:T(8,128)(2,1)S(1)} %get-tuple-element.354), channel_id=1, source_target_pairs={{0,4},{2,6},{4,0},{6,2},{8,12},{10,14},{12,8},{14,10},{16,20},{18,... | collective-permute-start | bytes 294920 | tf_op jit(solution)/shard_map/ppermute | solution.py:343
  137.3 61.2 %collective-permute-start.17 = (bf16[512,384]{1,0:T(8,128)(2,1)S(1)}, bf16[512,384]{1,0:T(8,128)(2,1)}, u32[]{:S(2)}, u32[]{:S(2)}) collective-permute-start(bf16[512,384]{1,0:T(8,128)(2,1)S(1)} %pad_maximum_fusion.10.refs_0_), channel_id=1, source_target_pairs={{0,24},{2,26},{4,28},{6,30},{8,0},{10,2},{12,4},{14,6},{16,8},{18,... | collective-permute-start | bytes 1179656 | tf_op jit(solution)/shard_map/ppermute | solution.py:346
  138.1 43.1 %collective-permute-start.15 = (bf16[512,384]{1,0:T(8,128)(2,1)S(1)}, bf16[512,384]{1,0:T(8,128)(2,1)}, u32[]{:S(2)}, u32[]{:S(2)}) collective-permute-start(bf16[512,384]{1,0:T(8,128)(2,1)S(1)} %pad_maximum_fusion.10.refs_0_), channel_id=1, source_target_pairs={{0,8},{2,10},{4,12},{6,14},{8,16},{10,18},{12,20},{14,22},{16,24},... | collective-permute-start | bytes 1179656 | tf_op jit(solution)/shard_map/ppermute | solution.py:345
  140.5 43.9 %collective-permute-start.8 = (bf16[512,384]{1,0:T(8,128)(2,1)S(1)}, bf16[512,384]{1,0:T(8,128)(2,1)S(1)}, u32[]{:S(2)}, u32[]{:S(2)}) collective-permute-start(bf16[512,384]{1,0:T(8,128)(2,1)S(1)} %pad_maximum_fusion.8.refs_0_), channel_id=1, source_target_pairs={{0,24},{2,26},{4,28},{6,30},{8,0},{10,2},{12,4},{14,6},{16,8},{18,... | collective-permute-start | bytes 1179656 | tf_op jit(solution)/shard_map/ppermute | solution.py:346
  146.9 33.8 %collective-permute-start.33 = (bf16[512,384]{1,0:T(8,128)(2,1)S(1)}, bf16[512,384]{1,0:T(8,128)(2,1)}, u32[]{:S(2)}, u32[]{:S(2)}) collective-permute-start(bf16[512,384]{1,0:T(8,128)(2,1)S(1)} %pad_maximum_fusion.14.refs_0_), channel_id=1, source_target_pairs={{0,8},{2,10},{4,12},{6,14},{8,16},{10,18},{12,20},{14,22},{16,24},... | collective-permute-start | bytes 1179656 | tf_op jit(solution)/shard_map/ppermute | solution.py:345
  147.5 41.5 %collective-permute-start.7 = (bf16[512,384]{1,0:T(8,128)(2,1)S(1)}, bf16[512,384]{1,0:T(8,128)(2,1)S(1)}, u32[]{:S(2)}, u32[]{:S(2)}) collective-permute-start(bf16[512,384]{1,0:T(8,128)(2,1)S(1)} %collective-permute-done.6.refs_1_), channel_id=1, source_target_pairs={{0,8},{2,10},{4,12},{6,14},{8,16},{10,18},{12,20},{14,22},{16,24},... | collective-permute-start | bytes 1179656 | tf_op jit(solution)/shard_map/ppermute | solution.py:347
  180.7 16.9 %collective-permute-start.24 = (bf16[512,384]{1,0:T(8,128)(2,1)S(1)}, bf16[512,384]{1,0:T(8,128)(2,1)S(1)}, u32[]{:S(2)}, u32[]{:S(2)}) collective-permute-start(bf16[512,384]{1,0:T(8,128)(2,1)S(1)} %pad_maximum_fusion.12.refs_0_), channel_id=1, source_target_pairs={{0,8},{2,10},{4,12},{6,14},{8,16},{10,18},{12,20},{14,22},{16,24},... | collective-permute-start | bytes 1179656 | tf_op jit(solution)/shard_map/ppermute | solution.py:345
  181.2 24.8 %collective-permute-start.16 = (bf16[512,384]{1,0:T(8,128)(2,1)}, bf16[512,384]{1,0:T(8,128)(2,1)}, u32[]{:S(2)}, u32[]{:S(2)}) collective-permute-start(bf16[512,384]{1,0:T(8,128)(2,1)} %collective-permute-done.15.refs_1_), channel_id=1, source_target_pairs={{0,8},{2,10},{4,12},{6,14},{8,16},{10,18},{12,20},{14,22},{16,24},... | collective-permute-start | bytes 1179656 | tf_op jit(solution)/shard_map/ppermute | solution.py:347
  184.4 30.2 %collective-permute-start.35 = (bf16[512,384]{1,0:T(8,128)(2,1)S(1)}, bf16[512,384]{1,0:T(8,128)(2,1)S(1)}, u32[]{:S(2)}, u32[]{:S(2)}) collective-permute-start(bf16[512,384]{1,0:T(8,128)(2,1)S(1)} %pad_maximum_fusion.14.refs_0_), channel_id=1, source_target_pairs={{0,24},{2,26},{4,28},{6,30},{8,0},{10,2},{12,4},{14,6},{16,8},{18,... | collective-permute-start | bytes 1179656 | tf_op jit(solution)/shard_map/ppermute | solution.py:346
  189.0 33.7 %collective-permute-start.34 = (bf16[512,384]{1,0:T(8,128)(2,1)}, bf16[512,384]{1,0:T(8,128)(2,1)S(1)}, u32[]{:S(2)}, u32[]{:S(2)}) collective-permute-start(bf16[512,384]{1,0:T(8,128)(2,1)} %collective-permute-done.33.refs_1_), channel_id=1, source_target_pairs={{0,8},{2,10},{4,12},{6,14},{8,16},{10,18},{12,20},{14,22},{16,24},... | collective-permute-start | bytes 1179656 | tf_op jit(solution)/shard_map/ppermute | solution.py:347
  197.7 33.8 %collective-permute-start.26 = (bf16[512,384]{1,0:T(8,128)(2,1)S(1)}, bf16[512,384]{1,0:T(8,128)(2,1)S(1)}, u32[]{:S(2)}, u32[]{:S(2)}) collective-permute-start(bf16[512,384]{1,0:T(8,128)(2,1)S(1)} %pad_maximum_fusion.12.refs_0_), channel_id=1, source_target_pairs={{0,24},{2,26},{4,28},{6,30},{8,0},{10,2},{12,4},{14,6},{16,8},{18,... | collective-permute-start | bytes 1179656 | tf_op jit(solution)/shard_map/ppermute | solution.py:346
  198.5 41.2 %collective-permute-start.25 = (bf16[512,384]{1,0:T(8,128)(2,1)S(1)}, bf16[512,384]{1,0:T(8,128)(2,1)S(1)}, u32[]{:S(2)}, u32[]{:S(2)}) collective-permute-start(bf16[512,384]{1,0:T(8,128)(2,1)S(1)} %collective-permute-done.24.refs_1_), channel_id=1, source_target_pairs={{0,8},{2,10},{4,12},{6,14},{8,16},{10,18},{12,20},{14,22},{16,24},... | collective-permute-start | bytes 1179656 | tf_op jit(solution)/shard_map/ppermute | solution.py:347
  206.0 41.7 %collective-permute-start.11 = (bf16[256,384]{1,0:T(8,128)(2,1)}, bf16[256,384]{1,0:T(8,128)(2,1)}, u32[]{:S(2)}, u32[]{:S(2)}) collective-permute-start(bf16[256,384]{1,0:T(8,128)(2,1)} %get-tuple-element.323), channel_id=1, source_target_pairs={{0,2},{2,0},{4,6},{6,4},{8,10},{10,8},{12,14},{14,12},{16,18},{18,... | collective-permute-start | bytes 589832 | tf_op jit(solution)/shard_map/ppermute | solution.py:375
  214.6 35.0 %collective-permute-start.10 = (bf16[256,384]{1,0:T(8,128)(2,1)}, bf16[256,384]{1,0:T(8,128)(2,1)S(1)}, u32[]{:S(2)}, u32[]{:S(2)}) collective-permute-start(bf16[256,384]{1,0:T(8,128)(2,1)} %get-tuple-element.324), channel_id=1, source_target_pairs={{0,4},{2,6},{4,0},{6,2},{8,12},{10,14},{12,8},{14,10},{16,20},{18,... | collective-permute-start | bytes 589832 | tf_op jit(solution)/shard_map/ppermute | solution.py:375
  222.8 27.5 %collective-permute-start.9 = (bf16[256,384]{1,0:T(8,128)(2,1)}, bf16[256,384]{1,0:T(8,128)(2,1)}, u32[]{:S(2)}, u32[]{:S(2)}) collective-permute-start(bf16[256,384]{1,0:T(8,128)(2,1)} %get-tuple-element.325), channel_id=1, source_target_pairs={{0,6},{2,4},{4,2},{6,0},{8,14},{10,12},{12,10},{14,8},{16,22},{18,... | collective-permute-start | bytes 589832 | tf_op jit(solution)/shard_map/ppermute | solution.py:375
  231.4 33.5 %collective-permute-start.20 = (bf16[256,384]{1,0:T(8,128)(2,1)S(1)}, bf16[256,384]{1,0:T(8,128)(2,1)S(1)}, u32[]{:S(2)}, u32[]{:S(2)}) collective-permute-start(bf16[256,384]{1,0:T(8,128)(2,1)S(1)} %get-tuple-element.320), channel_id=1, source_target_pairs={{0,2},{2,0},{4,6},{6,4},{8,10},{10,8},{12,14},{14,12},{16,18},{18,... | collective-permute-start | bytes 589832 | tf_op jit(solution)/shard_map/ppermute | solution.py:375
  239.7 26.8 %collective-permute-start.19 = (bf16[256,384]{1,0:T(8,128)(2,1)S(1)}, bf16[256,384]{1,0:T(8,128)(2,1)S(1)}, u32[]{:S(2)}, u32[]{:S(2)}) collective-permute-start(bf16[256,384]{1,0:T(8,128)(2,1)S(1)} %get-tuple-element.321), channel_id=1, source_target_pairs={{0,4},{2,6},{4,0},{6,2},{8,12},{10,14},{12,8},{14,10},{16,20},{18,... | collective-permute-start | bytes 589832 | tf_op jit(solution)/shard_map/ppermute | solution.py:375
  247.7 19.6 %collective-permute-start.18 = (bf16[256,384]{1,0:T(8,128)(2,1)S(1)}, bf16[256,384]{1,0:T(8,128)(2,1)}, u32[]{:S(2)}, u32[]{:S(2)}) collective-permute-start(bf16[256,384]{1,0:T(8,128)(2,1)S(1)} %get-tuple-element.322), channel_id=1, source_target_pairs={{0,6},{2,4},{4,2},{6,0},{8,14},{10,12},{12,10},{14,8},{16,22},{18,... | collective-permute-start | bytes 589832 | tf_op jit(solution)/shard_map/ppermute | solution.py:375
  250.3 26.0 %collective-permute-start.29 = (bf16[256,384]{1,0:T(8,128)(2,1)S(1)}, bf16[256,384]{1,0:T(8,128)(2,1)S(1)}, u32[]{:S(2)}, u32[]{:S(2)}) collective-permute-start(bf16[256,384]{1,0:T(8,128)(2,1)S(1)} %get-tuple-element.317), channel_id=1, source_target_pairs={{0,2},{2,0},{4,6},{6,4},{8,10},{10,8},{12,14},{14,12},{16,18},{18,... | collective-permute-start | bytes 589832 | tf_op jit(solution)/shard_map/ppermute | solution.py:375
  250.3 32.7 %collective-permute-start.28 = (bf16[256,384]{1,0:T(8,128)(2,1)S(1)}, bf16[256,384]{1,0:T(8,128)(2,1)}, u32[]{:S(2)}, u32[]{:S(2)}) collective-permute-start(bf16[256,384]{1,0:T(8,128)(2,1)S(1)} %get-tuple-element.318), channel_id=1, source_target_pairs={{0,4},{2,6},{4,0},{6,2},{8,12},{10,14},{12,8},{14,10},{16,20},{18,... | collective-permute-start | bytes 589832 | tf_op jit(solution)/shard_map/ppermute | solution.py:375
  260.1 17.9 %all-to-all-start.4 = ((bf16[16,16,512]{2,1,0:T(8,128)(2,1)}), bf16[16,16,512]{2,1,0:T(8,128)(2,1)S(1)}, u32[]{:S(2)}, u32[]{:S(2)}) async-start(bf16[16,16,512]{2,1,0:T(8,128)(2,1)} %hidden.4), calls=%async_computation.4 | async-start | bytes 524288 | tf_op jit(solution)/shard_map/all_to_all | solution.py:379
  265.0 18.0 %collective-permute-start.27 = (bf16[256,384]{1,0:T(8,128)(2,1)S(1)}, bf16[256,384]{1,0:T(8,128)(2,1)S(1)}, u32[]{:S(2)}, u32[]{:S(2)}) collective-permute-start(bf16[256,384]{1,0:T(8,128)(2,1)S(1)} %get-tuple-element.319), channel_id=1, source_target_pairs={{0,6},{2,4},{4,2},{6,0},{8,14},{10,12},{12,10},{14,8},{16,22},{18,... | collective-permute-start | bytes 589832 | tf_op jit(solution)/shard_map/ppermute | solution.py:375
  267.2 30.4 %collective-permute-start.38 = (bf16[256,384]{1,0:T(8,128)(2,1)S(1)}, bf16[256,384]{1,0:T(8,128)(2,1)S(1)}, u32[]{:S(2)}, u32[]{:S(2)}) collective-permute-start(bf16[256,384]{1,0:T(8,128)(2,1)S(1)} %get-tuple-element.314), channel_id=1, source_target_pairs={{0,2},{2,0},{4,6},{6,4},{8,10},{10,8},{12,14},{14,12},{16,18},{18,... | collective-permute-start | bytes 589832 | tf_op jit(solution)/shard_map/ppermute | solution.py:375
  267.3 30.3 %collective-permute-start.37 = (bf16[256,384]{1,0:T(8,128)(2,1)S(1)}, bf16[256,384]{1,0:T(8,128)(2,1)S(1)}, u32[]{:S(2)}, u32[]{:S(2)}) collective-permute-start(bf16[256,384]{1,0:T(8,128)(2,1)S(1)} %get-tuple-element.315), channel_id=1, source_target_pairs={{0,4},{2,6},{4,0},{6,2},{8,12},{10,14},{12,8},{14,10},{16,20},{18,... | collective-permute-start | bytes 589832 | tf_op jit(solution)/shard_map/ppermute | solution.py:375
  276.3 21.4 %collective-permute-start.36 = (bf16[256,384]{1,0:T(8,128)(2,1)S(1)}, bf16[256,384]{1,0:T(8,128)(2,1)S(1)}, u32[]{:S(2)}, u32[]{:S(2)}) collective-permute-start(bf16[256,384]{1,0:T(8,128)(2,1)S(1)} %get-tuple-element.316), channel_id=1, source_target_pairs={{0,6},{2,4},{4,2},{6,0},{8,14},{10,12},{12,10},{14,8},{16,22},{18,... | collective-permute-start | bytes 589832 | tf_op jit(solution)/shard_map/ppermute | solution.py:375
  291.6 14.7 %all-to-all-start.6 = ((bf16[16,16,512]{2,1,0:T(8,128)(2,1)}), bf16[16,16,512]{2,1,0:T(8,128)(2,1)S(1)}, u32[]{:S(2)}, u32[]{:S(2)}) async-start(bf16[16,16,512]{2,1,0:T(8,128)(2,1)} %hidden.6), calls=%async_computation.6 | async-start | bytes 524288 | tf_op jit(solution)/shard_map/all_to_all | solution.py:379
  306.3 31.1 %all-to-all-start.7 = ((bf16[16,16,512]{2,1,0:T(8,128)(2,1)}), bf16[16,16,512]{2,1,0:T(8,128)(2,1)S(1)}, u32[]{:S(2)}, u32[]{:S(2)}) async-start(bf16[16,16,512]{2,1,0:T(8,128)(2,1)} %hidden.7), calls=%async_computation.7 | async-start | bytes 524288 | tf_op jit(solution)/shard_map/all_to_all | solution.py:379
  (42 other events, 417.5 us)

commit v2 on v1

v2 whole, which is shorter than its diff:
```python
import jax
import jax.numpy as jnp
from jax import lax
from jax.experimental import pallas as pl
from jax.experimental.pallas import tpu as pltpu
from jax.sharding import PartitionSpec as P

ZLEN = 4


def layer_norm(values):
    center = jnp.mean(values, axis=-1, keepdims=True)
    shifted = values - center
    spread = jnp.mean(shifted * shifted, axis=-1, keepdims=True)
    return shifted * lax.rsqrt(spread + 1e-05)


def retention(queries, keys_scaled, values_all, gates_all, start_state, counts_int, head_ids):
    row_count = queries.shape[0]
    draft_len = queries.shape[1]
    heads_dev = start_state.shape[1]
    key_dim = start_state.shape[2]
    value_dim = start_state.shape[3]
    query_heads = queries.reshape(row_count, draft_len, heads_dev, key_dim)
    key_heads = keys_scaled.reshape(row_count, draft_len, heads_dev, key_dim)
    value_heads = values_all.reshape(row_count, draft_len, heads_dev, value_dim)
    gate_heads = gates_all.reshape(row_count, draft_len, heads_dev, value_dim)
    decay_rate = 1.0 - jnp.exp2(-5.0 - head_ids)
    positions = jnp.arange(draft_len, dtype=jnp.float32)
    distance = positions[:, None] - positions[None, :]
    causal = distance >= 0.0
    decay_mask = jnp.where(
        causal[None], jnp.power(decay_rate[:, None, None], jnp.maximum(distance, 0.0)[None]), 0.0
    )
    scores = (
        jnp.einsum("nthk,nshk->nhts", query_heads, key_heads, preferred_element_type=jnp.float32)
        * decay_mask[None]
    )
    weights = scores.astype(jnp.bfloat16)
    inside_terms = jnp.einsum(
        "nhts,nshv->nthv", weights, value_heads, preferred_element_type=jnp.float32
    )
    state_terms = jnp.einsum(
        "nthk,nhkv->nthv", query_heads, start_state, preferred_element_type=jnp.float32
    )
    state_terms = (
        state_terms * jnp.power(decay_rate[None, :], positions[:, None] + 1.0)[None, :, :, None]
    )
    mixture = layer_norm(inside_terms + state_terms)
    hidden = (jax.nn.silu(gate_heads.astype(jnp.float32)) * mixture).astype(jnp.bfloat16)
    hidden = hidden.reshape(row_count, draft_len, heads_dev * value_dim)
    counts = counts_int.astype(jnp.float32)[:, None]
    remaining = jnp.maximum(counts - 1.0 - positions[None, :], 0.0)
    within = positions[None, :] < counts
    scale_rows = jnp.where(
        within[:, :, None], jnp.power(decay_rate[None, None, :], remaining[:, :, None]), 0.0
    )
    kept_keys = (key_heads.astype(jnp.float32) * scale_rows[..., None]).astype(jnp.bfloat16)
    updated = jnp.einsum(
        "nshk,nshv->nhkv", kept_keys, value_heads, preferred_element_type=jnp.float32
    )
    updated = updated + jnp.power(decay_rate[None, :], counts)[
        :, :, None, None
    ] * start_state.astype(jnp.float32)
    return (hidden, updated.astype(jnp.bfloat16))


def after(value, *needed):
    return lax.optimization_barrier((value, needed))[0]


def token_rows(draft_ids, worker_slot, embedding, asked=None, found=None):
    width = lax.axis_size("req")
    own_rows, draft_len = draft_ids.shape
    count = own_rows * draft_len
    vocab_rows, cols = embedding.shape
    cap = -(-2 * count // width)
    lanes = -(-(cap + 2) // 128) * 128
    ids = draft_ids.reshape(count)
    holder = ids // vocab_rows
    local = ids - holder * vocab_rows
    order = jnp.arange(count, dtype=jnp.int32)
    same = ids[:, None] == ids[None, :]
    first_at = jnp.min(jnp.where(same, order[None, :], count), axis=1)
    is_first = first_at == order
    peers = is_first[None, :] & (holder[:, None] == holder[None, :])
    rank = jnp.sum((peers & (order[None, :] < first_at[:, None])).astype(jnp.int32), axis=1)
    most = jnp.max(jnp.sum(peers.astype(jnp.int32), axis=1))
    own_rounds = (most + cap - 1) // cap

    def requests(turn):
        spot = jnp.where(is_first & (rank // cap == turn), holder * cap + rank % cap, -1)
        hit = spot[None, :] == jnp.arange(width * cap, dtype=jnp.int32)[:, None]
        return jnp.sum(jnp.where(hit, local[None, :], 0), axis=1).reshape(width, cap)

    def rows_for(wanted, needed=None):
        picked = jnp.take(embedding, wanted.reshape(width * cap), axis=0, mode="clip")
        if needed is not None:
            picked = after(picked, needed)
        got = lax.all_to_all(
            picked.reshape(width, cap, cols), "req", split_axis=0, concat_axis=0, tiled=True
        )
        return jnp.take(got.reshape(width * cap, cols), holder * cap + rank % cap, axis=0, mode="clip")

    target = worker_slot // own_rows
    place = worker_slot - target * own_rows
    to_target = target[None, :] == jnp.arange(width, dtype=jnp.int32)[:, None]
    place_for = jnp.sum(jnp.where(to_target, place[None, :], 0), axis=1)
    table = jnp.concatenate(
        [
            requests(0),
            place_for[:, None],
            jnp.full((width, 1), own_rounds, jnp.int32),
            jnp.zeros((width, lanes - cap - 2), jnp.int32),
        ],
        axis=1,
    )
    heard = lax.all_to_all(table, "req", split_axis=0, concat_axis=0, tiled=True)
    if asked is not None:
        heard = after(heard, asked)
    place_of = heard[:, cap]
    rounds = jnp.max(heard[:, cap + 1])
    tokens = rows_for(heard[:, :cap], found)

    def more(carry):
        return carry[0] < rounds

    def step(carry):
        turn, held = carry
        wanted = lax.all_to_all(
            requests(turn), "req", split_axis=0, concat_axis=0, tiled=True
        )
        fresh = rows_for(wanted)
        return turn + 1, jnp.where((rank // cap == turn)[:, None], fresh, held)

    def finish(first):
        return lax.while_loop(more, step, (jnp.int32(1), first))[1]

    return tokens, finish, place_of


def pack_kernel(heads, chunks, group, member_ref, q_ref, k_ref, v_ref, g_ref, *refs):
    outs, whole = refs[:-1], refs[-1]
    key_dim, value_dim = q_ref.shape[1] // heads, v_ref.shape[1] // heads
    share = 2 * (key_dim + value_dim) // group
    member = member_ref[0]
    for c, chunk in enumerate(chunks):
        for spot, j in enumerate(chunk):
            at = 0
            for ref, size in (
                (q_ref, key_dim), (k_ref, key_dim), (v_ref, value_dim), (g_ref, value_dim)
            ):
                whole[j, :, at : at + size] = ref[:, j * size : (j + 1) * size]
                at += size
            for k in range(group):
                start = pl.multiple_of((member ^ k) * share, 128)
                outs[c * group + k][:, spot * share : (spot + 1) * share] = whole[
                    j, :, pl.ds(start, share)
                ]


def pack(heads, chunks, group, member, tables):
    rows = tables[0].shape[0]
    width = sum(table.shape[1] for table in tables) // heads
    shapes = [(rows, len(chunk) * width // group) for chunk in chunks for _ in range(group)]
    flat = pl.pallas_call(
        lambda *refs: pack_kernel(heads, chunks, group, *refs),
        out_shape=[jax.ShapeDtypeStruct(shape, jnp.bfloat16) for shape in shapes],
        grid_spec=pltpu.PrefetchScalarGridSpec(
            num_scalar_prefetch=1,
            grid=(1,),
            in_specs=[pl.BlockSpec(table.shape, lambda i, *_: (0, 0)) for table in tables],
            out_specs=[pl.BlockSpec(shape, lambda i, *_: (0, 0)) for shape in shapes],
            scratch_shapes=[pltpu.VMEM((heads, rows, width), jnp.bfloat16)],
        ),
        name="pack",
    )(member, *tables)
    return [flat[c * group : (c + 1) * group] for c in range(len(chunks))]


def norm_kernel(low_ref, member_ref, own_ref, own_far_ref, side_ref, side_far_ref, out_ref):
    low = low_ref[0] == 0
    member = member_ref[0]
    half = own_ref.shape[1]
    blocks = 4
    for s, (near_ref, far_ref) in enumerate(((own_ref, own_far_ref), (side_ref, side_far_ref))):
        near = near_ref[...].astype(jnp.float32)
        far = far_ref[...].astype(jnp.float32)
        size = 2 * half
        center = (
            jnp.sum(near, axis=-1, keepdims=True) + jnp.sum(far, axis=-1, keepdims=True)
        ) / size
        near = near - center
        far = far - center
        spread = (
            jnp.sum(near * near, axis=-1, keepdims=True)
            + jnp.sum(far * far, axis=-1, keepdims=True)
        ) / size
        scale = lax.rsqrt(spread + 1e-05)
        near = (near * scale).astype(jnp.bfloat16)
        far = (far * scale).astype(jnp.bfloat16)
        pair = (jnp.where(low, near, far), jnp.where(low, far, near))
        for c in range(2 * half // 128):
            z, b = c // blocks, c % blocks
            start = pl.multiple_of((z * blocks + (member ^ b)) * 128, 128)
            at = c * 128
            piece = pair[at // half][:, at % half : at % half + 128]
            out_ref[s, :, pl.ds(start, 128)] = piece


def norm(low, member, own, own_far, side, side_far):
    rows, half = own.shape
    block = 64
    spec = pl.BlockSpec((block, half), lambda i, *_: (i, 0))
    return pl.pallas_call(
        norm_kernel,
        out_shape=jax.ShapeDtypeStruct((2, rows, 2 * half), jnp.bfloat16),
        grid_spec=pltpu.PrefetchScalarGridSpec(
            num_scalar_prefetch=2,
            grid=(rows // block,),
            in_specs=[spec] * 4,
            out_specs=pl.BlockSpec((2, block, 2 * half), lambda i, *_: (0, i, 0)),
        ),
        name="norm",
    )(low, member, own, own_far, side, side_far)


def project_kernel(zpos_ref, mine_ref, there_ref, *refs):
    count = (len(refs)) // 2
    pieces, outs = refs[:count], refs[count:]
    depth = pieces[0].shape[0]
    rows = mine_ref.shape[1]
    quarter = depth // 4

    def product(x_ref, swapped):
        total = None
        for step, piece in enumerate(pieces):
            shard = lax.rem(zpos_ref[0] + (count - step), count)
            start = pl.multiple_of(shard * depth, 128)
            table = piece[...]
            if swapped:
                order = (1, 0, 3, 2)
                table = jnp.concatenate(
                    [table[b * quarter : (b + 1) * quarter] for b in order], axis=0
                )
            left = x_ref[:, :, pl.ds(start, depth)].reshape(2 * rows, depth)
            term = jnp.dot(left, table, preferred_element_type=jnp.float32)
            total = term if total is None else total + term
        return total.astype(jnp.bfloat16)

    @pl.when(pl.program_id(0) == 0)
    def _():
        got = product(mine_ref, False)
        outs[0][...] = got[:rows]
        outs[2][...] = got[rows:]

    @pl.when(pl.program_id(0) == 1)
    def _():
        got = product(there_ref, True)
        outs[1][...] = got[:rows]
        outs[3][...] = got[rows:]


def project(zpos, mine, there, pieces):
    _, rows, size = mine.shape
    width = pieces[0].shape[1]
    whole = pl.BlockSpec(mine.shape, lambda i, z: (0, 0, 0))
    return pl.pallas_call(
        project_kernel,
        out_shape=[jax.ShapeDtypeStruct((rows, width), jnp.bfloat16)] * 4,
        grid_spec=pltpu.PrefetchScalarGridSpec(
            num_scalar_prefetch=1,
            grid=(2,),
            in_specs=[whole, whole]
            + [pl.BlockSpec(piece.shape, lambda i, z: (0, 0)) for piece in pieces],
            out_specs=[pl.BlockSpec((rows, width), lambda i, z: (0, 0))] * 4,
        ),
        cost_estimate=pl.CostEstimate(
            flops=8 * rows * width * size,
            bytes_accessed=2 * (4 * rows * size + size * width + 4 * rows * width),
            transcendentals=0,
        ),
        name="project",
    )(zpos, mine, there, *pieces)


GROUP = 8


def retain_kernel(
    head, key_dim, value_dim, count, do_hidden, do_update,
    to_ref, acc_ref, rate_ref, member_ref, *refs,
):
    parts, state_ref = refs[:count], refs[count]
    outs = refs[-(do_hidden + do_update) :]
    draft = parts[0].shape[0] // GROUP
    rows = draft * GROUP
    log_rate = rate_ref[head]
    member = member_ref[0]
    mix = jnp.concatenate(canonical(member, [part[...] for part in parts]), axis=1)
    base = pl.program_id(0) * GROUP
    query = mix[:, :key_dim]
    keys = mix[:, key_dim : 2 * key_dim] * jnp.bfloat16(key_dim**-0.5)
    values = mix[:, 2 * key_dim : 2 * key_dim + value_dim]
    states = [state_ref[r, 0] for r in range(GROUP)]
    span = [slice(r * draft, (r + 1) * draft) for r in range(GROUP)]
    if do_hidden:
        gate = mix[:, 2 * key_dim + value_dim :].astype(jnp.float32)
        shift = draft.bit_length() - 1
        t_pos = lax.broadcasted_iota(jnp.int32, (rows, rows), 0)
        s_pos = lax.broadcasted_iota(jnp.int32, (rows, rows), 1)
        away = t_pos - s_pos
        inside_draft = (away >= 0) & (t_pos >> shift == s_pos >> shift)
        mask = jnp.where(
            inside_draft, jnp.exp(jnp.maximum(away, 0).astype(jnp.float32) * log_rate), 0.0
        )
        after = (lax.broadcasted_iota(jnp.int32, (rows, value_dim), 0) & (draft - 1)) + 1
        fade = jnp.exp(after.astype(jnp.float32) * log_rate)
        scores = lax.dot_general(
            query, keys, (((1,), (1,)), ((), ())), preferred_element_type=jnp.float32
        )
        carried = jnp.concatenate(
            [
                jnp.dot(query[span[r]], states[r], preferred_element_type=jnp.float32)
                for r in range(GROUP)
            ],
            axis=0,
        )
        weights = (scores * mask).astype(jnp.bfloat16)
        inside = jnp.dot(weights, values, preferred_element_type=jnp.float32)
        mixture = layer_norm(inside + carried * fade)
        answer = (jax.nn.silu(gate) * mixture).astype(jnp.bfloat16)
        for r in range(GROUP):
            outs[0][to_ref[base + r]] = answer[span[r]]
    if do_update:
        spot = lax.broadcasted_iota(jnp.int32, (draft, key_dim), 0)
        for r in range(GROUP):
            taken = acc_ref[base + r]
            left = jnp.maximum(taken - 1 - spot, 0).astype(jnp.float32)
            scale = jnp.where(spot < taken, jnp.exp(left * log_rate), 0.0)
            kept = (keys[span[r]].astype(jnp.float32) * scale).astype(jnp.bfloat16)
            fresh = lax.dot_general(
                kept, values[span[r]], (((0,), (0,)), ((), ())), preferred_element_type=jnp.float32
            )
            fade = jnp.exp(
                jnp.full((8, value_dim), taken.astype(jnp.float32) * log_rate, jnp.float32)
            )[:1]
            outs[-1][r, 0] = (fresh + fade * states[r].astype(jnp.float32)).astype(jnp.bfloat16)


def retain(head, at, spot, width, do_hidden, do_update, scalars, parts, state, answers, states):
    rows, _, key_dim, value_dim = state.shape
    draft = parts[0].shape[0] // rows
    share = 2 * (key_dim + value_dim) // len(parts)
    state_spec = pl.BlockSpec((GROUP, 1, key_dim, value_dim), lambda i, *_: (i, head, 0, 0))
    out_shape, out_specs, earlier = [], [], []
    if do_hidden:
        out_shape.append(jax.ShapeDtypeStruct((rows, draft, width * value_dim), jnp.bfloat16))
        out_specs.append(pl.BlockSpec((rows, draft, value_dim), lambda i, *_: (0, 0, spot)))
        earlier.append(answers)
    if do_update:
        out_shape.append(jax.ShapeDtypeStruct(state.shape, jnp.bfloat16))
        out_specs.append(state_spec)
        earlier.append(states)
    first = len(scalars) + len(parts) + 1
    more, aliases = [], {}
    for out, one in enumerate(earlier):
        if one is not None:
            aliases[first + len(more)] = out
            more.append(one)
    return pl.pallas_call(
        lambda *refs: retain_kernel(
            head, key_dim, value_dim, len(parts), do_hidden, do_update, *refs
        ),
        out_shape=out_shape,
        grid_spec=pltpu.PrefetchScalarGridSpec(
            num_scalar_prefetch=len(scalars),
            grid=(rows // GROUP,),
            in_specs=[
                pl.BlockSpec((GROUP * draft, share), lambda i, *_: (i, at)) for _ in parts
            ]
            + [state_spec]
            + [pl.BlockSpec(memory_space=pl.ANY) for _ in more],
            out_specs=out_specs,
        ),
        input_output_aliases=aliases,
        cost_estimate=pl.CostEstimate(
            flops=2 * rows * draft * key_dim * value_dim * 8,
            bytes_accessed=2 * rows * key_dim * value_dim * (1 + do_update),
            transcendentals=0,
        ),
        name="retain",
    )(*scalars, *parts, state, *more)


def settle_kernel(place_ref, *refs):
    parts, out_ref = refs[:-1], refs[-1]
    for s in range(parts[0].shape[0]):
        row = place_ref[s]
        at = 0
        for part in parts:
            out_ref[row, :, at : at + part.shape[2]] = part[s]
            at += part.shape[2]


def settle(place_of, parts):
    rows, draft, _ = parts[0].shape
    whole = (rows, draft, sum(part.shape[2] for part in parts))
    return pl.pallas_call(
        settle_kernel,
        out_shape=jax.ShapeDtypeStruct(whole, jnp.bfloat16),
        grid_spec=pltpu.PrefetchScalarGridSpec(
            num_scalar_prefetch=1,
            grid=(1,),
            in_specs=[pl.BlockSpec(part.shape, lambda i, *_: (0, 0, 0)) for part in parts],
            out_specs=pl.BlockSpec(whole, lambda i, *_: (0, 0, 0)),
        ),
        name="settle",
    )(place_of, *parts)


def canonical(member, pieces):
    pieces = list(pieces)
    bit = 1
    while bit < len(pieces):
        swap = (member & bit) != 0
        pieces = [jnp.where(swap, pieces[k ^ bit], pieces[k]) for k in range(len(pieces))]
        bit *= 2
    return pieces


def swap_perm(group, k):
    return [(z * group + m, z * group + (m ^ k)) for z in range(ZLEN) for m in range(group)]


def ring_perm(group, shift):
    return [
        (z * group + m, ((z + shift) % ZLEN) * group + m) for z in range(ZLEN) for m in range(group)
    ]


def fast_device(
    draft_ids, worker_slot, accepted, embedding, w_query, w_key, w_value, w_gate, old_state
):
    own_rows, draft = draft_ids.shape
    heads = old_state.shape[1]
    key_dim, value_dim = old_state.shape[2:]
    group = lax.axis_size("req") // ZLEN
    member = lax.axis_index("req") % group
    zpos = lax.axis_index("req") // group

    head_ids = (lax.axis_index("head") * heads + jnp.arange(heads, dtype=jnp.int32)).astype(
        jnp.float32
    )
    log_rate = jnp.log1p(-jnp.exp2(-5.0 - head_ids))

    me = member.reshape(1).astype(jnp.int32)
    where_z = zpos.reshape(1).astype(jnp.int32)
    low = lax.axis_index("head").reshape(1).astype(jnp.int32)
    target = worker_slot // own_rows
    scalars = (target, accepted, log_rate, me)

    chunks = ((0, 1), (2,), (3,))
    packed = pack(heads, chunks, group, me, (w_query, w_key, w_value, w_gate))

    def swaps(c):
        parts = [part if k == 0 else side(part, k) for k, part in enumerate(packed[c])]
        return jnp.concatenate(parts, axis=0)

    def up(piece):
        return lax.ppermute(piece, "req", ring_perm(group, 1))

    def down(piece):
        return lax.ppermute(piece, "req", ring_perm(group, -1))

    def side(rows, k):
        return lax.ppermute(rows, "req", swap_perm(group, k))

    def fence(*values):
        return lax.optimization_barrier(values)

    plane_a, plane_b = swaps(0), swaps(1)
    one_b = up(plane_b)
    first, finish, place_of = token_rows(
        draft_ids, worker_slot, embedding, asked=(plane_a, plane_b), found=(one_b,)
    )
    plane_c = swaps(2)
    one_a = up(plane_a)
    first, one_a = fence(first, one_a)
    half = finish(first)

    three_a = down(after(plane_a, half))
    other = lax.ppermute(half, "head", [(0, 1), (1, 0)])
    half_x = side(half, 2)
    half, other, half_x, three_a, plane_b, plane_c = fence(
        half, other, half_x, three_a, plane_b, plane_c
    )
    other_x = side(other, 2)
    two_a = up(after(one_a, other))
    other_x, two_a, one_b, plane_b = fence(other_x, two_a, one_b, plane_b)
    mine = norm(low, me, half, other, half_x, other_x)
    there = side(mine, 1)
    three_b = down(plane_b)
    two_b = up(one_b)
    mine, there = fence(mine, there)

    def hand_back(parts):
        return [part if k == 0 else side(part, k) for k, part in enumerate(parts)]

    def send(answer):
        return lax.all_to_all(answer, "req", split_axis=0, concat_axis=0, tiled=True)

    made_a = project(where_z, mine, there, (plane_a, one_a, two_a, three_a))
    made_a, two_b, three_b, plane_c = fence(made_a, two_b, three_b, plane_c)
    mix_a = hand_back(made_a)
    one_c, three_c = up(plane_c), down(plane_c)
    made_b = project(where_z, mine, there, (plane_b, one_b, two_b, three_b))
    made_b, one_c = fence(made_b, one_c)
    mix_b = hand_back(made_b)
    two_c = up(one_c)
    mix_a, three_c = fence(mix_a, three_c)
    ahead, new_state = retain(0, 0, 0, 2, True, True, scalars, mix_a, old_state, None, None)
    ahead, two_c, three_c, new_state = fence(ahead, two_c, three_c, new_state)
    made_c = project(where_z, mine, there, (plane_c, one_c, two_c, three_c))
    mix_a, made_c = fence(mix_a, made_c)
    mix_c = hand_back(made_c)
    ahead, new_state = retain(1, 1, 1, 2, True, True, scalars, mix_a, old_state, ahead, new_state)
    front = send(ahead)
    behind, new_state = retain(2, 0, 0, 2, True, True, scalars, mix_b, old_state, None, new_state)
    (behind,) = retain(3, 0, 1, 2, True, False, scalars, mix_c, old_state, behind, None)
    back = send(behind)
    (new_state,) = retain(3, 0, 0, 1, False, True, scalars, mix_c, old_state, None, new_state)
    return settle(place_of, [front, back]), new_state


def plain_device(
    draft_ids, worker_slot, accepted, embedding, w_query, w_key, w_value, w_gate, old_state
):
    own_rows, draft = draft_ids.shape
    tables = [
        lax.all_gather(table, "req", axis=0, tiled=True)
        for table in (w_query, w_key, w_value, w_gate)
    ]
    half, finish, place_of = token_rows(draft_ids, worker_slot, embedding)
    half = finish(half)
    tokens = lax.all_gather(half, "head", axis=1, tiled=True)
    normed = layer_norm(tokens.astype(jnp.float32)).astype(jnp.bfloat16)
    raw = [jnp.dot(normed, table, preferred_element_type=jnp.float32) for table in tables]
    raw[1] = raw[1] * old_state.shape[2] ** (-0.5)
    made = [one.astype(jnp.bfloat16).reshape(own_rows, draft, -1) for one in raw]
    heads = old_state.shape[1]
    head_ids = (lax.axis_index("head") * heads + jnp.arange(heads, dtype=jnp.int32)).astype(
        jnp.float32
    )
    answer, new_state = retention(*made, old_state, accepted, head_ids)
    width = lax.axis_size("req")
    target = worker_slot // own_rows
    ahead = jnp.zeros((width,) + answer.shape[1:], answer.dtype).at[target].set(answer)
    received = lax.all_to_all(ahead, "req", split_axis=0, concat_axis=0, tiled=True)
    mine = lax.axis_index("req")
    valid = lax.all_to_all(
        (target[None, :] == jnp.arange(width)[:, None]).any(axis=1).astype(jnp.int32)[:, None],
        "req", split_axis=0, concat_axis=0, tiled=True,
    )[:, 0]
    spot = jnp.where(valid > 0, place_of, own_rows)
    hidden = jnp.zeros_like(answer).at[spot].set(received, mode="drop")
    return hidden, new_state


def solution(mesh):
    width, head_width = mesh.shape["req"], mesh.shape["head"]
    fast = head_width == 2 and width == 16
    return jax.shard_map(
        fast_device if fast else plain_device,
        mesh=mesh,
        in_specs=(
            P("req", None),
            P("req"),
            P("req"),
            P("req", "head"),
            P("req", "head"),
            P("req", "head"),
            P("req", "head"),
            P("req", "head"),
            P("req", "head", None, None),
        ),
        out_specs=(P("req", None, "head"), P("req", "head", None, None)),
        check_vma=False,
    )
```

time: 344 us -> 254 us (0.74)
  waiting for transfers between devices: 143 us -> 111 us
  Pallas kernels: 78.3 us -> 58.5 us
  other arithmetic: 24.3 us -> 5.59 us
  blocking collectives: 11.1 us -> 0 us
  local copies, waits for them, and re-layouts: 22.3 us -> 17.7 us
    ppermute x38 -> x30, waiting for transfers between devices: 106 us -> 58.4 us  [the longest x21 44.7 us: side(): return lax.ppermute(rows, 'req', swap_perm(group, k))]
    pallas_call x12 -> x10, Pallas kernels: 75.4 us -> 55.6 us  [the longest x5 28 us: retain(): pl.pallas_call(lambda *refs: retain_kernel(head, key_dim, value_dim, len(...]
    all_to_all x1, waiting for transfers between devices: 23.9 us -> 38.2 us  [rows_for(): lax.all_to_all(picked.reshape(width, cap, cols), 'req', split_axis=0, con...]
    all_to_all x4 -> x3, waiting for transfers between devices: 1.07 us -> 14.3 us  [the longest x2 8.79 us: send(): lax.all_to_all(answer, 'req', split_axis=0, concat_axis=0, tiled=True)]
    ppermute x1, waiting for transfers between devices: 11.8 us -> 0.01 us  [fast_device(): other = lax.ppermute(half, 'head', [(0, 1), (1, 0)])]
    all_to_all x1 -> x0, blocking collectives: 11.1 us -> none  [token_rows(): lax.all_to_all(table, 'req', split_axis=0, concat_axis=0, tiled=True)]
    select_n x11 -> x0, other arithmetic: 10.7 us -> none  [the longest x8 6.48 us: canonical(): jnp.where(swap, pieces[k ^ bit], pieces[k])]
    concatenate x12 -> x1, other arithmetic: 9.25 us -> 0.04 us  [swaps(): return jnp.concatenate(parts, axis=0)]
  transfers between devices with their start and end apart: 44 -> 35, of which waited for: 13 -> 15; matrix products, arithmetic and copies ran while one was open for 9% -> 7% of each run, Pallas kernels for 22% -> 14%
where the time goes in v2:
time: 254 us; the launch traced here: 252 us
  waiting for transfers between devices  111 us (44%)
  Pallas kernels  58.5 us (23%)
  starting transfers between devices  56.8 us (22%)
  local copies, waits for them, and re-layouts  17.7 us (7%)
  other arithmetic  5.59 us (2%)
    ppermute x21, waiting for transfers between devices, side(): return lax.ppermute(rows, 'req', swap_perm(group, k))  44.7 us
    all_to_all x1, waiting for transfers between devices, rows_for(): lax.all_to_all(picked.reshape(width, cap, cols), 'req', split_axis=0, con...  38.2 us
    pallas_call x5, Pallas kernels, retain(): pl.pallas_call(lambda *refs: retain_kernel(head, key_dim, value_dim, len(...  28 us
    pallas_call x3, Pallas kernels, project(): pl.pallas_call(project_kernel, out_shape=[jax.ShapeDtypeStruct((rows, wid...  20.1 us
    ppermute x21, starting transfers between devices, side(): return lax.ppermute(rows, 'req', swap_perm(group, k))  17.2 us
    ppermute x6, starting transfers between devices, up(): return lax.ppermute(piece, 'req', ring_perm(group, 1))  14.2 us
    all_to_all x2, starting transfers between devices, send(): lax.all_to_all(answer, 'req', split_axis=0, concat_axis=0, tiled=True)  11.4 us
    all_to_all x2, waiting for transfers between devices, send(): lax.all_to_all(answer, 'req', split_axis=0, concat_axis=0, tiled=True)  8.79 us
  transfers between devices with their start and end apart: 35, of which 15 were waited for; matrix products, arithmetic and copies ran while one was open for 7% of the time, Pallas kernels for 14%

profile of v2, /device:TPU:9, one launch (start us, length us, event | category | flops | bytes accessed | tf_op | source)
XLA Modules:
  0.0 252.0 jit_solution(8472428772004293733)
XLA Ops:
  0.6 2.6 %pack.1 = (bf16[128,768]{1,0:T(8,128)(2,1)}, bf16[128,768]{1,0:T(8,128)(2,1)}, bf16[128,768]{1,0:T(8,128)(2,1)}, bf16[128,768]{1,0:T(8,128)(2,1)}, bf16[128,384]...) custom-call(s32[1]{0:T(128)} %bitcast.10.refs_0_.member_ref.refs_3_,, ...), custom_call_target="tpu_custom_call" | custom-call | tf_op jit(solution)/shard_map/pack/pallas_call | solution.py:166
  15.8 5.8 %all-to-all-start.2 = ((s32[16,1,128]{2,1,0:T(1,128)}), s32[16,1,128]{2,1,0:T(1,128)S(1)}, u32[]{:S(2)}, u32[]{:S(2)}) async-start(s32[16,1,128]{2,1,0:T(1,128)} %bitcast.8), calls=%async_computation.2 | async-start | bytes 16384 | tf_op jit(solution)/shard_map/all_to_all | solution.py:118
  21.7 5.5 %all-to-all-done.2 = s32[16,1,128]{2,1,0:T(1,128)S(1)} async-done(((s32[16,1,128]{2,1,0:T(1,128)}), s32[16,1,128]{2,1,0:T(1,128)S(1)}, u32[]{:S(2)}, u32[]{:S(2)}) %all-to-all-start.2) | async-done | bytes 8224 | tf_op jit(solution)/shard_map/all_to_all | solution.py:118
  27.3 7.8 %gather_fusion.2 = bf16[512,1024]{1,0:T(8,128)(2,1)} fusion(bf16[4000,1024]{1,0:T(8,128)(2,1)} %param.14, s32[1024]{0:T(1024)S(1)} %pad_clamp_fusion.3), kind=kCustom, calls=%fused_computation.2 | custom fusion | bytes 2099200 | tf_op jit(solution)/shard_map/jit(_take)/gather | solution.py:97
  35.9 5.3 %all-to-all-start.3 = ((bf16[16,32,1024]{2,1,0:T(8,128)(2,1)}), bf16[16,32,1024]{2,1,0:T(8,128)(2,1)S(1)}, u32[]{:S(2)}, u32[]{:S(2)}) async-start(bf16[16,32,1024]{2,1,0:T(8,128)(2,1)} %bitcast.13), calls=%async_computation.3 | async-start | bytes 2097152 | tf_op jit(solution)/shard_map/all_to_all | solution.py:100
  44.7 38.2 %all-to-all-done.3 = bf16[16,32,1024]{2,1,0:T(8,128)(2,1)S(1)} async-done(((bf16[16,32,1024]{2,1,0:T(8,128)(2,1)}), bf16[16,32,1024]{2,1,0:T(8,128)(2,1)S(1)}, u32[]{:S(2)}, u32[]{:S(2)}) %all-to-all-start.3) | async-done | bytes 1048608 | tf_op jit(solution)/shard_map/all_to_all | solution.py:100
  89.9 10.9 %collective-permute-done.12 = bf16[128,384]{1,0:T(8,128)(2,1)S(1)} collective-permute-done((bf16[128,384]{1,0:T(8,128)(2,1)S(1)}, bf16[128,384]{1,0:T(8,128)(2,1)S(1)}, u32[]{:S(2)}, u32[]{:S(2)}) %collective-permute-start.12) | collective-permute-done | bytes 98336 | tf_op jit(solution)/shard_map/ppermute | solution.py:477
  100.8 2.3 collective-permute-done.13
  106.5 11.7 %collective-permute-done.14.side_far_ref = bf16[256,1024]{1,0:T(8,128)(2,1)S(1)} collective-permute-done((bf16[256,1024]{1,0:T(8,128)(2,1)S(1)}, bf16[256,1024]{1,0:T(8,128)(2,1)S(1)}, u32[]{:S(2)}, u32[]{:S(2)}) %collective-permute-start.14) | collective-permute-done | bytes 524320 | tf_op jit(solution)/shard_map/ppermute | solution.py:477
  118.2 5.6 %collective-permute-done.15.refs_2_ = bf16[512,768]{1,0:T(8,128)(2,1)S(1)} collective-permute-done((bf16[512,768]{1,0:T(8,128)(2,1)}, bf16[512,768]{1,0:T(8,128)(2,1)S(1)}, u32[]{:S(2)}, u32[]{:S(2)}) %collective-permute-start.15) | collective-permute-done | bytes 786464 | tf_op jit(solution)/shard_map/ppermute | solution.py:471
  123.8 4.8 %norm.1.mine_ref = bf16[2,256,2048]{2,1,0:T(8,128)(2,1)} custom-call(s32[1]{0:T(128)} %bitcast.12.low_ref, s32[1]{0:T(128)} %bitcast.10.refs_0_.member_ref.refs_3_, bf16[256,1024]{1,0:T(8,128)(2,1)S(1)} %get-tuple-element.349.own_ref, bf16[256,1024]{1,0:T(8,128)(2,1)} %copy-done.9, bf16[256,1024]{1,0:T(8,128)(2,1)} %copy-done.8, bf16[256,1024]{1,0:T(8,128)(2,1)} %copy-done.10), custom_call_target="tpu_custom_call" | custom-call | tf_op jit(solution)/shard_map/norm/pallas_call | solution.py:215
  128.7 1.5 collective-permute-start.16
  130.3 1.7 collective-permute-start.18
  132.0 2.3 collective-permute-done.16.there_ref
  134.3 8.0 %project.3 = (bf16[256,768]{1,0:T(8,128)(2,1)}, bf16[256,768]{1,0:T(8,128)(2,1)}, bf16[256,768]{1,0:T(8,128)(2,1)}, bf16[256,768]{1,0:T(8,128)(2,1)}) custom-call(s32[1]{0:T(128)} %bitcast.11.zpos_ref, bf16[2,256,2048]{2,1,0:T(8,128)(2,1)} %norm.1.mine_ref, bf16[2,256,2048]{2,1,0:T(8,128)(2,1)} %collective-permute-done.16.there_ref, ...), custom_call_target="tpu_custom_call" | custom-call | flops 3221225472 | bytes 8912896 | tf_op jit(solution)/shard_map/project/pallas_call | solution.py:268
  142.3 7.1 %collective-permute-done.18.refs_3_ = bf16[512,384]{1,0:T(8,128)(2,1)S(1)} collective-permute-done((bf16[512,384]{1,0:T(8,128)(2,1)}, bf16[512,384]{1,0:T(8,128)(2,1)S(1)}, u32[]{:S(2)}, u32[]{:S(2)}) %collective-permute-start.18) | collective-permute-done | bytes 393248 | tf_op jit(solution)/shard_map/ppermute | solution.py:474
  149.4 2.9 %collective-permute-start.23 = (bf16[512,384]{1,0:T(8,128)(2,1)S(1)}, bf16[512,384]{1,0:T(8,128)(2,1)S(1)}, u32[]{:S(2)}, u32[]{:S(2)}) collective-permute-start(bf16[512,384]{1,0:T(8,128)(2,1)S(1)} %pad_maximum_fusion.refs_0_), channel_id=1, source_target_pairs={{0,8},{2,10},{4,12},{6,14},{8,16},{10,18},{12,20},{14,22},{16,24},... | collective-permute-start | bytes 1179656 | tf_op jit(solution)/shard_map/ppermute | solution.py:471
  155.0 6.1 %project.4 = (bf16[256,384]{1,0:T(8,128)(2,1)}, bf16[256,384]{1,0:T(8,128)(2,1)}, bf16[256,384]{1,0:T(8,128)(2,1)}, bf16[256,384]{1,0:T(8,128)(2,1)}) custom-call(s32[1]{0:T(128)} %bitcast.11.zpos_ref, bf16[2,256,2048]{2,1,0:T(8,128)(2,1)} %norm.1.mine_ref, bf16[2,256,2048]{2,1,0:T(8,128)(2,1)} %collective-permute-done.16.there_ref, ...), custom_call_target="tpu_custom_call" | custom-call | flops 1610612736 | bytes 6553600 | tf_op jit(solution)/shard_map/project/pallas_call | solution.py:268
  161.1 8.3 %collective-permute-start.24 = (bf16[512,384]{1,0:T(8,128)(2,1)S(1)}, bf16[512,384]{1,0:T(8,128)(2,1)S(1)}, u32[]{:S(2)}, u32[]{:S(2)}) collective-permute-start(bf16[512,384]{1,0:T(8,128)(2,1)S(1)} %collective-permute-done.23.refs_1_), channel_id=1, source_target_pairs={{0,8},{2,10},{4,12},{6,14},{8,16},{10,18},{12,20},{14,22},{16,24},... | collective-permute-start | bytes 1179656 | tf_op jit(solution)/shard_map/ppermute | solution.py:471
  170.0 2.8 %collective-permute-done.21.refs_7_ = bf16[256,768]{1,0:T(8,128)(2,1)S(1)} collective-permute-done((bf16[256,768]{1,0:T(8,128)(2,1)}, bf16[256,768]{1,0:T(8,128)(2,1)S(1)}, u32[]{:S(2)}, u32[]{:S(2)}) %collective-permute-start.21) | collective-permute-done | bytes 393248 | tf_op jit(solution)/shard_map/ppermute | solution.py:477
  173.6 6.0 %retain.5 = (bf16[16,16,1024]{2,1,0:T(8,128)(2,1)}, bf16[16,4,256,512]{3,2,1,0:T(8,128)(2,1)}) custom-call(s32[16]{0:T(128)} %copy-done.18, s32[16]{0:T(128)} %refs_1_.11, f32[4]{0:T(128)} %negate_log-plus-one_fusion.refs_2_, s32[1]{0:T(128)} %bitcast.10.refs_0_.member_ref.refs_3_, bf16[256,768]{1,0:T(8,128)(2,1)} %get-tuple-element.392.refs_4_, ...), custom_call_target="tpu_custom_call" | custom-call | flops 536870912 | bytes 8388608 | tf_op jit(solution)/shard_map/retain/pallas_call | solution.py:371
  180.4 6.1 %project.5 = (bf16[256,384]{1,0:T(8,128)(2,1)}, bf16[256,384]{1,0:T(8,128)(2,1)}, bf16[256,384]{1,0:T(8,128)(2,1)}, bf16[256,384]{1,0:T(8,128)(2,1)}) custom-call(s32[1]{0:T(128)} %bitcast.11.zpos_ref, bf16[2,256,2048]{2,1,0:T(8,128)(2,1)} %norm.1.mine_ref, bf16[2,256,2048]{2,1,0:T(8,128)(2,1)} %collective-permute-done.16.there_ref, ...), custom_call_target="tpu_custom_call" | custom-call | flops 1610612736 | bytes 6553600 | tf_op jit(solution)/shard_map/project/pallas_call | solution.py:268
  186.5 6.1 %retain.6 = (bf16[16,16,1024]{2,1,0:T(8,128)(2,1)}, bf16[16,4,256,512]{3,2,1,0:T(8,128)(2,1)}) custom-call(s32[16]{0:T(128)} %copy-done.18, s32[16]{0:T(128)} %refs_1_.11, f32[4]{0:T(128)} %negate_log-plus-one_fusion.refs_2_, s32[1]{0:T(128)} %bitcast.10.refs_0_.member_ref.refs_3_, ...), custom_call_target="tpu_custom_call", output_to_operand_aliasing={{0}: (9, {}), {1}: (10, {})} | custom-call | flops 536870912 | bytes 8388608 | tf_op jit(solution)/shard_map/retain/pallas_call | solution.py:371
  192.6 6.2 %all-to-all-start.4 = ((bf16[16,16,1024]{2,1,0:T(8,128)(2,1)}), bf16[16,16,1024]{2,1,0:T(8,128)(2,1)S(1)}, u32[]{:S(2)}, u32[]{:S(2)}) async-start(bf16[16,16,1024]{2,1,0:T(8,128)(2,1)} %get-tuple-element.398), calls=%async_computation.4 | async-start | bytes 1048576 | tf_op jit(solution)/shard_map/all_to_all | solution.py:511
  203.2 6.8 %collective-permute-done.29.refs_6_ = bf16[256,384]{1,0:T(8,128)(2,1)S(1)} collective-permute-done((bf16[256,384]{1,0:T(8,128)(2,1)S(1)}, bf16[256,384]{1,0:T(8,128)(2,1)S(1)}, u32[]{:S(2)}, u32[]{:S(2)}) %collective-permute-start.29) | collective-permute-done | bytes 196640 | tf_op jit(solution)/shard_map/ppermute | solution.py:477
  210.1 5.6 %collective-permute-done.30.refs_7_ = bf16[256,384]{1,0:T(8,128)(2,1)S(1)} collective-permute-done((bf16[256,384]{1,0:T(8,128)(2,1)S(1)}, bf16[256,384]{1,0:T(8,128)(2,1)S(1)}, u32[]{:S(2)}, u32[]{:S(2)}) %collective-permute-start.30) | collective-permute-done | bytes 196640 | tf_op jit(solution)/shard_map/ppermute | solution.py:477
  216.3 6.0 %retain.7 = (bf16[16,16,1024]{2,1,0:T(8,128)(2,1)}, bf16[16,4,256,512]{3,2,1,0:T(8,128)(2,1)}) custom-call(s32[16]{0:T(128)} %copy-done.18, s32[16]{0:T(128)} %refs_1_.11, f32[4]{0:T(128)} %negate_log-plus-one_fusion.refs_2_, s32[1]{0:T(128)} %bitcast.10.refs_0_.member_ref.refs_3_, ...), custom_call_target="tpu_custom_call", output_to_operand_aliasing={{1}: (9, {})} | custom-call | flops 536870912 | bytes 8388608 | tf_op jit(solution)/shard_map/retain/pallas_call | solution.py:371
  224.3 4.7 %retain.8 = bf16[16,16,1024]{2,1,0:T(8,128)(2,1)} custom-call(s32[16]{0:T(128)} %copy-done.18, s32[16]{0:T(128)} %refs_1_.11, f32[4]{0:T(128)} %negate_log-plus-one_fusion.refs_2_, s32[1]{0:T(128)} %bitcast.10.refs_0_.member_ref.refs_3_, bf16[256,384]{1,0:T(8,128)(2,1)} %get-tuple-element.399.refs_4_, ...), custom_call_target="tpu_custom_call", output_to_operand_aliasing={{}: (9, {})} | custom-call | flops 536870912 | bytes 4194304 | tf_op jit(solution)/shard_map/retain/pallas_call | solution.py:371
  228.9 5.2 %all-to-all-start.5 = ((bf16[16,16,1024]{2,1,0:T(8,128)(2,1)}), bf16[16,16,1024]{2,1,0:T(8,128)(2,1)S(1)}, u32[]{:S(2)}, u32[]{:S(2)}) async-start(bf16[16,16,1024]{2,1,0:T(8,128)(2,1)} %retain.8), calls=%async_computation.5 | async-start | bytes 1048576 | tf_op jit(solution)/shard_map/all_to_all | solution.py:511
  234.1 5.4 %retain.9 = bf16[16,4,256,512]{3,2,1,0:T(8,128)(2,1)} custom-call(s32[16]{0:T(128)} %copy-done.18, s32[16]{0:T(128)} %refs_1_.11, f32[4]{0:T(128)} %negate_log-plus-one_fusion.refs_2_, s32[1]{0:T(128)} %bitcast.10.refs_0_.member_ref.refs_3_, bf16[256,384]{1,0:T(8,128)(2,1)} %get-tuple-element.399.refs_4_, ...), custom_call_target="tpu_custom_call", output_to_operand_aliasing={{}: (9, {})} | custom-call | flops 536870912 | bytes 8388608 | tf_op jit(solution)/shard_map/retain/pallas_call | solution.py:371
  239.5 8.8 %all-to-all-done.5.refs_1_ = bf16[16,16,1024]{2,1,0:T(8,128)(2,1)S(1)} async-done(((bf16[16,16,1024]{2,1,0:T(8,128)(2,1)}), bf16[16,16,1024]{2,1,0:T(8,128)(2,1)S(1)}, u32[]{:S(2)}, u32[]{:S(2)}) %all-to-all-start.5) | async-done | bytes 524320 | tf_op jit(solution)/shard_map/all_to_all | solution.py:511
  249.1 2.9 %settle.1 = bf16[16,16,2048]{2,1,0:T(8,128)(2,1)} custom-call(s32[16]{0:T(128)} %get-tuple-element.411.place_ref, bf16[16,16,1024]{2,1,0:T(8,128)(2,1)} %copy-done, bf16[16,16,1024]{2,1,0:T(8,128)(2,1)} %copy-done.1), custom_call_target="tpu_custom_call" | custom-call | tf_op jit(solution)/shard_map/settle/pallas_call | solution.py:409
  (159 shorter events, 39.4 us)
Async XLA Ops:
  3.3 10.2 %collective-permute-start.3 = (bf16[128,384]{1,0:T(8,128)(2,1)}, bf16[128,384]{1,0:T(8,128)(2,1)S(1)}, u32[]{:S(2)}, u32[]{:S(2)}) collective-permute-start(bf16[128,384]{1,0:T(8,128)(2,1)} %get-tuple-element.337), channel_id=1, source_target_pairs={{0,2},{2,0},{4,6},{6,4},{8,10},{10,8},{12,14},{14,12},{16,18},{18,... | collective-permute-start | bytes 294920 | tf_op jit(solution)/shard_map/ppermute | solution.py:477
  3.9 10.3 %collective-permute-start.4 = (bf16[128,384]{1,0:T(8,128)(2,1)}, bf16[128,384]{1,0:T(8,128)(2,1)S(1)}, u32[]{:S(2)}, u32[]{:S(2)}) collective-permute-start(bf16[128,384]{1,0:T(8,128)(2,1)} %get-tuple-element.338), channel_id=1, source_target_pairs={{0,4},{2,6},{4,0},{6,2},{8,12},{10,14},{12,8},{14,10},{16,20},{18,... | collective-permute-start | bytes 294920 | tf_op jit(solution)/shard_map/ppermute | solution.py:477
  5.1 9.2 %collective-permute-start.5 = (bf16[128,384]{1,0:T(8,128)(2,1)}, bf16[128,384]{1,0:T(8,128)(2,1)S(1)}, u32[]{:S(2)}, u32[]{:S(2)}) collective-permute-start(bf16[128,384]{1,0:T(8,128)(2,1)} %get-tuple-element.339), channel_id=1, source_target_pairs={{0,6},{2,4},{4,2},{6,0},{8,14},{10,12},{12,10},{14,8},{16,22},{18,... | collective-permute-start | bytes 294920 | tf_op jit(solution)/shard_map/ppermute | solution.py:477
  5.6 10.1 %collective-permute-start = (bf16[128,768]{1,0:T(8,128)(2,1)}, bf16[128,768]{1,0:T(8,128)(2,1)S(1)}, u32[]{:S(2)}, u32[]{:S(2)}) collective-permute-start(bf16[128,768]{1,0:T(8,128)(2,1)} %get-tuple-element.333), channel_id=1, source_target_pairs={{0,2},{2,0},{4,6},{6,4},{8,10},{10,8},{12,14},{14,12},{16,18},{18,... | collective-permute-start | bytes 589832 | tf_op jit(solution)/shard_map/ppermute | solution.py:477
  5.8 9.9 %collective-permute-start.1 = (bf16[128,768]{1,0:T(8,128)(2,1)}, bf16[128,768]{1,0:T(8,128)(2,1)S(1)}, u32[]{:S(2)}, u32[]{:S(2)}) collective-permute-start(bf16[128,768]{1,0:T(8,128)(2,1)} %get-tuple-element.334), channel_id=1, source_target_pairs={{0,4},{2,6},{4,0},{6,2},{8,12},{10,14},{12,8},{14,10},{16,20},{18,... | collective-permute-start | bytes 589832 | tf_op jit(solution)/shard_map/ppermute | solution.py:477
  13.4 8.2 %collective-permute-start.2 = (bf16[128,768]{1,0:T(8,128)(2,1)}, bf16[128,768]{1,0:T(8,128)(2,1)S(1)}, u32[]{:S(2)}, u32[]{:S(2)}) collective-permute-start(bf16[128,768]{1,0:T(8,128)(2,1)} %get-tuple-element.335), channel_id=1, source_target_pairs={{0,6},{2,4},{4,2},{6,0},{8,14},{10,12},{12,10},{14,8},{16,22},{18,... | collective-permute-start | bytes 589832 | tf_op jit(solution)/shard_map/ppermute | solution.py:477
  14.4 20.7 %collective-permute-start.6 = (bf16[512,384]{1,0:T(8,128)(2,1)S(1)}, bf16[512,384]{1,0:T(8,128)(2,1)S(1)}, u32[]{:S(2)}, u32[]{:S(2)}) collective-permute-start(bf16[512,384]{1,0:T(8,128)(2,1)S(1)} %constant_dynamic-update-slice_fusion.4.refs_0_), channel_id=1, source_target_pairs={{0,8},{2,10},{4,12},{6,14},{8,16},{10,18},{12,20},{14,22},{16,24},... | collective-permute-start | bytes 1179656 | tf_op jit(solution)/shard_map/ppermute | solution.py:471
  15.8 11.4 %all-to-all-start.2 = ((s32[16,1,128]{2,1,0:T(1,128)}), s32[16,1,128]{2,1,0:T(1,128)S(1)}, u32[]{:S(2)}, u32[]{:S(2)}) async-start(s32[16,1,128]{2,1,0:T(1,128)} %bitcast.8), calls=%async_computation.2 | async-start | bytes 16384 | tf_op jit(solution)/shard_map/all_to_all | solution.py:118
  35.9 47.0 %all-to-all-start.3 = ((bf16[16,32,1024]{2,1,0:T(8,128)(2,1)}), bf16[16,32,1024]{2,1,0:T(8,128)(2,1)S(1)}, u32[]{:S(2)}, u32[]{:S(2)}) async-start(bf16[16,32,1024]{2,1,0:T(8,128)(2,1)} %bitcast.13), calls=%async_computation.3 | async-start | bytes 2097152 | tf_op jit(solution)/shard_map/all_to_all | solution.py:100
  41.1 42.9 %collective-permute-start.7 = (bf16[512,768]{1,0:T(8,128)(2,1)S(1)}, bf16[512,768]{1,0:T(8,128)(2,1)}, u32[]{:S(2)}, u32[]{:S(2)}) collective-permute-start(bf16[512,768]{1,0:T(8,128)(2,1)S(1)} %constant_dynamic-update-slice_fusion.refs_0_), channel_id=1, source_target_pairs={{0,8},{2,10},{4,12},{6,14},{8,16},{10,18},{12,20},{14,22},{16,24},... | collective-permute-start | bytes 2359304 | tf_op jit(solution)/shard_map/ppermute | solution.py:471
  84.8 19.4 %collective-permute-start.10 = (bf16[512,768]{1,0:T(8,128)(2,1)S(1)}, bf16[512,768]{1,0:T(8,128)(2,1)S(1)}, u32[]{:S(2)}, u32[]{:S(2)}) collective-permute-start(bf16[512,768]{1,0:T(8,128)(2,1)S(1)} %constant_dynamic-update-slice_fusion.refs_0_), channel_id=1, source_target_pairs={{0,24},{2,26},{4,28},{6,30},{8,0},{10,2},{12,4},{14,6},{16,8},{18,... | collective-permute-start | bytes 2359304 | tf_op jit(solution)/shard_map/ppermute | solution.py:474
  84.9 18.3 %collective-permute-start.9 = (bf16[256,1024]{1,0:T(8,128)(2,1)S(1)}, bf16[256,1024]{1,0:T(8,128)(2,1)S(1)}, u32[]{:S(2)}, u32[]{:S(2)}) collective-permute-start(bf16[256,1024]{1,0:T(8,128)(2,1)S(1)} %get-tuple-element.349.own_ref), channel_id=1, source_target_pairs={{0,4},{2,6},{4,0},{6,2},{8,12},{10,14},{12,8},{14,10},{16,20},{18,... | collective-permute-start | bytes 1572872 | tf_op jit(solution)/shard_map/ppermute | solution.py:477
  86.2 17.0 %collective-permute-start.8 = (bf16[256,1024]{1,0:T(8,128)(2,1)S(1)}, bf16[256,1024]{1,0:T(8,128)(2,1)S(1)}, u32[]{:S(2)}, u32[]{:S(2)}) collective-permute-start(bf16[256,1024]{1,0:T(8,128)(2,1)S(1)} %get-tuple-element.349.own_ref), channel_id=1, source_target_pairs={{0,1},{1,0},{2,3},{3,2},{4,5},{5,4},{6,7},{7,6},{8,9},{9,8},{10,11... | collective-permute-start | bytes 1572872 | tf_op jit(solution)/shard_map/ppermute | solution.py:493
  88.2 12.6 %collective-permute-start.12 = (bf16[128,384]{1,0:T(8,128)(2,1)S(1)}, bf16[128,384]{1,0:T(8,128)(2,1)S(1)}, u32[]{:S(2)}, u32[]{:S(2)}) collective-permute-start(bf16[128,384]{1,0:T(8,128)(2,1)S(1)} %copy-done.34), channel_id=1, source_target_pairs={{0,4},{2,6},{4,0},{6,2},{8,12},{10,14},{12,8},{14,10},{16,20},{18,... | collective-permute-start | bytes 294920 | tf_op jit(solution)/shard_map/ppermute | solution.py:477
  89.1 14.0 %collective-permute-start.13 = (bf16[128,384]{1,0:T(8,128)(2,1)S(1)}, bf16[128,384]{1,0:T(8,128)(2,1)S(1)}, u32[]{:S(2)}, u32[]{:S(2)}) collective-permute-start(bf16[128,384]{1,0:T(8,128)(2,1)S(1)} %copy-done.33), channel_id=1, source_target_pairs={{0,6},{2,4},{4,2},{6,0},{8,14},{10,12},{12,10},{14,8},{16,22},{18,... | collective-permute-start | bytes 294920 | tf_op jit(solution)/shard_map/ppermute | solution.py:477
  105.1 18.7 %collective-permute-start.15 = (bf16[512,768]{1,0:T(8,128)(2,1)}, bf16[512,768]{1,0:T(8,128)(2,1)S(1)}, u32[]{:S(2)}, u32[]{:S(2)}) collective-permute-start(bf16[512,768]{1,0:T(8,128)(2,1)} %collective-permute-done.7.refs_1_), channel_id=1, source_target_pairs={{0,8},{2,10},{4,12},{6,14},{8,16},{10,18},{12,20},{14,22},{16,24},... | collective-permute-start | bytes 2359304 | tf_op jit(solution)/shard_map/ppermute | solution.py:471
  105.3 12.9 %collective-permute-start.14 = (bf16[256,1024]{1,0:T(8,128)(2,1)S(1)}, bf16[256,1024]{1,0:T(8,128)(2,1)S(1)}, u32[]{:S(2)}, u32[]{:S(2)}) collective-permute-start(bf16[256,1024]{1,0:T(8,128)(2,1)S(1)} %collective-permute-done.8.own_far_ref), channel_id=1, source_target_pairs={{0,4},{2,6},{4,0},{6,2},{8,12},{10,14},{12,8},{14,10},{16,20},{18,... | collective-permute-start | bytes 1572872 | tf_op jit(solution)/shard_map/ppermute | solution.py:477
  130.1 12.1 %collective-permute-start.17 = (bf16[512,384]{1,0:T(8,128)(2,1)}, bf16[512,384]{1,0:T(8,128)(2,1)S(1)}, u32[]{:S(2)}, u32[]{:S(2)}) collective-permute-start(bf16[512,384]{1,0:T(8,128)(2,1)} %copy-done.21), channel_id=1, source_target_pairs={{0,8},{2,10},{4,12},{6,14},{8,16},{10,18},{12,20},{14,22},{16,24},... | collective-permute-start | bytes 1179656 | tf_op jit(solution)/shard_map/ppermute | solution.py:471
  130.3 19.1 %collective-permute-start.18 = (bf16[512,384]{1,0:T(8,128)(2,1)}, bf16[512,384]{1,0:T(8,128)(2,1)S(1)}, u32[]{:S(2)}, u32[]{:S(2)}) collective-permute-start(bf16[512,384]{1,0:T(8,128)(2,1)} %copy-done.17), channel_id=1, source_target_pairs={{0,24},{2,26},{4,28},{6,30},{8,0},{10,2},{12,4},{14,6},{16,8},{18,... | collective-permute-start | bytes 1179656 | tf_op jit(solution)/shard_map/ppermute | solution.py:474
  149.4 11.7 %collective-permute-start.23 = (bf16[512,384]{1,0:T(8,128)(2,1)S(1)}, bf16[512,384]{1,0:T(8,128)(2,1)S(1)}, u32[]{:S(2)}, u32[]{:S(2)}) collective-permute-start(bf16[512,384]{1,0:T(8,128)(2,1)S(1)} %pad_maximum_fusion.refs_0_), channel_id=1, source_target_pairs={{0,8},{2,10},{4,12},{6,14},{8,16},{10,18},{12,20},{14,22},{16,24},... | collective-permute-start | bytes 1179656 | tf_op jit(solution)/shard_map/ppermute | solution.py:471
  152.3 20.6 %collective-permute-start.22 = (bf16[512,384]{1,0:T(8,128)(2,1)S(1)}, bf16[512,384]{1,0:T(8,128)(2,1)S(1)}, u32[]{:S(2)}, u32[]{:S(2)}) collective-permute-start(bf16[512,384]{1,0:T(8,128)(2,1)S(1)} %pad_maximum_fusion.refs_0_), channel_id=1, source_target_pairs={{0,24},{2,26},{4,28},{6,30},{8,0},{10,2},{12,4},{14,6},{16,8},{18,... | collective-permute-start | bytes 1179656 | tf_op jit(solution)/shard_map/ppermute | solution.py:474
  152.3 17.7 %collective-permute-start.19 = (bf16[256,768]{1,0:T(8,128)(2,1)}, bf16[256,768]{1,0:T(8,128)(2,1)S(1)}, u32[]{:S(2)}, u32[]{:S(2)}) collective-permute-start(bf16[256,768]{1,0:T(8,128)(2,1)} %get-tuple-element.368), channel_id=1, source_target_pairs={{0,2},{2,0},{4,6},{6,4},{8,10},{10,8},{12,14},{14,12},{16,18},{18,... | collective-permute-start | bytes 1179656 | tf_op jit(solution)/shard_map/ppermute | solution.py:477
  153.4 16.6 %collective-permute-start.20 = (bf16[256,768]{1,0:T(8,128)(2,1)}, bf16[256,768]{1,0:T(8,128)(2,1)S(1)}, u32[]{:S(2)}, u32[]{:S(2)}) collective-permute-start(bf16[256,768]{1,0:T(8,128)(2,1)} %get-tuple-element.369), channel_id=1, source_target_pairs={{0,4},{2,6},{4,0},{6,2},{8,12},{10,14},{12,8},{14,10},{16,20},{18,... | collective-permute-start | bytes 1179656 | tf_op jit(solution)/shard_map/ppermute | solution.py:477
  154.4 18.4 %collective-permute-start.21 = (bf16[256,768]{1,0:T(8,128)(2,1)}, bf16[256,768]{1,0:T(8,128)(2,1)S(1)}, u32[]{:S(2)}, u32[]{:S(2)}) collective-permute-start(bf16[256,768]{1,0:T(8,128)(2,1)} %get-tuple-element.370), channel_id=1, source_target_pairs={{0,6},{2,4},{4,2},{6,0},{8,14},{10,12},{12,10},{14,8},{16,22},{18,... | collective-permute-start | bytes 1179656 | tf_op jit(solution)/shard_map/ppermute | solution.py:477
  161.1 18.5 %collective-permute-start.24 = (bf16[512,384]{1,0:T(8,128)(2,1)S(1)}, bf16[512,384]{1,0:T(8,128)(2,1)S(1)}, u32[]{:S(2)}, u32[]{:S(2)}) collective-permute-start(bf16[512,384]{1,0:T(8,128)(2,1)S(1)} %collective-permute-done.23.refs_1_), channel_id=1, source_target_pairs={{0,8},{2,10},{4,12},{6,14},{8,16},{10,18},{12,20},{14,22},{16,24},... | collective-permute-start | bytes 1179656 | tf_op jit(solution)/shard_map/ppermute | solution.py:471
  192.6 36.4 %all-to-all-start.4 = ((bf16[16,16,1024]{2,1,0:T(8,128)(2,1)}), bf16[16,16,1024]{2,1,0:T(8,128)(2,1)S(1)}, u32[]{:S(2)}, u32[]{:S(2)}) async-start(bf16[16,16,1024]{2,1,0:T(8,128)(2,1)} %get-tuple-element.398), calls=%async_computation.4 | async-start | bytes 1048576 | tf_op jit(solution)/shard_map/all_to_all | solution.py:511
  199.2 10.9 %collective-permute-start.29 = (bf16[256,384]{1,0:T(8,128)(2,1)S(1)}, bf16[256,384]{1,0:T(8,128)(2,1)S(1)}, u32[]{:S(2)}, u32[]{:S(2)}) collective-permute-start(bf16[256,384]{1,0:T(8,128)(2,1)S(1)} %copy-done.28), channel_id=1, source_target_pairs={{0,4},{2,6},{4,0},{6,2},{8,12},{10,14},{12,8},{14,10},{16,20},{18,... | collective-permute-start | bytes 589832 | tf_op jit(solution)/shard_map/ppermute | solution.py:477
  200.4 15.2 %collective-permute-start.30 = (bf16[256,384]{1,0:T(8,128)(2,1)S(1)}, bf16[256,384]{1,0:T(8,128)(2,1)S(1)}, u32[]{:S(2)}, u32[]{:S(2)}) collective-permute-start(bf16[256,384]{1,0:T(8,128)(2,1)S(1)} %copy-done.27), channel_id=1, source_target_pairs={{0,6},{2,4},{4,2},{6,0},{8,14},{10,12},{12,10},{14,8},{16,22},{18,... | collective-permute-start | bytes 589832 | tf_op jit(solution)/shard_map/ppermute | solution.py:477
  201.0 21.3 %collective-permute-start.25 = (bf16[256,384]{1,0:T(8,128)(2,1)S(1)}, bf16[256,384]{1,0:T(8,128)(2,1)S(1)}, u32[]{:S(2)}, u32[]{:S(2)}) collective-permute-start(bf16[256,384]{1,0:T(8,128)(2,1)S(1)} %copy-done.32), channel_id=1, source_target_pairs={{0,2},{2,0},{4,6},{6,4},{8,10},{10,8},{12,14},{14,12},{16,18},{18,... | collective-permute-start | bytes 589832 | tf_op jit(solution)/shard_map/ppermute | solution.py:477
  201.1 21.2 %collective-permute-start.26 = (bf16[256,384]{1,0:T(8,128)(2,1)S(1)}, bf16[256,384]{1,0:T(8,128)(2,1)S(1)}, u32[]{:S(2)}, u32[]{:S(2)}) collective-permute-start(bf16[256,384]{1,0:T(8,128)(2,1)S(1)} %copy-done.31), channel_id=1, source_target_pairs={{0,4},{2,6},{4,0},{6,2},{8,12},{10,14},{12,8},{14,10},{16,20},{18,... | collective-permute-start | bytes 589832 | tf_op jit(solution)/shard_map/ppermute | solution.py:477
  202.3 21.3 %collective-permute-start.27 = (bf16[256,384]{1,0:T(8,128)(2,1)S(1)}, bf16[256,384]{1,0:T(8,128)(2,1)S(1)}, u32[]{:S(2)}, u32[]{:S(2)}) collective-permute-start(bf16[256,384]{1,0:T(8,128)(2,1)S(1)} %copy-done.30), channel_id=1, source_target_pairs={{0,6},{2,4},{4,2},{6,0},{8,14},{10,12},{12,10},{14,8},{16,22},{18,... | collective-permute-start | bytes 589832 | tf_op jit(solution)/shard_map/ppermute | solution.py:477
  228.9 19.3 %all-to-all-start.5 = ((bf16[16,16,1024]{2,1,0:T(8,128)(2,1)}), bf16[16,16,1024]{2,1,0:T(8,128)(2,1)S(1)}, u32[]{:S(2)}, u32[]{:S(2)}) async-start(bf16[16,16,1024]{2,1,0:T(8,128)(2,1)} %retain.8), calls=%async_computation.5 | async-start | bytes 1048576 | tf_op jit(solution)/shard_map/all_to_all | solution.py:511
  (39 other events, 512.0 us)

commit v3 on v2

--- a/solution.py
+++ b/solution.py
@@ -69,74 +69,79 @@
     return lax.optimization_barrier((value, needed))[0]
 
 
-def token_rows(draft_ids, worker_slot, embedding, asked=None, found=None):
-    width = lax.axis_size("req")
-    own_rows, draft_len = draft_ids.shape
-    count = own_rows * draft_len
-    vocab_rows, cols = embedding.shape
-    cap = -(-2 * count // width)
-    lanes = -(-(cap + 2) // 128) * 128
-    ids = draft_ids.reshape(count)
-    holder = ids // vocab_rows
-    local = ids - holder * vocab_rows
-    order = jnp.arange(count, dtype=jnp.int32)
-    same = ids[:, None] == ids[None, :]
-    first_at = jnp.min(jnp.where(same, order[None, :], count), axis=1)
-    is_first = first_at == order
-    peers = is_first[None, :] & (holder[:, None] == holder[None, :])
-    rank = jnp.sum((peers & (order[None, :] < first_at[:, None])).astype(jnp.int32), axis=1)
-    most = jnp.max(jnp.sum(peers.astype(jnp.int32), axis=1))
-    own_rounds = (most + cap - 1) // cap
-
-    def requests(turn):
-        spot = jnp.where(is_first & (rank // cap == turn), holder * cap + rank % cap, -1)
-        hit = spot[None, :] == jnp.arange(width * cap, dtype=jnp.int32)[:, None]
-        return jnp.sum(jnp.where(hit, local[None, :], 0), axis=1).reshape(width, cap)
-
-    def rows_for(wanted, needed=None):
-        picked = jnp.take(embedding, wanted.reshape(width * cap), axis=0, mode="clip")
+class Asked:
+    def __init__(self, draft_ids, worker_slot, embedding):
+        self.embedding = embedding
+        self.width = width = lax.axis_size("req")
+        own_rows, draft_len = draft_ids.shape
+        count = own_rows * draft_len
+        vocab_rows, self.cols = embedding.shape
+        self.cap = cap = -(-2 * count // width)
+        lanes = -(-(cap + 2) // 128) * 128
+        ids = draft_ids.reshape(count)
+        self.holder = holder = ids // vocab_rows
+        self.local = ids - holder * vocab_rows
+        order = jnp.arange(count, dtype=jnp.int32)
+        same = ids[:, None] == ids[None, :]
+        first_at = jnp.min(jnp.where(same, order[None, :], count), axis=1)
+        self.is_first = is_first = first_at == order
+        peers = is_first[None, :] & (holder[:, None] == holder[None, :])
+        self.rank = jnp.sum((peers & (order[None, :] < first_at[:, None])).astype(jnp.int32), axis=1)
+        most = jnp.max(jnp.sum(peers.astype(jnp.int32), axis=1))
+        own_rounds = (most + cap - 1) // cap
+        target = worker_slot // own_rows
+        place = worker_slot - target * own_rows
+        to_target = target[None, :] == jnp.arange(width, dtype=jnp.int32)[:, None]
+        place_for = jnp.sum(jnp.where(to_target, place[None, :], 0), axis=1)
+        self.table = jnp.concatenate(
+            [
+                self.requests(0),
+                place_for[:, None],
+                jnp.full((width, 1), own_rounds, jnp.int32),
+                jnp.zeros((width, lanes - cap - 2), jnp.int32),
+            ],
+            axis=1,
+        )
+
+    def requests(self, turn):
+        cap = self.cap
+        now = self.is_first & (self.rank // cap == turn)
+        spot = jnp.where(now, self.holder * cap + self.rank % cap, -1)
+        hit = spot[None, :] == jnp.arange(self.width * cap, dtype=jnp.int32)[:, None]
+        return jnp.sum(jnp.where(hit, self.local[None, :], 0), axis=1).reshape(self.width, cap)
+
+    def rows_for(self, wanted, needed=None):
+        rows = self.width * self.cap
+        picked = jnp.take(self.embedding, wanted.reshape(rows), axis=0, mode="clip")
         if needed is not None:
             picked = after(picked, needed)
-        got = lax.all_to_all(
-            picked.reshape(width, cap, cols), "req", split_axis=0, concat_axis=0, tiled=True
-        )
-        return jnp.take(got.reshape(width * cap, cols), holder * cap + rank % cap, axis=0, mode="clip")
-
-    target = worker_slot // own_rows
-    place = worker_slot - target * own_rows
-    to_target = target[None, :] == jnp.arange(width, dtype=jnp.int32)[:, None]
-    place_for = jnp.sum(jnp.where(to_target, place[None, :], 0), axis=1)
-    table = jnp.concatenate(
-        [
-            requests(0),
-            place_for[:, None],
-            jnp.full((width, 1), own_rounds, jnp.int32),
-            jnp.zeros((width, lanes - cap - 2), jnp.int32),
-        ],
-        axis=1,
-    )
-    heard = lax.all_to_all(table, "req", split_axis=0, concat_axis=0, tiled=True)
-    if asked is not None:
-        heard = after(heard, asked)
-    place_of = heard[:, cap]
-    rounds = jnp.max(heard[:, cap + 1])
-    tokens = rows_for(heard[:, :cap], found)
-
-    def more(carry):
-        return carry[0] < rounds
-
-    def step(carry):
-        turn, held = carry
-        wanted = lax.all_to_all(
-            requests(turn), "req", split_axis=0, concat_axis=0, tiled=True
-        )
-        fresh = rows_for(wanted)
-        return turn + 1, jnp.where((rank // cap == turn)[:, None], fresh, held)
-
-    def finish(first):
-        return lax.while_loop(more, step, (jnp.int32(1), first))[1]
-
-    return tokens, finish, place_of
+        got = trade(picked.reshape(self.width, self.cap, self.cols)).reshape(rows, self.cols)
+        return jnp.take(got, self.holder * self.cap + self.rank % self.cap, axis=0, mode="clip")
+
+    def fetch(self, asked=None, found=None):
+        heard = trade(self.table)
+        if asked is not None:
+            heard = after(heard, asked)
+        place_of = heard[:, self.cap]
+        rounds = jnp.max(heard[:, self.cap + 1])
+        first = self.rows_for(heard[:, : self.cap], found)
+
+        def step(carry):
+            turn, held = carry
+            fresh = self.rows_for(trade(self.requests(turn)))
+            return turn + 1, jnp.where((self.rank // self.cap == turn)[:, None], fresh, held)
+
+        def finish(rows):
+            return lax.while_loop(lambda carry: carry[0] < rounds, step, (jnp.int32(1), rows))[1]
+
+        return first, finish, place_of
+
+
+def trade(table):
+    return lax.all_to_all(table, "req", split_axis=0, concat_axis=0, tiled=True)
+
+
+BRIEF = pl.CostEstimate(flops=1, bytes_accessed=1, transcendentals=0)
 
 
 def pack_kernel(heads, chunks, group, member_ref, q_ref, k_ref, v_ref, g_ref, *refs):
@@ -173,6 +178,7 @@
             out_specs=[pl.BlockSpec(shape, lambda i, *_: (0, 0)) for shape in shapes],
             scratch_shapes=[pltpu.VMEM((heads, rows, width), jnp.bfloat16)],
         ),
+        cost_estimate=BRIEF,
         name="pack",
     )(member, *tables)
     return [flat[c * group : (c + 1) * group] for c in range(len(chunks))]
@@ -221,23 +227,26 @@
             in_specs=[spec] * 4,
             out_specs=pl.BlockSpec((2, block, 2 * half), lambda i, *_: (0, i, 0)),
         ),
+        cost_estimate=BRIEF,
         name="norm",
     )(low, member, own, own_far, side, side_far)
 
 
-def project_kernel(zpos_ref, mine_ref, there_ref, *refs):
-    count = (len(refs)) // 2
+def project_kernel(count, zpos_ref, mine_ref, there_ref, *refs):
     pieces, outs = refs[:count], refs[count:]
-    depth = pieces[0].shape[0]
-    rows = mine_ref.shape[1]
+    rows, size = mine_ref.shape[1:]
+    depth = size // ZLEN
     quarter = depth // 4
+    share = outs[0].shape[1]
 
     def product(x_ref, swapped):
         total = None
-        for step, piece in enumerate(pieces):
-            shard = lax.rem(zpos_ref[0] + (count - step), count)
-            start = pl.multiple_of(shard * depth, 128)
-            table = piece[...]
+        for step in range(ZLEN):
+            if count == 1:
+                table, start = pieces[0][step * depth : (step + 1) * depth], step * depth
+            else:
+                shard = lax.rem(zpos_ref[0] + (ZLEN - step), ZLEN)
+                table, start = pieces[step][...], pl.multiple_of(shard * depth, 128)
             if swapped:
                 order = (1, 0, 3, 2)
                 table = jnp.concatenate(
@@ -248,40 +257,41 @@
             total = term if total is None else total + term
         return total.astype(jnp.bfloat16)
 
+    def keep(got, k):
+        for spot in range(len(outs) // 4):
+            for half in range(2):
+                outs[spot * 4 + k + 2 * half][...] = got[
+                    half * rows : (half + 1) * rows, spot * share : (spot + 1) * share
+                ]
+
     @pl.when(pl.program_id(0) == 0)
     def _():
-        got = product(mine_ref, False)
-        outs[0][...] = got[:rows]
-        outs[2][...] = got[rows:]
+        keep(product(mine_ref, False), 0)
 
     @pl.when(pl.program_id(0) == 1)
     def _():
-        got = product(there_ref, True)
-        outs[1][...] = got[:rows]
-        outs[3][...] = got[rows:]
-
-
-def project(zpos, mine, there, pieces):
+        keep(product(there_ref, True), 1)
+
+
+def project(zpos, mine, there, pieces, count=1):
     _, rows, size = mine.shape
     width = pieces[0].shape[1]
     whole = pl.BlockSpec(mine.shape, lambda i, z: (0, 0, 0))
-    return pl.pallas_call(
-        project_kernel,
-        out_shape=[jax.ShapeDtypeStruct((rows, width), jnp.bfloat16)] * 4,
+    shape = (rows, width // count)
+    outs = pl.pallas_call(
+        lambda *refs: project_kernel(len(pieces), *refs),
+        out_shape=[jax.ShapeDtypeStruct(shape, jnp.bfloat16)] * (4 * count),
         grid_spec=pltpu.PrefetchScalarGridSpec(
             num_scalar_prefetch=1,
             grid=(2,),
             in_specs=[whole, whole]
             + [pl.BlockSpec(piece.shape, lambda i, z: (0, 0)) for piece in pieces],
-            out_specs=[pl.BlockSpec((rows, width), lambda i, z: (0, 0))] * 4,
-        ),
-        cost_estimate=pl.CostEstimate(
-            flops=8 * rows * width * size,
-            bytes_accessed=2 * (4 * rows * size + size * width + 4 * rows * width),
-            transcendentals=0,
-        ),
+            out_specs=[pl.BlockSpec(shape, lambda i, z: (0, 0))] * (4 * count),
+        ),
+        cost_estimate=BRIEF,
         name="project",
     )(zpos, mine, there, *pieces)
+    return [outs[spot * 4 : spot * 4 + 4] for spot in range(count)]
 
 
 GROUP = 8
@@ -384,30 +394,28 @@
             out_specs=out_specs,
         ),
         input_output_aliases=aliases,
-        cost_estimate=pl.CostEstimate(
-            flops=2 * rows * draft * key_dim * value_dim * 8,
-            bytes_accessed=2 * rows * key_dim * value_dim * (1 + do_update),
-            transcendentals=0,
-        ),
+        cost_estimate=BRIEF,
         name="retain",
     )(*scalars, *parts, state, *more)
 
 
-def settle_kernel(place_ref, *refs):
+def settle_kernel(order, place_ref, *refs):
     parts, out_ref = refs[:-1], refs[-1]
+    value_dim = out_ref.shape[2] // sum(len(heads) for heads in order)
     for s in range(parts[0].shape[0]):
         row = place_ref[s]
-        at = 0
-        for part in parts:
-            out_ref[row, :, at : at + part.shape[2]] = part[s]
-            at += part.shape[2]
-
-
-def settle(place_of, parts):
+        for part, heads in zip(parts, order):
+            for spot, j in enumerate(heads):
+                out_ref[row, :, j * value_dim : (j + 1) * value_dim] = part[
+                    s, :, spot * value_dim : (spot + 1) * value_dim
+                ]
+
+
+def settle(place_of, order, parts):
     rows, draft, _ = parts[0].shape
     whole = (rows, draft, sum(part.shape[2] for part in parts))
     return pl.pallas_call(
-        settle_kernel,
+        lambda *refs: settle_kernel(order, *refs),
         out_shape=jax.ShapeDtypeStruct(whole, jnp.bfloat16),
         grid_spec=pltpu.PrefetchScalarGridSpec(
             num_scalar_prefetch=1,
@@ -415,6 +423,7 @@
             in_specs=[pl.BlockSpec(part.shape, lambda i, *_: (0, 0, 0)) for part in parts],
             out_specs=pl.BlockSpec(whole, lambda i, *_: (0, 0, 0)),
         ),
+        cost_estimate=BRIEF,
         name="settle",
     )(place_of, *parts)
 
@@ -461,7 +470,8 @@
     scalars = (target, accepted, log_rate, me)
 
     chunks = ((0, 1), (2,), (3,))
-    packed = pack(heads, chunks, group, me, (w_query, w_key, w_value, w_gate))
+    tokens = Asked(draft_ids, worker_slot, embedding)
+    packed = pack(heads, chunks, group, after(me, tokens.table), (w_query, w_key, w_value, w_gate))
 
     def swaps(c):
         parts = [part if k == 0 else side(part, k) for k, part in enumerate(packed[c])]
@@ -479,58 +489,50 @@
     def fence(*values):
         return lax.optimization_barrier(values)
 
-    plane_a, plane_b = swaps(0), swaps(1)
-    one_b = up(plane_b)
-    first, finish, place_of = token_rows(
-        draft_ids, worker_slot, embedding, asked=(plane_a, plane_b), found=(one_b,)
-    )
-    plane_c = swaps(2)
-    one_a = up(plane_a)
-    first, one_a = fence(first, one_a)
+    def hand_back(parts):
+        return [part if k == 0 else side(part, k) for k, part in enumerate(parts)]
+
+    plane_b, plane_a = swaps(1), swaps(0)
+    one_b, three_b = up(plane_b), down(plane_b)
+    first, finish, place_of = tokens.fetch(asked=(plane_b,), found=(one_b,))
+    first, three_b, plane_a = fence(first, three_b, plane_a)
     half = finish(first)
 
-    three_a = down(after(plane_a, half))
+    two_b, one_a = up(after(one_b, half)), up(after(plane_a, half))
     other = lax.ppermute(half, "head", [(0, 1), (1, 0)])
     half_x = side(half, 2)
-    half, other, half_x, three_a, plane_b, plane_c = fence(
-        half, other, half_x, three_a, plane_b, plane_c
-    )
+    half, other, half_x, two_b = fence(half, other, half_x, two_b)
     other_x = side(other, 2)
-    two_a = up(after(one_a, other))
-    other_x, two_a, one_b, plane_b = fence(other_x, two_a, one_b, plane_b)
+    three_a = down(after(plane_a, other))
+    plane_c = swaps(2)
+    other_x, one_a, plane_c = fence(other_x, one_a, plane_c)
+    two_a = up(one_a)
     mine = norm(low, me, half, other, half_x, other_x)
     there = side(mine, 1)
-    three_b = down(plane_b)
-    two_b = up(one_b)
-    mine, there = fence(mine, there)
-
-    def hand_back(parts):
-        return [part if k == 0 else side(part, k) for k, part in enumerate(parts)]
-
-    def send(answer):
-        return lax.all_to_all(answer, "req", split_axis=0, concat_axis=0, tiled=True)
-
-    made_a = project(where_z, mine, there, (plane_a, one_a, two_a, three_a))
-    made_a, two_b, three_b, plane_c = fence(made_a, two_b, three_b, plane_c)
-    mix_a = hand_back(made_a)
+
+    (made_b,) = project(where_z, mine, there, (plane_b, one_b, two_b, three_b))
+    made_b, three_a = fence(made_b, three_a)
+    mix_b, two_a, plane_c = fence(hand_back(made_b), two_a, plane_c)
     one_c, three_c = up(plane_c), down(plane_c)
-    made_b = project(where_z, mine, there, (plane_b, one_b, two_b, three_b))
-    made_b, one_c = fence(made_b, one_c)
-    mix_b = hand_back(made_b)
+    made_0, made_1 = project(where_z, mine, there, (plane_a, one_a, two_a, three_a), 2)
+    mix_b, one_c, made_0, made_1 = fence(mix_b, one_c, made_0, made_1)
+    mix_0, mix_1 = hand_back(made_0), hand_back(made_1)
     two_c = up(one_c)
-    mix_a, three_c = fence(mix_a, three_c)
-    ahead, new_state = retain(0, 0, 0, 2, True, True, scalars, mix_a, old_state, None, None)
-    ahead, two_c, three_c, new_state = fence(ahead, two_c, three_c, new_state)
-    made_c = project(where_z, mine, there, (plane_c, one_c, two_c, three_c))
-    mix_a, made_c = fence(mix_a, made_c)
+    front, new_state = retain(2, 0, 0, 1, True, True, scalars, mix_b, old_state, None, None)
+    front, mix_0, three_c = fence(front, mix_0, three_c)
+    front = trade(front)
+    (made_c,) = project(where_z, mine, there, (plane_c, one_c, two_c, three_c))
     mix_c = hand_back(made_c)
-    ahead, new_state = retain(1, 1, 1, 2, True, True, scalars, mix_a, old_state, ahead, new_state)
-    front = send(ahead)
-    behind, new_state = retain(2, 0, 0, 2, True, True, scalars, mix_b, old_state, None, new_state)
-    (behind,) = retain(3, 0, 1, 2, True, False, scalars, mix_c, old_state, behind, None)
-    back = send(behind)
-    (new_state,) = retain(3, 0, 0, 1, False, True, scalars, mix_c, old_state, None, new_state)
-    return settle(place_of, [front, back]), new_state
+    mix_0, made_c = fence(mix_0, made_c)
+    (back,) = retain(0, 0, 0, 3, True, False, scalars, mix_0, old_state, None, None)
+    (back,) = retain(1, 0, 1, 3, True, False, scalars, mix_1, old_state, back, None)
+    back, mix_c = fence(back, mix_c)
+    (back,) = retain(3, 0, 2, 3, True, False, scalars, mix_c, old_state, back, None)
+    back, mix_0, mix_1, mix_c = fence(back, mix_0, mix_1, mix_c)
+    back = trade(back)
+    for j, mix in ((0, mix_0), (1, mix_1), (3, mix_c)):
+        (new_state,) = retain(j, 0, 0, 1, False, True, scalars, mix, old_state, None, new_state)
+    return settle(place_of, ((2,), (0, 1, 3)), [front, back]), new_state
 
 
 def plain_device(
@@ -541,7 +543,7 @@
         lax.all_gather(table, "req", axis=0, tiled=True)
         for table in (w_query, w_key, w_value, w_gate)
     ]
-    half, finish, place_of = token_rows(draft_ids, worker_slot, embedding)
+    half, finish, place_of = Asked(draft_ids, worker_slot, embedding).fetch()
     half = finish(half)
     tokens = lax.all_gather(half, "head", axis=1, tiled=True)
     normed = layer_norm(tokens.astype(jnp.float32)).astype(jnp.bfloat16)

time: 254 us -> 242 us (0.953)
  waiting for transfers between devices: 111 us -> 83.1 us
  blocking collectives: 0 us -> 11.5 us
  Pallas kernels: 58.5 us -> 66.2 us
  starting transfers between devices: 56.8 us -> 50.2 us
  local copies, waits for them, and re-layouts: 17.7 us -> 20.4 us
    all_to_all x4 -> x3, waiting for transfers between devices: 52.5 us -> 11.9 us  [trade(): return lax.all_to_all(table, 'req', split_axis=0, concat_axis=0, tiled=True)]
    ppermute x6, waiting for transfers between devices: 5.62 us -> 23.3 us  [up(): return lax.ppermute(piece, 'req', ring_perm(group, 1))]
    all_to_all x0 -> x1, blocking collectives: none -> 11.5 us  [trade(): return lax.all_to_all(table, 'req', split_axis=0, concat_axis=0, tiled=True)]
    ppermute x6, starting transfers between devices: 14.2 us -> 4.51 us  [up(): return lax.ppermute(piece, 'req', ring_perm(group, 1))]
    pallas_call x5 -> x7, Pallas kernels: 28 us -> 36 us  [retain(): pl.pallas_call(lambda *refs: retain_kernel(head, key_dim, value_dim, len(...]
    ppermute x21 -> x24, waiting for transfers between devices: 44.7 us -> 37.5 us  [side(): return lax.ppermute(rows, 'req', swap_perm(group, k))]
    ppermute x21 -> x24, starting transfers between devices: 17.2 us -> 24.1 us  [side(): return lax.ppermute(rows, 'req', swap_perm(group, k))]
    all_to_all x4 -> x3, starting transfers between devices: 22.5 us -> 16.5 us  [trade(): return lax.all_to_all(table, 'req', split_axis=0, concat_axis=0, tiled=True)]
  transfers between devices with their start and end apart: 35 -> 37, of which waited for: 15 -> 17; matrix products, arithmetic and copies ran while one was open for 7% -> 6% of each run, Pallas kernels for 14% -> 23%
where the time goes in v3:
time: 242 us
  waiting for transfers between devices  83.1 us (34%)
  Pallas kernels  66.2 us (27%)
  starting transfers between devices  50.2 us (21%)
  local copies, waits for them, and re-layouts  20.4 us (8%)
  blocking collectives  11.5 us (5%)
  other arithmetic  7.97 us (3%)
    ppermute x24, waiting for transfers between devices, side(): return lax.ppermute(rows, 'req', swap_perm(group, k))  37.5 us
    pallas_call x7, Pallas kernels, retain(): pl.pallas_call(lambda *refs: retain_kernel(head, key_dim, value_dim, len(...  36 us
    ppermute x24, starting transfers between devices, side(): return lax.ppermute(rows, 'req', swap_perm(group, k))  24.1 us
    ppermute x6, waiting for transfers between devices, up(): return lax.ppermute(piece, 'req', ring_perm(group, 1))  23.3 us
    pallas_call x3, Pallas kernels, project(): pl.pallas_call(lambda *refs: project_kernel(len(pieces), *refs), out_shap...  20.1 us
    all_to_all x3, starting transfers between devices, trade(): return lax.all_to_all(table, 'req', split_axis=0, concat_axis=0, tiled=True)  16.5 us
    all_to_all x3, waiting for transfers between devices, trade(): return lax.all_to_all(table, 'req', split_axis=0, concat_axis=0, tiled=True)  11.9 us
    all_to_all x1, blocking collectives, trade(): return lax.all_to_all(table, 'req', split_axis=0, concat_axis=0, tiled=True)  11.5 us
  transfers between devices with their start and end apart: 37, of which 17 were waited for; matrix products, arithmetic and copies ran while one was open for 6% of the time, Pallas kernels for 23%

profile of v3, /device:TPU:9, one launch (start us, length us, event | category | flops | bytes accessed | tf_op | source)
XLA Modules:
  0.0 241.5 jit_solution(9004293633163965703)
XLA Ops:
  5.5 2.6 %pack.1 = (bf16[128,768]{1,0:T(8,128)(2,1)}, bf16[128,768]{1,0:T(8,128)(2,1)}, bf16[128,768]{1,0:T(8,128)(2,1)}, bf16[128,768]{1,0:T(8,128)(2,1)}, bf16[128,384]...) custom-call(s32[1]{0:T(128)} %bitcast.10.refs_0_.member_ref.refs_3_,, ...), custom_call_target="tpu_custom_call" | custom-call | flops 1 | bytes 1 | tf_op jit(solution)/shard_map/pack/pallas_call | solution.py:171
  11.4 1.9 collective-permute-done.1
  13.4 2.2 collective-permute-done.2
  17.0 11.5 %all_to_all.56 = s32[16,1,128]{2,1,0:T(1,128)S(1)} all-to-all(s32[16,1,128]{2,1,0:T(1,128)S(1)} %bitcast.46), channel_id=1, replica_groups=mesh['req'=16,'head'=2] {'req'}, dimensions={0} | all-to-all | bytes 16384 | tf_op jit(solution)/shard_map/all_to_all | solution.py:141
  28.5 7.8 %gather_fusion.2 = bf16[512,1024]{1,0:T(8,128)(2,1)} fusion(bf16[4000,1024]{1,0:T(8,128)(2,1)} %param.14, s32[1024]{0:T(1024)S(1)} %pad_clamp_fusion.3), kind=kCustom, calls=%fused_computation.2 | custom fusion | bytes 2099200 | tf_op jit(solution)/shard_map/jit(_take)/gather | solution.py:115
  36.4 5.4 %all-to-all-start.3 = ((bf16[16,32,1024]{2,1,0:T(8,128)(2,1)}), bf16[16,32,1024]{2,1,0:T(8,128)(2,1)S(1)}, u32[]{:S(2)}, u32[]{:S(2)}) async-start(bf16[16,32,1024]{2,1,0:T(8,128)(2,1)} %bitcast.13), calls=%async_computation.3 | async-start | bytes 2097152 | tf_op jit(solution)/shard_map/all_to_all | solution.py:141
  46.2 9.6 %collective-permute-done.7 = bf16[128,768]{1,0:T(8,128)(2,1)S(1)} collective-permute-done((bf16[128,768]{1,0:T(8,128)(2,1)}, bf16[128,768]{1,0:T(8,128)(2,1)S(1)}, u32[]{:S(2)}, u32[]{:S(2)}) %collective-permute-start.7) | collective-permute-done | bytes 196640 | tf_op jit(solution)/shard_map/ppermute | solution.py:487
  55.8 6.5 %collective-permute-done.6 = bf16[128,768]{1,0:T(8,128)(2,1)S(1)} collective-permute-done((bf16[128,768]{1,0:T(8,128)(2,1)S(1)}, bf16[128,768]{1,0:T(8,128)(2,1)S(1)}, u32[]{:S(2)}, u32[]{:S(2)}) %collective-permute-start.6) | collective-permute-done | bytes 196640 | tf_op jit(solution)/shard_map/ppermute | solution.py:487
  64.7 8.4 %all-to-all-done.3 = bf16[16,32,1024]{2,1,0:T(8,128)(2,1)S(1)} async-done(((bf16[16,32,1024]{2,1,0:T(8,128)(2,1)}), bf16[16,32,1024]{2,1,0:T(8,128)(2,1)S(1)}, u32[]{:S(2)}, u32[]{:S(2)}) %all-to-all-start.3) | async-done | bytes 1048608 | tf_op jit(solution)/shard_map/all_to_all | solution.py:141
  81.7 6.3 %collective-permute-done.10.refs_5_ = bf16[512,384]{1,0:T(8,128)(2,1)S(1)} collective-permute-done((bf16[512,384]{1,0:T(8,128)(2,1)S(1)}, bf16[512,384]{1,0:T(8,128)(2,1)S(1)}, u32[]{:S(2)}, u32[]{:S(2)}) %collective-permute-start.10) | collective-permute-done | bytes 393248 | tf_op jit(solution)/shard_map/ppermute | solution.py:481
  91.1 3.6 %collective-permute-start.15 = (bf16[128,384]{1,0:T(8,128)(2,1)}, bf16[128,384]{1,0:T(8,128)(2,1)S(1)}, u32[]{:S(2)}, u32[]{:S(2)}) collective-permute-start(bf16[128,384]{1,0:T(8,128)(2,1)} %get-tuple-element.375), channel_id=1, source_target_pairs={{0,6},{2,4},{4,2},{6,0},{8,14},{10,12},{12,10},{14,8},{16,22},{18,... | collective-permute-start | bytes 294920 | tf_op jit(solution)/shard_map/ppermute | solution.py:487
  95.2 11.6 %collective-permute-done.15 = bf16[128,384]{1,0:T(8,128)(2,1)S(1)} collective-permute-done((bf16[128,384]{1,0:T(8,128)(2,1)}, bf16[128,384]{1,0:T(8,128)(2,1)S(1)}, u32[]{:S(2)}, u32[]{:S(2)}) %collective-permute-start.15) | collective-permute-done | bytes 98336 | tf_op jit(solution)/shard_map/ppermute | solution.py:487
  109.4 4.5 %norm.1.refs_1_ = bf16[2,256,2048]{2,1,0:T(8,128)(2,1)} custom-call(s32[1]{0:T(128)} %bitcast.12.low_ref, s32[1]{0:T(128)} %bitcast.10.refs_0_.member_ref.refs_3_, bf16[256,1024]{1,0:T(8,128)(2,1)S(1)} %get-tuple-element.367.own_ref, bf16[256,1024]{1,0:T(8,128)(2,1)} %copy-done.16, bf16[256,1024]{1,0:T(8,128)(2,1)} %copy-done.17, ...), custom_call_target="tpu_custom_call" | custom-call | flops 1 | bytes 1 | tf_op jit(solution)/shard_map/norm/pallas_call | solution.py:221
  115.5 2.2 collective-permute-start.17
  120.9 6.2 %project.3 = (bf16[256,384]{1,0:T(8,128)(2,1)}, bf16[256,384]{1,0:T(8,128)(2,1)}, bf16[256,384]{1,0:T(8,128)(2,1)}, bf16[256,384]{1,0:T(8,128)(2,1)}) custom-call(s32[1]{0:T(128)} %bitcast.11.refs_0_, bf16[2,256,2048]{2,1,0:T(8,128)(2,1)} %norm.1.refs_1_, bf16[2,256,2048]{2,1,0:T(8,128)(2,1)} %copy-done, bf16[512,384]{1,0:T(8,128)(2,1)} %copy-done.15, ...), custom_call_target="tpu_custom_call" | custom-call | flops 1 | bytes 1 | tf_op jit(solution)/shard_map/project/pallas_call | solution.py:281
  127.1 8.9 %collective-permute-done.17.refs_6_ = bf16[512,768]{1,0:T(8,128)(2,1)} collective-permute-done((bf16[512,768]{1,0:T(8,128)(2,1)S(1)}, bf16[512,768]{1,0:T(8,128)(2,1)}, u32[]{:S(2)}, u32[]{:S(2)}) %collective-permute-start.17) | collective-permute-done | bytes 786464 | tf_op jit(solution)/shard_map/ppermute | solution.py:484
  138.2 16.5 %collective-permute-done.21.refs_5_ = bf16[512,768]{1,0:T(8,128)(2,1)} collective-permute-done((bf16[512,768]{1,0:T(8,128)(2,1)}, bf16[512,768]{1,0:T(8,128)(2,1)}, u32[]{:S(2)}, u32[]{:S(2)}) %collective-permute-start.21) | collective-permute-done | bytes 786464 | tf_op jit(solution)/shard_map/ppermute | solution.py:481
  156.3 7.9 %project.4 = (bf16[256,384]{1,0:T(8,128)(2,1)}, bf16[256,384]{1,0:T(8,128)(2,1)}, bf16[256,384]{1,0:T(8,128)(2,1)}, bf16[256,384]{1,0:T(8,128)(2,1)}, bf16[256,3...) custom-call(s32[1]{0:T(128)} %bitcast.11.refs_0_, ...), custom_call_target="tpu_custom_call" | custom-call | flops 1 | bytes 1 | tf_op jit(solution)/shard_map/project/pallas_call | solution.py:281
  164.7 3.1 %collective-permute-start.23 = (bf16[256,384]{1,0:T(8,128)(2,1)}, bf16[256,384]{1,0:T(8,128)(2,1)S(1)}, u32[]{:S(2)}, u32[]{:S(2)}) collective-permute-start(bf16[256,384]{1,0:T(8,128)(2,1)} %get-tuple-element.411), channel_id=1, source_target_pairs={{0,2},{2,0},{4,6},{6,4},{8,10},{10,8},{12,14},{14,12},{16,18},{18,... | collective-permute-start | bytes 589832 | tf_op jit(solution)/shard_map/ppermute | solution.py:487
  170.0 6.1 %retain.7 = (bf16[16,16,512]{2,1,0:T(8,128)(2,1)}, bf16[16,4,256,512]{3,2,1,0:T(8,128)(2,1)}) custom-call(s32[16]{0:T(128)} %copy-done.32, s32[16]{0:T(128)} %refs_1_.15, f32[4]{0:T(128)} %negate_log-plus-one_fusion.refs_2_, s32[1]{0:T(128)} %bitcast.10.refs_0_.member_ref.refs_3_, bf16[256,384]{1,0:T(8,128)(2,1)} %get-tuple-element.405.refs_4_, ...), custom_call_target="tpu_custom_call" | custom-call | flops 1 | bytes 1 | tf_op jit(solution)/shard_map/retain/pallas_call | solution.py:381
  176.1 2.9 %collective-permute-done.25.refs_7_ = bf16[256,384]{1,0:T(8,128)(2,1)S(1)} collective-permute-done((bf16[256,384]{1,0:T(8,128)(2,1)}, bf16[256,384]{1,0:T(8,128)(2,1)S(1)}, u32[]{:S(2)}, u32[]{:S(2)}) %collective-permute-start.25) | collective-permute-done | bytes 196640 | tf_op jit(solution)/shard_map/ppermute | solution.py:487
  179.1 5.3 %all-to-all-start.4 = ((bf16[16,16,512]{2,1,0:T(8,128)(2,1)}), bf16[16,16,512]{2,1,0:T(8,128)(2,1)S(1)}, u32[]{:S(2)}, u32[]{:S(2)}) async-start(bf16[16,16,512]{2,1,0:T(8,128)(2,1)} %get-tuple-element.414), calls=%async_computation.4 | async-start | bytes 524288 | tf_op jit(solution)/shard_map/all_to_all | solution.py:141
  187.4 6.1 %project.5 = (bf16[256,384]{1,0:T(8,128)(2,1)}, bf16[256,384]{1,0:T(8,128)(2,1)}, bf16[256,384]{1,0:T(8,128)(2,1)}, bf16[256,384]{1,0:T(8,128)(2,1)}) custom-call(s32[1]{0:T(128)} %bitcast.11.refs_0_, bf16[2,256,2048]{2,1,0:T(8,128)(2,1)} %norm.1.refs_1_, bf16[2,256,2048]{2,1,0:T(8,128)(2,1)} %copy-done, bf16[512,384]{1,0:T(8,128)(2,1)} %pad_maximum_fusion.1.refs_3_, ...), custom_call_target="tpu_custom_call" | custom-call | flops 1 | bytes 1 | tf_op jit(solution)/shard_map/project/pallas_call | solution.py:281
  195.6 4.6 %retain.8.refs_9_ = bf16[16,16,1536]{2,1,0:T(8,128)(2,1)} custom-call(s32[16]{0:T(128)} %copy-done.32, s32[16]{0:T(128)} %refs_1_.15, f32[4]{0:T(128)} %negate_log-plus-one_fusion.refs_2_, s32[1]{0:T(128)} %bitcast.10.refs_0_.member_ref.refs_3_, bf16[256,384]{1,0:T(8,128)(2,1)} %get-tuple-element.447.refs_4_, bf16[256,384]{1,0:T(8,128)(2,1)} %copy-done.5, ...), custom_call_target="tpu_custom_call" | custom-call | flops 1 | bytes 1 | tf_op jit(solution)/shard_map/retain/pallas_call | solution.py:381
  201.6 4.6 %retain.9.refs_9_ = bf16[16,16,1536]{2,1,0:T(8,128)(2,1)} custom-call(s32[16]{0:T(128)} %copy-done.32, s32[16]{0:T(128)} %refs_1_.15, f32[4]{0:T(128)} %negate_log-plus-one_fusion.refs_2_, s32[1]{0:T(128)} %bitcast.10.refs_0_.member_ref.refs_3_, bf16[256,384]{1,0:T(8,128)(2,1)} %get-tuple-element.443.refs_4_, ...), custom_call_target="tpu_custom_call", output_to_operand_aliasing={{}: (9, {})} | custom-call | flops 1 | bytes 1 | tf_op jit(solution)/shard_map/retain/pallas_call | solution.py:381
  207.7 4.6 %retain.10 = bf16[16,16,1536]{2,1,0:T(8,128)(2,1)} custom-call(s32[16]{0:T(128)} %copy-done.32, s32[16]{0:T(128)} %refs_1_.15, f32[4]{0:T(128)} %negate_log-plus-one_fusion.refs_2_, s32[1]{0:T(128)} %bitcast.10.refs_0_.member_ref.refs_3_, bf16[256,384]{1,0:T(8,128)(2,1)} %get-tuple-element.439.refs_4_, ...), custom_call_target="tpu_custom_call", output_to_operand_aliasing={{}: (9, {})} | custom-call | flops 1 | bytes 1 | tf_op jit(solution)/shard_map/retain/pallas_call | solution.py:381
  212.3 5.8 %all-to-all-start.5 = ((bf16[16,16,1536]{2,1,0:T(8,128)(2,1)}), bf16[16,16,1536]{2,1,0:T(8,128)(2,1)S(1)}, u32[]{:S(2)}, u32[]{:S(2)}) async-start(bf16[16,16,1536]{2,1,0:T(8,128)(2,1)} %retain.10), calls=%async_computation.5 | async-start | bytes 1572864 | tf_op jit(solution)/shard_map/all_to_all | solution.py:141
  218.2 5.4 %retain.11.refs_9_ = bf16[16,4,256,512]{3,2,1,0:T(8,128)(2,1)} custom-call(s32[16]{0:T(128)} %copy-done.32, s32[16]{0:T(128)} %refs_1_.15, f32[4]{0:T(128)} %negate_log-plus-one_fusion.refs_2_, s32[1]{0:T(128)} %bitcast.10.refs_0_.member_ref.refs_3_, bf16[256,384]{1,0:T(8,128)(2,1)} %get-tuple-element.447.refs_4_, ...), custom_call_target="tpu_custom_call", output_to_operand_aliasing={{}: (9, {})} | custom-call | flops 1 | bytes 1 | tf_op jit(solution)/shard_map/retain/pallas_call | solution.py:381
  223.5 5.4 %retain.12.refs_9_ = bf16[16,4,256,512]{3,2,1,0:T(8,128)(2,1)} custom-call(s32[16]{0:T(128)} %copy-done.32, s32[16]{0:T(128)} %refs_1_.15, f32[4]{0:T(128)} %negate_log-plus-one_fusion.refs_2_, s32[1]{0:T(128)} %bitcast.10.refs_0_.member_ref.refs_3_, bf16[256,384]{1,0:T(8,128)(2,1)} %get-tuple-element.443.refs_4_, ...), custom_call_target="tpu_custom_call", output_to_operand_aliasing={{}: (9, {})} | custom-call | flops 1 | bytes 1 | tf_op jit(solution)/shard_map/retain/pallas_call | solution.py:381
  228.9 5.4 %retain.13 = bf16[16,4,256,512]{3,2,1,0:T(8,128)(2,1)} custom-call(s32[16]{0:T(128)} %copy-done.32, s32[16]{0:T(128)} %refs_1_.15, f32[4]{0:T(128)} %negate_log-plus-one_fusion.refs_2_, s32[1]{0:T(128)} %bitcast.10.refs_0_.member_ref.refs_3_, bf16[256,384]{1,0:T(8,128)(2,1)} %get-tuple-element.439.refs_4_, ...), custom_call_target="tpu_custom_call", output_to_operand_aliasing={{}: (9, {})} | custom-call | flops 1 | bytes 1 | tf_op jit(solution)/shard_map/retain/pallas_call | solution.py:381
  234.2 3.5 %all-to-all-done.5.refs_2_ = bf16[16,16,1536]{2,1,0:T(8,128)(2,1)S(1)} async-done(((bf16[16,16,1536]{2,1,0:T(8,128)(2,1)}), bf16[16,16,1536]{2,1,0:T(8,128)(2,1)S(1)}, u32[]{:S(2)}, u32[]{:S(2)}) %all-to-all-start.5) | async-done | bytes 786464 | tf_op jit(solution)/shard_map/all_to_all | solution.py:141
  238.6 2.9 %settle.1 = bf16[16,16,2048]{2,1,0:T(8,128)(2,1)} custom-call(s32[16]{0:T(128)} %get-tuple-element.453.refs_0_, bf16[16,16,512]{2,1,0:T(8,128)(2,1)} %copy-done.4, bf16[16,16,1536]{2,1,0:T(8,128)(2,1)} %copy-done.1), custom_call_target="tpu_custom_call" | custom-call | flops 1 | bytes 1 | tf_op jit(solution)/shard_map/settle/pallas_call | solution.py:417
  (169 shorter events, 50.5 us)
Async XLA Ops:
  15.6 20.8 %collective-permute-start.3 = (bf16[512,384]{1,0:T(8,128)(2,1)S(1)}, bf16[512,384]{1,0:T(8,128)(2,1)S(1)}, u32[]{:S(2)}, u32[]{:S(2)}) collective-permute-start(bf16[512,384]{1,0:T(8,128)(2,1)S(1)} %constant_dynamic-update-slice_fusion.refs_3_), channel_id=1, source_target_pairs={{0,8},{2,10},{4,12},{6,14},{8,16},{10,18},{12,20},{14,22},{16,24},... | collective-permute-start | bytes 1179656 | tf_op jit(solution)/shard_map/ppermute | solution.py:481
  36.4 36.7 %all-to-all-start.3 = ((bf16[16,32,1024]{2,1,0:T(8,128)(2,1)}), bf16[16,32,1024]{2,1,0:T(8,128)(2,1)S(1)}, u32[]{:S(2)}, u32[]{:S(2)}) async-start(bf16[16,32,1024]{2,1,0:T(8,128)(2,1)} %bitcast.13), calls=%async_computation.3 | async-start | bytes 2097152 | tf_op jit(solution)/shard_map/all_to_all | solution.py:141
  41.9 13.9 %collective-permute-start.7 = (bf16[128,768]{1,0:T(8,128)(2,1)}, bf16[128,768]{1,0:T(8,128)(2,1)S(1)}, u32[]{:S(2)}, u32[]{:S(2)}) collective-permute-start(bf16[128,768]{1,0:T(8,128)(2,1)} %get-tuple-element.363), channel_id=1, source_target_pairs={{0,6},{2,4},{4,2},{6,0},{8,14},{10,12},{12,10},{14,8},{16,22},{18,... | collective-permute-start | bytes 589832 | tf_op jit(solution)/shard_map/ppermute | solution.py:487
  43.3 19.0 %collective-permute-start.6 = (bf16[128,768]{1,0:T(8,128)(2,1)S(1)}, bf16[128,768]{1,0:T(8,128)(2,1)S(1)}, u32[]{:S(2)}, u32[]{:S(2)}) collective-permute-start(bf16[128,768]{1,0:T(8,128)(2,1)S(1)} %copy-done.38), channel_id=1, source_target_pairs={{0,4},{2,6},{4,0},{6,2},{8,12},{10,14},{12,8},{14,10},{16,20},{18,... | collective-permute-start | bytes 589832 | tf_op jit(solution)/shard_map/ppermute | solution.py:487
  43.6 18.7 %collective-permute-start.5 = (bf16[128,768]{1,0:T(8,128)(2,1)S(1)}, bf16[128,768]{1,0:T(8,128)(2,1)S(1)}, u32[]{:S(2)}, u32[]{:S(2)}) collective-permute-start(bf16[128,768]{1,0:T(8,128)(2,1)S(1)} %copy-done.37), channel_id=1, source_target_pairs={{0,2},{2,0},{4,6},{6,4},{8,10},{10,8},{12,14},{14,12},{16,18},{18,... | collective-permute-start | bytes 589832 | tf_op jit(solution)/shard_map/ppermute | solution.py:487
  44.2 30.8 %collective-permute-start.4 = (bf16[512,384]{1,0:T(8,128)(2,1)S(1)}, bf16[512,384]{1,0:T(8,128)(2,1)S(1)}, u32[]{:S(2)}, u32[]{:S(2)}) collective-permute-start(bf16[512,384]{1,0:T(8,128)(2,1)S(1)} %constant_dynamic-update-slice_fusion.refs_3_), channel_id=1, source_target_pairs={{0,24},{2,26},{4,28},{6,30},{8,0},{10,2},{12,4},{14,6},{16,8},{18,... | collective-permute-start | bytes 1179656 | tf_op jit(solution)/shard_map/ppermute | solution.py:484
  76.3 12.6 %collective-permute-start.8 = (bf16[256,1024]{1,0:T(8,128)(2,1)S(1)}, bf16[256,1024]{1,0:T(8,128)(2,1)S(1)}, u32[]{:S(2)}, u32[]{:S(2)}) collective-permute-start(bf16[256,1024]{1,0:T(8,128)(2,1)S(1)} %get-tuple-element.367.own_ref), channel_id=1, source_target_pairs={{0,1},{1,0},{2,3},{3,2},{4,5},{5,4},{6,7},{7,6},{8,9},{9,8},{10,11... | collective-permute-start | bytes 1572872 | tf_op jit(solution)/shard_map/ppermute | solution.py:502
  77.6 12.3 %collective-permute-start.9 = (bf16[256,1024]{1,0:T(8,128)(2,1)S(1)}, bf16[256,1024]{1,0:T(8,128)(2,1)S(1)}, u32[]{:S(2)}, u32[]{:S(2)}) collective-permute-start(bf16[256,1024]{1,0:T(8,128)(2,1)S(1)} %get-tuple-element.367.own_ref), channel_id=1, source_target_pairs={{0,4},{2,6},{4,0},{6,2},{8,12},{10,14},{12,8},{14,10},{16,20},{18,... | collective-permute-start | bytes 1572872 | tf_op jit(solution)/shard_map/ppermute | solution.py:487
  78.9 9.2 %collective-permute-start.10 = (bf16[512,384]{1,0:T(8,128)(2,1)S(1)}, bf16[512,384]{1,0:T(8,128)(2,1)S(1)}, u32[]{:S(2)}, u32[]{:S(2)}) collective-permute-start(bf16[512,384]{1,0:T(8,128)(2,1)S(1)} %collective-permute-done.3.refs_4_), channel_id=1, source_target_pairs={{0,8},{2,10},{4,12},{6,14},{8,16},{10,18},{12,20},{14,22},{16,24},... | collective-permute-start | bytes 1179656 | tf_op jit(solution)/shard_map/ppermute | solution.py:481
  80.1 28.5 %collective-permute-start.12 = (bf16[512,768]{1,0:T(8,128)(2,1)S(1)}, bf16[512,768]{1,0:T(8,128)(2,1)S(1)}, u32[]{:S(2)}, u32[]{:S(2)}) collective-permute-start(bf16[512,768]{1,0:T(8,128)(2,1)S(1)} %pad_maximum_fusion.refs_3_), channel_id=1, source_target_pairs={{0,8},{2,10},{4,12},{6,14},{8,16},{10,18},{12,20},{14,22},{16,24},... | collective-permute-start | bytes 2359304 | tf_op jit(solution)/shard_map/ppermute | solution.py:481
  89.9 18.6 %collective-permute-start.11 = (bf16[256,1024]{1,0:T(8,128)(2,1)S(1)}, bf16[256,1024]{1,0:T(8,128)(2,1)}, u32[]{:S(2)}, u32[]{:S(2)}) collective-permute-start(bf16[256,1024]{1,0:T(8,128)(2,1)S(1)} %collective-permute-done.8.own_far_ref), channel_id=1, source_target_pairs={{0,4},{2,6},{4,0},{6,2},{8,12},{10,14},{12,8},{14,10},{16,20},{18,... | collective-permute-start | bytes 1572872 | tf_op jit(solution)/shard_map/ppermute | solution.py:487
  91.1 15.7 %collective-permute-start.15 = (bf16[128,384]{1,0:T(8,128)(2,1)}, bf16[128,384]{1,0:T(8,128)(2,1)S(1)}, u32[]{:S(2)}, u32[]{:S(2)}) collective-permute-start(bf16[128,384]{1,0:T(8,128)(2,1)} %get-tuple-element.375), channel_id=1, source_target_pairs={{0,6},{2,4},{4,2},{6,0},{8,14},{10,12},{12,10},{14,8},{16,22},{18,... | collective-permute-start | bytes 294920 | tf_op jit(solution)/shard_map/ppermute | solution.py:487
  94.7 12.1 %collective-permute-start.14 = (bf16[128,384]{1,0:T(8,128)(2,1)}, bf16[128,384]{1,0:T(8,128)(2,1)S(1)}, u32[]{:S(2)}, u32[]{:S(2)}) collective-permute-start(bf16[128,384]{1,0:T(8,128)(2,1)} %get-tuple-element.374), channel_id=1, source_target_pairs={{0,4},{2,6},{4,0},{6,2},{8,12},{10,14},{12,8},{14,10},{16,20},{18,... | collective-permute-start | bytes 294920 | tf_op jit(solution)/shard_map/ppermute | solution.py:487
  95.2 11.6 %collective-permute-start.13 = (bf16[128,384]{1,0:T(8,128)(2,1)}, bf16[128,384]{1,0:T(8,128)(2,1)S(1)}, u32[]{:S(2)}, u32[]{:S(2)}) collective-permute-start(bf16[128,384]{1,0:T(8,128)(2,1)} %get-tuple-element.373), channel_id=1, source_target_pairs={{0,2},{2,0},{4,6},{6,4},{8,10},{10,8},{12,14},{14,12},{16,18},{18,... | collective-permute-start | bytes 294920 | tf_op jit(solution)/shard_map/ppermute | solution.py:487
  115.5 20.4 %collective-permute-start.17 = (bf16[512,768]{1,0:T(8,128)(2,1)S(1)}, bf16[512,768]{1,0:T(8,128)(2,1)}, u32[]{:S(2)}, u32[]{:S(2)}) collective-permute-start(bf16[512,768]{1,0:T(8,128)(2,1)S(1)} %pad_maximum_fusion.refs_3_), channel_id=1, source_target_pairs={{0,24},{2,26},{4,28},{6,30},{8,0},{10,2},{12,4},{14,6},{16,8},{18,... | collective-permute-start | bytes 2359304 | tf_op jit(solution)/shard_map/ppermute | solution.py:484
  117.8 37.0 %collective-permute-start.21 = (bf16[512,768]{1,0:T(8,128)(2,1)}, bf16[512,768]{1,0:T(8,128)(2,1)}, u32[]{:S(2)}, u32[]{:S(2)}) collective-permute-start(bf16[512,768]{1,0:T(8,128)(2,1)} %copy-done.14), channel_id=1, source_target_pairs={{0,8},{2,10},{4,12},{6,14},{8,16},{10,18},{12,20},{14,22},{16,24},... | collective-permute-start | bytes 2359304 | tf_op jit(solution)/shard_map/ppermute | solution.py:481
  136.0 18.8 %collective-permute-start.18 = (bf16[256,384]{1,0:T(8,128)(2,1)}, bf16[256,384]{1,0:T(8,128)(2,1)S(1)}, u32[]{:S(2)}, u32[]{:S(2)}) collective-permute-start(bf16[256,384]{1,0:T(8,128)(2,1)} %get-tuple-element.385), channel_id=1, source_target_pairs={{0,2},{2,0},{4,6},{6,4},{8,10},{10,8},{12,14},{14,12},{16,18},{18,... | collective-permute-start | bytes 589832 | tf_op jit(solution)/shard_map/ppermute | solution.py:487
  136.6 18.2 %collective-permute-start.19 = (bf16[256,384]{1,0:T(8,128)(2,1)}, bf16[256,384]{1,0:T(8,128)(2,1)S(1)}, u32[]{:S(2)}, u32[]{:S(2)}) collective-permute-start(bf16[256,384]{1,0:T(8,128)(2,1)} %get-tuple-element.386), channel_id=1, source_target_pairs={{0,4},{2,6},{4,0},{6,2},{8,12},{10,14},{12,8},{14,10},{16,20},{18,... | collective-permute-start | bytes 589832 | tf_op jit(solution)/shard_map/ppermute | solution.py:487
  136.9 17.9 %collective-permute-start.20 = (bf16[256,384]{1,0:T(8,128)(2,1)}, bf16[256,384]{1,0:T(8,128)(2,1)S(1)}, u32[]{:S(2)}, u32[]{:S(2)}) collective-permute-start(bf16[256,384]{1,0:T(8,128)(2,1)} %get-tuple-element.387), channel_id=1, source_target_pairs={{0,6},{2,4},{4,2},{6,0},{8,14},{10,12},{12,10},{14,8},{16,22},{18,... | collective-permute-start | bytes 589832 | tf_op jit(solution)/shard_map/ppermute | solution.py:487
  154.8 9.8 %collective-permute-start.22 = (bf16[512,384]{1,0:T(8,128)(2,1)S(1)}, bf16[512,384]{1,0:T(8,128)(2,1)S(1)}, u32[]{:S(2)}, u32[]{:S(2)}) collective-permute-start(bf16[512,384]{1,0:T(8,128)(2,1)S(1)} %copy-done.3), channel_id=1, source_target_pairs={{0,8},{2,10},{4,12},{6,14},{8,16},{10,18},{12,20},{14,22},{16,24},... | collective-permute-start | bytes 1179656 | tf_op jit(solution)/shard_map/ppermute | solution.py:481
  154.9 21.2 %collective-permute-start.26 = (bf16[512,384]{1,0:T(8,128)(2,1)S(1)}, bf16[512,384]{1,0:T(8,128)(2,1)S(1)}, u32[]{:S(2)}, u32[]{:S(2)}) collective-permute-start(bf16[512,384]{1,0:T(8,128)(2,1)S(1)} %copy-done.3), channel_id=1, source_target_pairs={{0,24},{2,26},{4,28},{6,30},{8,0},{10,2},{12,4},{14,6},{16,8},{18,... | collective-permute-start | bytes 1179656 | tf_op jit(solution)/shard_map/ppermute | solution.py:484
  164.7 11.4 %collective-permute-start.23 = (bf16[256,384]{1,0:T(8,128)(2,1)}, bf16[256,384]{1,0:T(8,128)(2,1)S(1)}, u32[]{:S(2)}, u32[]{:S(2)}) collective-permute-start(bf16[256,384]{1,0:T(8,128)(2,1)} %get-tuple-element.411), channel_id=1, source_target_pairs={{0,2},{2,0},{4,6},{6,4},{8,10},{10,8},{12,14},{14,12},{16,18},{18,... | collective-permute-start | bytes 589832 | tf_op jit(solution)/shard_map/ppermute | solution.py:487
  168.9 10.2 %collective-permute-start.25 = (bf16[256,384]{1,0:T(8,128)(2,1)}, bf16[256,384]{1,0:T(8,128)(2,1)S(1)}, u32[]{:S(2)}, u32[]{:S(2)}) collective-permute-start(bf16[256,384]{1,0:T(8,128)(2,1)} %get-tuple-element.413), channel_id=1, source_target_pairs={{0,6},{2,4},{4,2},{6,0},{8,14},{10,12},{12,10},{14,8},{16,22},{18,... | collective-permute-start | bytes 589832 | tf_op jit(solution)/shard_map/ppermute | solution.py:487
  169.4 17.2 %collective-permute-start.30 = (bf16[512,384]{1,0:T(8,128)(2,1)S(1)}, bf16[512,384]{1,0:T(8,128)(2,1)S(1)}, u32[]{:S(2)}, u32[]{:S(2)}) collective-permute-start(bf16[512,384]{1,0:T(8,128)(2,1)S(1)} %collective-permute-done.22.refs_4_), channel_id=1, source_target_pairs={{0,8},{2,10},{4,12},{6,14},{8,16},{10,18},{12,20},{14,22},{16,24},... | collective-permute-start | bytes 1179656 | tf_op jit(solution)/shard_map/ppermute | solution.py:481
  179.1 33.2 %all-to-all-start.4 = ((bf16[16,16,512]{2,1,0:T(8,128)(2,1)}), bf16[16,16,512]{2,1,0:T(8,128)(2,1)S(1)}, u32[]{:S(2)}, u32[]{:S(2)}) async-start(bf16[16,16,512]{2,1,0:T(8,128)(2,1)} %get-tuple-element.414), calls=%async_computation.4 | async-start | bytes 524288 | tf_op jit(solution)/shard_map/all_to_all | solution.py:141
  184.4 10.4 %collective-permute-start.27 = (bf16[256,384]{1,0:T(8,128)(2,1)S(1)}, bf16[256,384]{1,0:T(8,128)(2,1)S(1)}, u32[]{:S(2)}, u32[]{:S(2)}) collective-permute-start(bf16[256,384]{1,0:T(8,128)(2,1)S(1)} %copy-done.39), channel_id=1, source_target_pairs={{0,2},{2,0},{4,6},{6,4},{8,10},{10,8},{12,14},{14,12},{16,18},{18,... | collective-permute-start | bytes 589832 | tf_op jit(solution)/shard_map/ppermute | solution.py:487
  184.8 15.5 %collective-permute-start.28 = (bf16[256,384]{1,0:T(8,128)(2,1)S(1)}, bf16[256,384]{1,0:T(8,128)(2,1)S(1)}, u32[]{:S(2)}, u32[]{:S(2)}) collective-permute-start(bf16[256,384]{1,0:T(8,128)(2,1)S(1)} %copy-done.36), channel_id=1, source_target_pairs={{0,4},{2,6},{4,0},{6,2},{8,12},{10,14},{12,8},{14,10},{16,20},{18,... | collective-permute-start | bytes 589832 | tf_op jit(solution)/shard_map/ppermute | solution.py:487
  186.0 14.3 %collective-permute-start.29 = (bf16[256,384]{1,0:T(8,128)(2,1)S(1)}, bf16[256,384]{1,0:T(8,128)(2,1)S(1)}, u32[]{:S(2)}, u32[]{:S(2)}) collective-permute-start(bf16[256,384]{1,0:T(8,128)(2,1)S(1)} %copy-done.35), channel_id=1, source_target_pairs={{0,6},{2,4},{4,2},{6,0},{8,14},{10,12},{12,10},{14,8},{16,22},{18,... | collective-permute-start | bytes 589832 | tf_op jit(solution)/shard_map/ppermute | solution.py:487
  193.4 12.8 %collective-permute-start.31 = (bf16[256,384]{1,0:T(8,128)(2,1)}, bf16[256,384]{1,0:T(8,128)(2,1)S(1)}, u32[]{:S(2)}, u32[]{:S(2)}) collective-permute-start(bf16[256,384]{1,0:T(8,128)(2,1)} %get-tuple-element.426), channel_id=1, source_target_pairs={{0,2},{2,0},{4,6},{6,4},{8,10},{10,8},{12,14},{14,12},{16,18},{18,... | collective-permute-start | bytes 589832 | tf_op jit(solution)/shard_map/ppermute | solution.py:487
  193.6 12.7 %collective-permute-start.32 = (bf16[256,384]{1,0:T(8,128)(2,1)}, bf16[256,384]{1,0:T(8,128)(2,1)S(1)}, u32[]{:S(2)}, u32[]{:S(2)}) collective-permute-start(bf16[256,384]{1,0:T(8,128)(2,1)} %get-tuple-element.427), channel_id=1, source_target_pairs={{0,4},{2,6},{4,0},{6,2},{8,12},{10,14},{12,8},{14,10},{16,20},{18,... | collective-permute-start | bytes 589832 | tf_op jit(solution)/shard_map/ppermute | solution.py:487
  194.8 11.7 %collective-permute-start.33 = (bf16[256,384]{1,0:T(8,128)(2,1)}, bf16[256,384]{1,0:T(8,128)(2,1)S(1)}, u32[]{:S(2)}, u32[]{:S(2)}) collective-permute-start(bf16[256,384]{1,0:T(8,128)(2,1)} %get-tuple-element.428), channel_id=1, source_target_pairs={{0,6},{2,4},{4,2},{6,0},{8,14},{10,12},{12,10},{14,8},{16,22},{18,... | collective-permute-start | bytes 589832 | tf_op jit(solution)/shard_map/ppermute | solution.py:487
  212.3 25.4 %all-to-all-start.5 = ((bf16[16,16,1536]{2,1,0:T(8,128)(2,1)}), bf16[16,16,1536]{2,1,0:T(8,128)(2,1)S(1)}, u32[]{:S(2)}, u32[]{:S(2)}) async-start(bf16[16,16,1536]{2,1,0:T(8,128)(2,1)} %retain.10), calls=%async_computation.5 | async-start | bytes 1572864 | tf_op jit(solution)/shard_map/all_to_all | solution.py:141
  (44 other events, 479.9 us)

commit v4 on v3

--- a/solution.py
+++ b/solution.py
@@ -264,30 +264,20 @@
                     half * rows : (half + 1) * rows, spot * share : (spot + 1) * share
                 ]
 
-    @pl.when(pl.program_id(0) == 0)
-    def _():
-        keep(product(mine_ref, False), 0)
-
-    @pl.when(pl.program_id(0) == 1)
-    def _():
-        keep(product(there_ref, True), 1)
+    keep(product(mine_ref, False), 0)
+    keep(product(there_ref, True), 1)
 
 
 def project(zpos, mine, there, pieces, count=1):
     _, rows, size = mine.shape
     width = pieces[0].shape[1]
-    whole = pl.BlockSpec(mine.shape, lambda i, z: (0, 0, 0))
     shape = (rows, width // count)
+    held = pl.BlockSpec(memory_space=pltpu.VMEM)
     outs = pl.pallas_call(
         lambda *refs: project_kernel(len(pieces), *refs),
         out_shape=[jax.ShapeDtypeStruct(shape, jnp.bfloat16)] * (4 * count),
-        grid_spec=pltpu.PrefetchScalarGridSpec(
-            num_scalar_prefetch=1,
-            grid=(2,),
-            in_specs=[whole, whole]
-            + [pl.BlockSpec(piece.shape, lambda i, z: (0, 0)) for piece in pieces],
-            out_specs=[pl.BlockSpec(shape, lambda i, z: (0, 0))] * (4 * count),
-        ),
+        in_specs=[pl.BlockSpec(memory_space=pltpu.SMEM)] + [held] * (2 + len(pieces)),
+        out_specs=[held] * (4 * count),
         cost_estimate=BRIEF,
         name="project",
     )(zpos, mine, there, *pieces)
@@ -494,44 +484,44 @@
 
     plane_b, plane_a = swaps(1), swaps(0)
     one_b, three_b = up(plane_b), down(plane_b)
-    first, finish, place_of = tokens.fetch(asked=(plane_b,), found=(one_b,))
-    first, three_b, plane_a = fence(first, three_b, plane_a)
+    first, finish, place_of = tokens.fetch(asked=(plane_b,), found=(one_b, three_b))
+    first, plane_a = fence(first, plane_a)
     half = finish(first)
 
     two_b, one_a = up(after(one_b, half)), up(after(plane_a, half))
+    three_a = down(after(plane_a, half))
     other = lax.ppermute(half, "head", [(0, 1), (1, 0)])
     half_x = side(half, 2)
     half, other, half_x, two_b = fence(half, other, half_x, two_b)
     other_x = side(other, 2)
-    three_a = down(after(plane_a, other))
     plane_c = swaps(2)
     other_x, one_a, plane_c = fence(other_x, one_a, plane_c)
+    mine = norm(low, me, half, other, half_x, other_x)
+    mine, three_a, one_a = fence(mine, three_a, one_a)
     two_a = up(one_a)
-    mine = norm(low, me, half, other, half_x, other_x)
     there = side(mine, 1)
 
     (made_b,) = project(where_z, mine, there, (plane_b, one_b, two_b, three_b))
-    made_b, three_a = fence(made_b, three_a)
     mix_b, two_a, plane_c = fence(hand_back(made_b), two_a, plane_c)
     one_c, three_c = up(plane_c), down(plane_c)
-    made_0, made_1 = project(where_z, mine, there, (plane_a, one_a, two_a, three_a), 2)
-    mix_b, one_c, made_0, made_1 = fence(mix_b, one_c, made_0, made_1)
-    mix_0, mix_1 = hand_back(made_0), hand_back(made_1)
+    (made_a,) = project(where_z, mine, there, (plane_a, one_a, two_a, three_a))
+    mix_b, one_c, made_a = fence(mix_b, one_c, made_a)
+    mix_a = hand_back(made_a)
     two_c = up(one_c)
     front, new_state = retain(2, 0, 0, 1, True, True, scalars, mix_b, old_state, None, None)
-    front, mix_0, three_c = fence(front, mix_0, three_c)
     front = trade(front)
+    new_state, mix_a[2], three_c, two_c = fence(new_state, mix_a[2], three_c, two_c)
     (made_c,) = project(where_z, mine, there, (plane_c, one_c, two_c, three_c))
+    mix_a, made_c = fence(mix_a, made_c)
     mix_c = hand_back(made_c)
-    mix_0, made_c = fence(mix_0, made_c)
-    (back,) = retain(0, 0, 0, 3, True, False, scalars, mix_0, old_state, None, None)
-    (back,) = retain(1, 0, 1, 3, True, False, scalars, mix_1, old_state, back, None)
+    (back,) = retain(0, 0, 0, 3, True, False, scalars, mix_a, old_state, None, None)
+    (back,) = retain(1, 1, 1, 3, True, False, scalars, mix_a, old_state, back, None)
     back, mix_c = fence(back, mix_c)
     (back,) = retain(3, 0, 2, 3, True, False, scalars, mix_c, old_state, back, None)
-    back, mix_0, mix_1, mix_c = fence(back, mix_0, mix_1, mix_c)
+    back, mix_a, mix_c = fence(back, mix_a, mix_c)
     back = trade(back)
-    for j, mix in ((0, mix_0), (1, mix_1), (3, mix_c)):
-        (new_state,) = retain(j, 0, 0, 1, False, True, scalars, mix, old_state, None, new_state)
+    for j, at, mix in ((0, 0, mix_a), (1, 1, mix_a), (3, 0, mix_c)):
+        (new_state,) = retain(j, at, 0, 1, False, True, scalars, mix, old_state, None, new_state)
     return settle(place_of, ((2,), (0, 1, 3)), [front, back]), new_state
 
 

time: 242 us -> 236 us (0.975)
  blocking collectives: 11.5 us -> 19.7 us
  waiting for transfers between devices: 83.1 us -> 77.4 us
  other arithmetic: 7.97 us -> 3.55 us
  local copies, waits for them, and re-layouts: 20.4 us -> 17.4 us
    all_to_all x1, blocking collectives: 11.5 us -> 19.7 us  [trade(): return lax.all_to_all(table, 'req', split_axis=0, concat_axis=0, tiled=True)]
    ppermute x6, starting transfers between devices: 4.51 us -> 12 us  [up(): return lax.ppermute(piece, 'req', ring_perm(group, 1))]
    ppermute x6, waiting for transfers between devices: 23.3 us -> 16.2 us  [up(): return lax.ppermute(piece, 'req', ring_perm(group, 1))]
    ppermute x24 -> x21, starting transfers between devices: 24.1 us -> 17 us  [side(): return lax.ppermute(rows, 'req', swap_perm(group, k))]
    ppermute x24 -> x21, waiting for transfers between devices: 37.5 us -> 44.3 us  [side(): return lax.ppermute(rows, 'req', swap_perm(group, k))]
    all_to_all x3, waiting for transfers between devices: 11.9 us -> 7.85 us  [trade(): return lax.all_to_all(table, 'req', split_axis=0, concat_axis=0, tiled=True)]
    unnamed x81 -> x61, local copies, waits for them, and re-layouts: 9.9 us -> 7.02 us
    concatenate x2, other arithmetic: 2.76 us -> 0.09 us  [swaps(): return jnp.concatenate(parts, axis=0)]
  transfers between devices with their start and end apart: 37 -> 34, of which waited for: 17 -> 16; matrix products, arithmetic and copies ran while one was open for 6% -> 4% of each run, Pallas kernels for 23% -> 26%
where the time goes in v4:
time: 236 us; the launch traced here: 235 us
  waiting for transfers between devices  77.4 us (33%)
  Pallas kernels  65.4 us (28%)
  starting transfers between devices  48.9 us (21%)
  blocking collectives  19.7 us (8%)
  local copies, waits for them, and re-layouts  17.4 us (7%)
  other arithmetic  3.55 us (2%)
    ppermute x21, waiting for transfers between devices, side(): return lax.ppermute(rows, 'req', swap_perm(group, k))  44.3 us
    pallas_call x7, Pallas kernels, retain(): pl.pallas_call(lambda *refs: retain_kernel(head, key_dim, value_dim, len(...  35.9 us
    all_to_all x1, blocking collectives, trade(): return lax.all_to_all(table, 'req', split_axis=0, concat_axis=0, tiled=True)  19.7 us
    pallas_call x3, Pallas kernels, project(): pl.pallas_call(lambda *refs: project_kernel(len(pieces), *refs), out_shap...  19.1 us
    all_to_all x3, starting transfers between devices, trade(): return lax.all_to_all(table, 'req', split_axis=0, concat_axis=0, tiled=True)  17.2 us
    ppermute x21, starting transfers between devices, side(): return lax.ppermute(rows, 'req', swap_perm(group, k))  17 us
    ppermute x6, waiting for transfers between devices, up(): return lax.ppermute(piece, 'req', ring_perm(group, 1))  16.2 us
    ppermute x6, starting transfers between devices, up(): return lax.ppermute(piece, 'req', ring_perm(group, 1))  12 us
  transfers between devices with their start and end apart: 34, of which 16 were waited for; matrix products, arithmetic and copies ran while one was open for 4% of the time, Pallas kernels for 26%

profile of v4, /device:TPU:9, one launch (start us, length us, event | category | flops | bytes accessed | tf_op | source)
XLA Modules:
  0.0 234.7 jit_solution(6944663759201136344)
XLA Ops:
  4.5 2.6 %pack.1 = (bf16[128,768]{1,0:T(8,128)(2,1)}, bf16[128,768]{1,0:T(8,128)(2,1)}, bf16[128,768]{1,0:T(8,128)(2,1)}, bf16[128,768]{1,0:T(8,128)(2,1)}, bf16[128,384]...) custom-call(s32[1]{0:T(128)} %bitcast.10.refs_0_.member_ref.refs_3_,, ...), custom_call_target="tpu_custom_call" | custom-call | flops 1 | bytes 1 | tf_op jit(solution)/shard_map/pack/pallas_call | solution.py:171
  10.5 1.9 collective-permute-done.1
  12.4 2.2 collective-permute-done.2
  16.2 19.7 %all_to_all.56 = s32[16,1,128]{2,1,0:T(1,128)S(1)} all-to-all(s32[16,1,128]{2,1,0:T(1,128)S(1)} %bitcast.46), channel_id=1, replica_groups=mesh['req'=16,'head'=2] {'req'}, dimensions={0} | all-to-all | bytes 16384 | tf_op jit(solution)/shard_map/all_to_all | solution.py:141
  36.0 7.8 %gather_fusion.2 = bf16[512,1024]{1,0:T(8,128)(2,1)} fusion(bf16[4000,1024]{1,0:T(8,128)(2,1)} %param.14, s32[1024]{0:T(1024)S(1)} %pad_clamp_fusion.3), kind=kCustom, calls=%fused_computation.2 | custom fusion | bytes 2099200 | tf_op jit(solution)/shard_map/jit(_take)/gather | solution.py:115
  44.7 5.3 %all-to-all-start.3 = ((bf16[16,32,1024]{2,1,0:T(8,128)(2,1)}), bf16[16,32,1024]{2,1,0:T(8,128)(2,1)S(1)}, u32[]{:S(2)}, u32[]{:S(2)}) async-start(bf16[16,32,1024]{2,1,0:T(8,128)(2,1)} %bitcast.13), calls=%async_computation.3 | async-start | bytes 2097152 | tf_op jit(solution)/shard_map/all_to_all | solution.py:141
  53.1 10.8 %collective-permute-done.7 = bf16[128,768]{1,0:T(8,128)(2,1)S(1)} collective-permute-done((bf16[128,768]{1,0:T(8,128)(2,1)}, bf16[128,768]{1,0:T(8,128)(2,1)S(1)}, u32[]{:S(2)}, u32[]{:S(2)}) %collective-permute-start.7) | collective-permute-done | bytes 196640 | tf_op jit(solution)/shard_map/ppermute | solution.py:477
  63.9 6.5 %collective-permute-done.6 = bf16[128,768]{1,0:T(8,128)(2,1)S(1)} collective-permute-done((bf16[128,768]{1,0:T(8,128)(2,1)}, bf16[128,768]{1,0:T(8,128)(2,1)S(1)}, u32[]{:S(2)}, u32[]{:S(2)}) %collective-permute-start.6) | collective-permute-done | bytes 196640 | tf_op jit(solution)/shard_map/ppermute | solution.py:477
  70.4 4.4 %all-to-all-done.3 = bf16[16,32,1024]{2,1,0:T(8,128)(2,1)S(1)} async-done(((bf16[16,32,1024]{2,1,0:T(8,128)(2,1)}), bf16[16,32,1024]{2,1,0:T(8,128)(2,1)S(1)}, u32[]{:S(2)}, u32[]{:S(2)}) %all-to-all-start.3) | async-done | bytes 1048608 | tf_op jit(solution)/shard_map/all_to_all | solution.py:141
  80.7 8.4 %collective-permute-done.10.refs_5_ = bf16[512,384]{1,0:T(8,128)(2,1)S(1)} collective-permute-done((bf16[512,384]{1,0:T(8,128)(2,1)S(1)}, bf16[512,384]{1,0:T(8,128)(2,1)S(1)}, u32[]{:S(2)}, u32[]{:S(2)}) %collective-permute-start.10) | collective-permute-done | bytes 393248 | tf_op jit(solution)/shard_map/ppermute | solution.py:471
  96.0 13.6 %collective-permute-done.15 = bf16[128,384]{1,0:T(8,128)(2,1)S(1)} collective-permute-done((bf16[128,384]{1,0:T(8,128)(2,1)S(1)}, bf16[128,384]{1,0:T(8,128)(2,1)S(1)}, u32[]{:S(2)}, u32[]{:S(2)}) %collective-permute-start.15) | collective-permute-done | bytes 98336 | tf_op jit(solution)/shard_map/ppermute | solution.py:477
  111.2 4.9 %norm.1.refs_1_ = bf16[2,256,2048]{2,1,0:T(8,128)(2,1)} custom-call(s32[1]{0:T(128)} %bitcast.12.low_ref, s32[1]{0:T(128)} %bitcast.10.refs_0_.member_ref.refs_3_, bf16[256,1024]{1,0:T(8,128)(2,1)S(1)} %get-tuple-element.353.own_ref, bf16[256,1024]{1,0:T(8,128)(2,1)} %copy-done.14, bf16[256,1024]{1,0:T(8,128)(2,1)} %copy-done.15, ...), custom_call_target="tpu_custom_call" | custom-call | flops 1 | bytes 1 | tf_op jit(solution)/shard_map/norm/pallas_call | solution.py:221
  116.1 7.7 %collective-permute-done.16.refs_6_ = bf16[512,768]{1,0:T(8,128)(2,1)} collective-permute-done((bf16[512,768]{1,0:T(8,128)(2,1)S(1)}, bf16[512,768]{1,0:T(8,128)(2,1)}, u32[]{:S(2)}, u32[]{:S(2)}) %collective-permute-start.16) | collective-permute-done | bytes 786464 | tf_op jit(solution)/shard_map/ppermute | solution.py:474
  124.5 3.7 %collective-permute-done.17.refs_2_ = bf16[2,256,2048]{2,1,0:T(8,128)(2,1)S(1)} collective-permute-done((bf16[2,256,2048]{2,1,0:T(8,128)(2,1)}, bf16[2,256,2048]{2,1,0:T(8,128)(2,1)S(1)}, u32[]{:S(2)}, u32[]{:S(2)}) %collective-permute-start.17) | collective-permute-done | bytes 2097184 | tf_op jit(solution)/shard_map/ppermute | solution.py:477
  129.6 5.7 %project.3 = (bf16[256,384]{1,0:T(8,128)(2,1)}, bf16[256,384]{1,0:T(8,128)(2,1)}, bf16[256,384]{1,0:T(8,128)(2,1)}, bf16[256,384]{1,0:T(8,128)(2,1)}) custom-call(s32[1]{0:T(128)} %bitcast.11.refs_0_, bf16[2,256,2048]{2,1,0:T(8,128)(2,1)} %norm.1.refs_1_, bf16[2,256,2048]{2,1,0:T(8,128)(2,1)} %copy-done, bf16[512,384]{1,0:T(8,128)(2,1)} %copy-done.13, ...), custom_call_target="tpu_custom_call" | custom-call | flops 1 | bytes 1 | tf_op jit(solution)/shard_map/project/pallas_call | solution.py:276
  135.6 1.8 collective-permute-start.20
  137.4 6.2 %collective-permute-done.21.refs_5_ = bf16[512,768]{1,0:T(8,128)(2,1)S(1)} collective-permute-done((bf16[512,768]{1,0:T(8,128)(2,1)}, bf16[512,768]{1,0:T(8,128)(2,1)S(1)}, u32[]{:S(2)}, u32[]{:S(2)}) %collective-permute-start.21) | collective-permute-done | bytes 786464 | tf_op jit(solution)/shard_map/ppermute | solution.py:471
  143.6 3.1 %collective-permute-done.20.refs_7_ = bf16[256,384]{1,0:T(8,128)(2,1)S(1)} collective-permute-done((bf16[256,384]{1,0:T(8,128)(2,1)}, bf16[256,384]{1,0:T(8,128)(2,1)S(1)}, u32[]{:S(2)}, u32[]{:S(2)}) %collective-permute-start.20) | collective-permute-done | bytes 196640 | tf_op jit(solution)/shard_map/ppermute | solution.py:477
  148.2 7.6 %project.4 = (bf16[256,768]{1,0:T(8,128)(2,1)}, bf16[256,768]{1,0:T(8,128)(2,1)}, bf16[256,768]{1,0:T(8,128)(2,1)}, bf16[256,768]{1,0:T(8,128)(2,1)}) custom-call(s32[1]{0:T(128)} %bitcast.11.refs_0_, bf16[2,256,2048]{2,1,0:T(8,128)(2,1)} %norm.1.refs_1_, bf16[2,256,2048]{2,1,0:T(8,128)(2,1)} %copy-done, bf16[512,768]{1,0:T(8,128)(2,1)} %copy-done.5, ...), custom_call_target="tpu_custom_call" | custom-call | flops 1 | bytes 1 | tf_op jit(solution)/shard_map/project/pallas_call | solution.py:276
  158.8 8.5 %collective-permute-start.26 = (bf16[512,384]{1,0:T(8,128)(2,1)S(1)}, bf16[512,384]{1,0:T(8,128)(2,1)S(1)}, u32[]{:S(2)}, u32[]{:S(2)}) collective-permute-start(bf16[512,384]{1,0:T(8,128)(2,1)S(1)} %collective-permute-done.22.refs_4_), channel_id=1, source_target_pairs={{0,8},{2,10},{4,12},{6,14},{8,16},{10,18},{12,20},{14,22},{16,24},... | collective-permute-start | bytes 1179656 | tf_op jit(solution)/shard_map/ppermute | solution.py:471
  169.2 6.0 %retain.7 = (bf16[16,16,512]{2,1,0:T(8,128)(2,1)}, bf16[16,4,256,512]{3,2,1,0:T(8,128)(2,1)}) custom-call(s32[16]{0:T(128)} %copy-done.27, s32[16]{0:T(128)} %refs_1_.15, f32[4]{0:T(128)} %negate_log-plus-one_fusion.refs_2_, s32[1]{0:T(128)} %bitcast.10.refs_0_.member_ref.refs_3_, bf16[256,384]{1,0:T(8,128)(2,1)} %get-tuple-element.383.refs_4_, ...), custom_call_target="tpu_custom_call" | custom-call | flops 1 | bytes 1 | tf_op jit(solution)/shard_map/retain/pallas_call | solution.py:371
  175.2 5.3 %all-to-all-start.4 = ((bf16[16,16,512]{2,1,0:T(8,128)(2,1)}), bf16[16,16,512]{2,1,0:T(8,128)(2,1)S(1)}, u32[]{:S(2)}, u32[]{:S(2)}) async-start(bf16[16,16,512]{2,1,0:T(8,128)(2,1)} %get-tuple-element.387), calls=%async_computation.4 | async-start | bytes 524288 | tf_op jit(solution)/shard_map/all_to_all | solution.py:141
  181.3 5.7 %project.5 = (bf16[256,384]{1,0:T(8,128)(2,1)}, bf16[256,384]{1,0:T(8,128)(2,1)}, bf16[256,384]{1,0:T(8,128)(2,1)}, bf16[256,384]{1,0:T(8,128)(2,1)}) custom-call(s32[1]{0:T(128)} %bitcast.11.refs_0_, bf16[2,256,2048]{2,1,0:T(8,128)(2,1)} %norm.1.refs_1_, bf16[2,256,2048]{2,1,0:T(8,128)(2,1)} %copy-done, bf16[512,384]{1,0:T(8,128)(2,1)} %copy-done.6, ...), custom_call_target="tpu_custom_call" | custom-call | flops 1 | bytes 1 | tf_op jit(solution)/shard_map/project/pallas_call | solution.py:276
  189.3 4.6 %retain.8.refs_9_ = bf16[16,16,1536]{2,1,0:T(8,128)(2,1)} custom-call(s32[16]{0:T(128)} %copy-done.27, s32[16]{0:T(128)} %refs_1_.15, f32[4]{0:T(128)} %negate_log-plus-one_fusion.refs_2_, s32[1]{0:T(128)} %bitcast.10.refs_0_.member_ref.refs_3_, bf16[256,768]{1,0:T(8,128)(2,1)} %get-tuple-element.419.refs_4_, bf16[256,768]{1,0:T(8,128)(2,1)} %copy-done.1, ...), custom_call_target="tpu_custom_call" | custom-call | flops 1 | bytes 1 | tf_op jit(solution)/shard_map/retain/pallas_call | solution.py:371
  193.9 4.6 %retain.9.refs_9_ = bf16[16,16,1536]{2,1,0:T(8,128)(2,1)} custom-call(s32[16]{0:T(128)} %copy-done.27, s32[16]{0:T(128)} %refs_1_.15, f32[4]{0:T(128)} %negate_log-plus-one_fusion.refs_2_, s32[1]{0:T(128)} %bitcast.10.refs_0_.member_ref.refs_3_, bf16[256,768]{1,0:T(8,128)(2,1)} %get-tuple-element.419.refs_4_, ...), custom_call_target="tpu_custom_call", output_to_operand_aliasing={{}: (9, {})} | custom-call | flops 1 | bytes 1 | tf_op jit(solution)/shard_map/retain/pallas_call | solution.py:371
  200.0 4.6 %retain.10 = bf16[16,16,1536]{2,1,0:T(8,128)(2,1)} custom-call(s32[16]{0:T(128)} %copy-done.27, s32[16]{0:T(128)} %refs_1_.15, f32[4]{0:T(128)} %negate_log-plus-one_fusion.refs_2_, s32[1]{0:T(128)} %bitcast.10.refs_0_.member_ref.refs_3_, bf16[256,384]{1,0:T(8,128)(2,1)} %get-tuple-element.415.refs_4_, ...), custom_call_target="tpu_custom_call", output_to_operand_aliasing={{}: (9, {})} | custom-call | flops 1 | bytes 1 | tf_op jit(solution)/shard_map/retain/pallas_call | solution.py:371
  204.6 6.7 %all-to-all-start.5 = ((bf16[16,16,1536]{2,1,0:T(8,128)(2,1)}), bf16[16,16,1536]{2,1,0:T(8,128)(2,1)S(1)}, u32[]{:S(2)}, u32[]{:S(2)}) async-start(bf16[16,16,1536]{2,1,0:T(8,128)(2,1)} %retain.10), calls=%async_computation.5 | async-start | bytes 1572864 | tf_op jit(solution)/shard_map/all_to_all | solution.py:141
  211.3 5.4 %retain.11.refs_9_ = bf16[16,4,256,512]{3,2,1,0:T(8,128)(2,1)} custom-call(s32[16]{0:T(128)} %copy-done.27, s32[16]{0:T(128)} %refs_1_.15, f32[4]{0:T(128)} %negate_log-plus-one_fusion.refs_2_, s32[1]{0:T(128)} %bitcast.10.refs_0_.member_ref.refs_3_, bf16[256,768]{1,0:T(8,128)(2,1)} %get-tuple-element.419.refs_4_, ...), custom_call_target="tpu_custom_call", output_to_operand_aliasing={{}: (9, {})} | custom-call | flops 1 | bytes 1 | tf_op jit(solution)/shard_map/retain/pallas_call | solution.py:371
  216.7 5.4 %retain.12.refs_9_ = bf16[16,4,256,512]{3,2,1,0:T(8,128)(2,1)} custom-call(s32[16]{0:T(128)} %copy-done.27, s32[16]{0:T(128)} %refs_1_.15, f32[4]{0:T(128)} %negate_log-plus-one_fusion.refs_2_, s32[1]{0:T(128)} %bitcast.10.refs_0_.member_ref.refs_3_, bf16[256,768]{1,0:T(8,128)(2,1)} %get-tuple-element.419.refs_4_, ...), custom_call_target="tpu_custom_call", output_to_operand_aliasing={{}: (9, {})} | custom-call | flops 1 | bytes 1 | tf_op jit(solution)/shard_map/retain/pallas_call | solution.py:371
  222.0 5.4 %retain.13 = bf16[16,4,256,512]{3,2,1,0:T(8,128)(2,1)} custom-call(s32[16]{0:T(128)} %copy-done.27, s32[16]{0:T(128)} %refs_1_.15, f32[4]{0:T(128)} %negate_log-plus-one_fusion.refs_2_, s32[1]{0:T(128)} %bitcast.10.refs_0_.member_ref.refs_3_, bf16[256,384]{1,0:T(8,128)(2,1)} %get-tuple-element.415.refs_4_, ...), custom_call_target="tpu_custom_call", output_to_operand_aliasing={{}: (9, {})} | custom-call | flops 1 | bytes 1 | tf_op jit(solution)/shard_map/retain/pallas_call | solution.py:371
  227.4 3.5 %all-to-all-done.5.refs_2_ = bf16[16,16,1536]{2,1,0:T(8,128)(2,1)S(1)} async-done(((bf16[16,16,1536]{2,1,0:T(8,128)(2,1)}), bf16[16,16,1536]{2,1,0:T(8,128)(2,1)S(1)}, u32[]{:S(2)}, u32[]{:S(2)}) %all-to-all-start.5) | async-done | bytes 786464 | tf_op jit(solution)/shard_map/all_to_all | solution.py:141
  231.8 2.9 %settle.1 = bf16[16,16,2048]{2,1,0:T(8,128)(2,1)} custom-call(s32[16]{0:T(128)} %get-tuple-element.425.refs_0_, bf16[16,16,512]{2,1,0:T(8,128)(2,1)} %copy-done.7, bf16[16,16,1536]{2,1,0:T(8,128)(2,1)} %copy-done.4), custom_call_target="tpu_custom_call" | custom-call | flops 1 | bytes 1 | tf_op jit(solution)/shard_map/settle/pallas_call | solution.py:407
  (143 shorter events, 40.8 us)
Async XLA Ops:
  7.8 4.6 %collective-permute-start.1 = (bf16[128,384]{1,0:T(8,128)(2,1)}, bf16[128,384]{1,0:T(8,128)(2,1)S(1)}, u32[]{:S(2)}, u32[]{:S(2)}) collective-permute-start(bf16[128,384]{1,0:T(8,128)(2,1)} %get-tuple-element.342), channel_id=1, source_target_pairs={{0,4},{2,6},{4,0},{6,2},{8,12},{10,14},{12,8},{14,10},{16,20},{18,... | collective-permute-start | bytes 294920 | tf_op jit(solution)/shard_map/ppermute | solution.py:477
  9.0 5.6 %collective-permute-start.2 = (bf16[128,384]{1,0:T(8,128)(2,1)}, bf16[128,384]{1,0:T(8,128)(2,1)S(1)}, u32[]{:S(2)}, u32[]{:S(2)}) collective-permute-start(bf16[128,384]{1,0:T(8,128)(2,1)} %get-tuple-element.343), channel_id=1, source_target_pairs={{0,6},{2,4},{4,2},{6,0},{8,14},{10,12},{12,10},{14,8},{16,22},{18,... | collective-permute-start | bytes 294920 | tf_op jit(solution)/shard_map/ppermute | solution.py:477
  14.7 29.2 %collective-permute-start.3 = (bf16[512,384]{1,0:T(8,128)(2,1)S(1)}, bf16[512,384]{1,0:T(8,128)(2,1)S(1)}, u32[]{:S(2)}, u32[]{:S(2)}) collective-permute-start(bf16[512,384]{1,0:T(8,128)(2,1)S(1)} %constant_dynamic-update-slice_fusion.refs_3_), channel_id=1, source_target_pairs={{0,8},{2,10},{4,12},{6,14},{8,16},{10,18},{12,20},{14,22},{16,24},... | collective-permute-start | bytes 1179656 | tf_op jit(solution)/shard_map/ppermute | solution.py:471
  16.0 27.9 %collective-permute-start.4 = (bf16[512,384]{1,0:T(8,128)(2,1)S(1)}, bf16[512,384]{1,0:T(8,128)(2,1)S(1)}, u32[]{:S(2)}, u32[]{:S(2)}) collective-permute-start(bf16[512,384]{1,0:T(8,128)(2,1)S(1)} %constant_dynamic-update-slice_fusion.refs_3_), channel_id=1, source_target_pairs={{0,24},{2,26},{4,28},{6,30},{8,0},{10,2},{12,4},{14,6},{16,8},{18,... | collective-permute-start | bytes 1179656 | tf_op jit(solution)/shard_map/ppermute | solution.py:474
  44.7 30.1 %all-to-all-start.3 = ((bf16[16,32,1024]{2,1,0:T(8,128)(2,1)}), bf16[16,32,1024]{2,1,0:T(8,128)(2,1)S(1)}, u32[]{:S(2)}, u32[]{:S(2)}) async-start(bf16[16,32,1024]{2,1,0:T(8,128)(2,1)} %bitcast.13), calls=%async_computation.3 | async-start | bytes 2097152 | tf_op jit(solution)/shard_map/all_to_all | solution.py:141
  49.9 13.9 %collective-permute-start.7 = (bf16[128,768]{1,0:T(8,128)(2,1)}, bf16[128,768]{1,0:T(8,128)(2,1)S(1)}, u32[]{:S(2)}, u32[]{:S(2)}) collective-permute-start(bf16[128,768]{1,0:T(8,128)(2,1)} %get-tuple-element.349), channel_id=1, source_target_pairs={{0,6},{2,4},{4,2},{6,0},{8,14},{10,12},{12,10},{14,8},{16,22},{18,... | collective-permute-start | bytes 589832 | tf_op jit(solution)/shard_map/ppermute | solution.py:477
  51.4 19.0 %collective-permute-start.6 = (bf16[128,768]{1,0:T(8,128)(2,1)}, bf16[128,768]{1,0:T(8,128)(2,1)S(1)}, u32[]{:S(2)}, u32[]{:S(2)}) collective-permute-start(bf16[128,768]{1,0:T(8,128)(2,1)} %get-tuple-element.348), channel_id=1, source_target_pairs={{0,4},{2,6},{4,0},{6,2},{8,12},{10,14},{12,8},{14,10},{16,20},{18,... | collective-permute-start | bytes 589832 | tf_op jit(solution)/shard_map/ppermute | solution.py:477
  51.7 18.7 %collective-permute-start.5 = (bf16[128,768]{1,0:T(8,128)(2,1)}, bf16[128,768]{1,0:T(8,128)(2,1)S(1)}, u32[]{:S(2)}, u32[]{:S(2)}) collective-permute-start(bf16[128,768]{1,0:T(8,128)(2,1)} %get-tuple-element.347), channel_id=1, source_target_pairs={{0,2},{2,0},{4,6},{6,4},{8,10},{10,8},{12,14},{14,12},{16,18},{18,... | collective-permute-start | bytes 589832 | tf_op jit(solution)/shard_map/ppermute | solution.py:477
  76.7 13.8 %collective-permute-start.8 = (bf16[256,1024]{1,0:T(8,128)(2,1)S(1)}, bf16[256,1024]{1,0:T(8,128)(2,1)S(1)}, u32[]{:S(2)}, u32[]{:S(2)}) collective-permute-start(bf16[256,1024]{1,0:T(8,128)(2,1)S(1)} %get-tuple-element.353.own_ref), channel_id=1, source_target_pairs={{0,1},{1,0},{2,3},{3,2},{4,5},{5,4},{6,7},{7,6},{8,9},{9,8},{10,11... | collective-permute-start | bytes 1572872 | tf_op jit(solution)/shard_map/ppermute | solution.py:493
  78.0 13.5 %collective-permute-start.9 = (bf16[256,1024]{1,0:T(8,128)(2,1)S(1)}, bf16[256,1024]{1,0:T(8,128)(2,1)S(1)}, u32[]{:S(2)}, u32[]{:S(2)}) collective-permute-start(bf16[256,1024]{1,0:T(8,128)(2,1)S(1)} %get-tuple-element.353.own_ref), channel_id=1, source_target_pairs={{0,4},{2,6},{4,0},{6,2},{8,12},{10,14},{12,8},{14,10},{16,20},{18,... | collective-permute-start | bytes 1572872 | tf_op jit(solution)/shard_map/ppermute | solution.py:477
  79.2 9.9 %collective-permute-start.10 = (bf16[512,384]{1,0:T(8,128)(2,1)S(1)}, bf16[512,384]{1,0:T(8,128)(2,1)S(1)}, u32[]{:S(2)}, u32[]{:S(2)}) collective-permute-start(bf16[512,384]{1,0:T(8,128)(2,1)S(1)} %collective-permute-done.3.refs_4_), channel_id=1, source_target_pairs={{0,8},{2,10},{4,12},{6,14},{8,16},{10,18},{12,20},{14,22},{16,24},... | collective-permute-start | bytes 1179656 | tf_op jit(solution)/shard_map/ppermute | solution.py:471
  79.2 31.9 %collective-permute-start.12 = (bf16[512,768]{1,0:T(8,128)(2,1)S(1)}, bf16[512,768]{1,0:T(8,128)(2,1)S(1)}, u32[]{:S(2)}, u32[]{:S(2)}) collective-permute-start(bf16[512,768]{1,0:T(8,128)(2,1)S(1)} %pad_maximum_fusion.refs_3_), channel_id=1, source_target_pairs={{0,8},{2,10},{4,12},{6,14},{8,16},{10,18},{12,20},{14,22},{16,24},... | collective-permute-start | bytes 2359304 | tf_op jit(solution)/shard_map/ppermute | solution.py:471
  80.6 43.1 %collective-permute-start.16 = (bf16[512,768]{1,0:T(8,128)(2,1)S(1)}, bf16[512,768]{1,0:T(8,128)(2,1)}, u32[]{:S(2)}, u32[]{:S(2)}) collective-permute-start(bf16[512,768]{1,0:T(8,128)(2,1)S(1)} %pad_maximum_fusion.refs_3_), channel_id=1, source_target_pairs={{0,24},{2,26},{4,28},{6,30},{8,0},{10,2},{12,4},{14,6},{16,8},{18,... | collective-permute-start | bytes 2359304 | tf_op jit(solution)/shard_map/ppermute | solution.py:474
  92.3 18.8 %collective-permute-start.11 = (bf16[256,1024]{1,0:T(8,128)(2,1)S(1)}, bf16[256,1024]{1,0:T(8,128)(2,1)}, u32[]{:S(2)}, u32[]{:S(2)}) collective-permute-start(bf16[256,1024]{1,0:T(8,128)(2,1)S(1)} %collective-permute-done.8.own_far_ref), channel_id=1, source_target_pairs={{0,4},{2,6},{4,0},{6,2},{8,12},{10,14},{12,8},{14,10},{16,20},{18,... | collective-permute-start | bytes 1572872 | tf_op jit(solution)/shard_map/ppermute | solution.py:477
  93.0 16.5 %collective-permute-start.15 = (bf16[128,384]{1,0:T(8,128)(2,1)S(1)}, bf16[128,384]{1,0:T(8,128)(2,1)S(1)}, u32[]{:S(2)}, u32[]{:S(2)}) collective-permute-start(bf16[128,384]{1,0:T(8,128)(2,1)S(1)} %copy-done.28), channel_id=1, source_target_pairs={{0,6},{2,4},{4,2},{6,0},{8,14},{10,12},{12,10},{14,8},{16,22},{18,... | collective-permute-start | bytes 294920 | tf_op jit(solution)/shard_map/ppermute | solution.py:477
  94.8 14.7 %collective-permute-start.14 = (bf16[128,384]{1,0:T(8,128)(2,1)}, bf16[128,384]{1,0:T(8,128)(2,1)S(1)}, u32[]{:S(2)}, u32[]{:S(2)}) collective-permute-start(bf16[128,384]{1,0:T(8,128)(2,1)} %get-tuple-element.360), channel_id=1, source_target_pairs={{0,4},{2,6},{4,0},{6,2},{8,12},{10,14},{12,8},{14,10},{16,20},{18,... | collective-permute-start | bytes 294920 | tf_op jit(solution)/shard_map/ppermute | solution.py:477
  123.7 4.5 %collective-permute-start.17 = (bf16[2,256,2048]{2,1,0:T(8,128)(2,1)}, bf16[2,256,2048]{2,1,0:T(8,128)(2,1)S(1)}, u32[]{:S(2)}, u32[]{:S(2)}) collective-permute-start(bf16[2,256,2048]{2,1,0:T(8,128)(2,1)} %norm.1.refs_1_), channel_id=1, source_target_pairs={{0,2},{2,0},{4,6},{6,4},{8,10},{10,8},{12,14},{14,12},{16,18},{18,... | collective-permute-start | bytes 6291464 | tf_op jit(solution)/shard_map/ppermute | solution.py:477
  124.2 19.4 %collective-permute-start.21 = (bf16[512,768]{1,0:T(8,128)(2,1)}, bf16[512,768]{1,0:T(8,128)(2,1)S(1)}, u32[]{:S(2)}, u32[]{:S(2)}) collective-permute-start(bf16[512,768]{1,0:T(8,128)(2,1)} %copy-done.11), channel_id=1, source_target_pairs={{0,8},{2,10},{4,12},{6,14},{8,16},{10,18},{12,20},{14,22},{16,24},... | collective-permute-start | bytes 2359304 | tf_op jit(solution)/shard_map/ppermute | solution.py:471
  135.3 8.3 %collective-permute-start.18 = (bf16[256,384]{1,0:T(8,128)(2,1)}, bf16[256,384]{1,0:T(8,128)(2,1)S(1)}, u32[]{:S(2)}, u32[]{:S(2)}) collective-permute-start(bf16[256,384]{1,0:T(8,128)(2,1)} %get-tuple-element.367), channel_id=1, source_target_pairs={{0,2},{2,0},{4,6},{6,4},{8,10},{10,8},{12,14},{14,12},{16,18},{18,... | collective-permute-start | bytes 589832 | tf_op jit(solution)/shard_map/ppermute | solution.py:477
  135.6 8.0 %collective-permute-start.19 = (bf16[256,384]{1,0:T(8,128)(2,1)}, bf16[256,384]{1,0:T(8,128)(2,1)S(1)}, u32[]{:S(2)}, u32[]{:S(2)}) collective-permute-start(bf16[256,384]{1,0:T(8,128)(2,1)} %get-tuple-element.368), channel_id=1, source_target_pairs={{0,4},{2,6},{4,0},{6,2},{8,12},{10,14},{12,8},{14,10},{16,20},{18,... | collective-permute-start | bytes 589832 | tf_op jit(solution)/shard_map/ppermute | solution.py:477
  135.6 11.0 %collective-permute-start.20 = (bf16[256,384]{1,0:T(8,128)(2,1)}, bf16[256,384]{1,0:T(8,128)(2,1)S(1)}, u32[]{:S(2)}, u32[]{:S(2)}) collective-permute-start(bf16[256,384]{1,0:T(8,128)(2,1)} %get-tuple-element.369), channel_id=1, source_target_pairs={{0,6},{2,4},{4,2},{6,0},{8,14},{10,12},{12,10},{14,8},{16,22},{18,... | collective-permute-start | bytes 589832 | tf_op jit(solution)/shard_map/ppermute | solution.py:477
  146.7 10.8 %collective-permute-start.22 = (bf16[512,384]{1,0:T(8,128)(2,1)S(1)}, bf16[512,384]{1,0:T(8,128)(2,1)S(1)}, u32[]{:S(2)}, u32[]{:S(2)}) collective-permute-start(bf16[512,384]{1,0:T(8,128)(2,1)S(1)} %pad_maximum_fusion.1.refs_3_), channel_id=1, source_target_pairs={{0,8},{2,10},{4,12},{6,14},{8,16},{10,18},{12,20},{14,22},{16,24},... | collective-permute-start | bytes 1179656 | tf_op jit(solution)/shard_map/ppermute | solution.py:471
  147.0 33.4 %collective-permute-start.25 = (bf16[512,384]{1,0:T(8,128)(2,1)S(1)}, bf16[512,384]{1,0:T(8,128)(2,1)}, u32[]{:S(2)}, u32[]{:S(2)}) collective-permute-start(bf16[512,384]{1,0:T(8,128)(2,1)S(1)} %pad_maximum_fusion.1.refs_3_), channel_id=1, source_target_pairs={{0,24},{2,26},{4,28},{6,30},{8,0},{10,2},{12,4},{14,6},{16,8},{18,... | collective-permute-start | bytes 1179656 | tf_op jit(solution)/shard_map/ppermute | solution.py:474
  157.5 29.6 %collective-permute-start.23 = (bf16[256,768]{1,0:T(8,128)(2,1)}, bf16[256,768]{1,0:T(8,128)(2,1)S(1)}, u32[]{:S(2)}, u32[]{:S(2)}) collective-permute-start(bf16[256,768]{1,0:T(8,128)(2,1)} %get-tuple-element.389), channel_id=1, source_target_pairs={{0,2},{2,0},{4,6},{6,4},{8,10},{10,8},{12,14},{14,12},{16,18},{18,... | collective-permute-start | bytes 1179656 | tf_op jit(solution)/shard_map/ppermute | solution.py:477
  158.7 21.8 %collective-permute-start.24 = (bf16[256,768]{1,0:T(8,128)(2,1)}, bf16[256,768]{1,0:T(8,128)(2,1)S(1)}, u32[]{:S(2)}, u32[]{:S(2)}) collective-permute-start(bf16[256,768]{1,0:T(8,128)(2,1)} %get-tuple-element.391), channel_id=1, source_target_pairs={{0,4},{2,6},{4,0},{6,2},{8,12},{10,14},{12,8},{14,10},{16,20},{18,... | collective-permute-start | bytes 1179656 | tf_op jit(solution)/shard_map/ppermute | solution.py:477
  158.8 21.7 %collective-permute-start.26 = (bf16[512,384]{1,0:T(8,128)(2,1)S(1)}, bf16[512,384]{1,0:T(8,128)(2,1)S(1)}, u32[]{:S(2)}, u32[]{:S(2)}) collective-permute-start(bf16[512,384]{1,0:T(8,128)(2,1)S(1)} %collective-permute-done.22.refs_4_), channel_id=1, source_target_pairs={{0,8},{2,10},{4,12},{6,14},{8,16},{10,18},{12,20},{14,22},{16,24},... | collective-permute-start | bytes 1179656 | tf_op jit(solution)/shard_map/ppermute | solution.py:471
  167.3 19.8 %collective-permute-start.27 = (bf16[256,768]{1,0:T(8,128)(2,1)}, bf16[256,768]{1,0:T(8,128)(2,1)S(1)}, u32[]{:S(2)}, u32[]{:S(2)}) collective-permute-start(bf16[256,768]{1,0:T(8,128)(2,1)} %get-tuple-element.394), channel_id=1, source_target_pairs={{0,6},{2,4},{4,2},{6,0},{8,14},{10,12},{12,10},{14,8},{16,22},{18,... | collective-permute-start | bytes 1179656 | tf_op jit(solution)/shard_map/ppermute | solution.py:477
  175.2 29.4 %all-to-all-start.4 = ((bf16[16,16,512]{2,1,0:T(8,128)(2,1)}), bf16[16,16,512]{2,1,0:T(8,128)(2,1)S(1)}, u32[]{:S(2)}, u32[]{:S(2)}) async-start(bf16[16,16,512]{2,1,0:T(8,128)(2,1)} %get-tuple-element.387), calls=%async_computation.4 | async-start | bytes 524288 | tf_op jit(solution)/shard_map/all_to_all | solution.py:141
  187.1 11.5 %collective-permute-start.28 = (bf16[256,384]{1,0:T(8,128)(2,1)}, bf16[256,384]{1,0:T(8,128)(2,1)S(1)}, u32[]{:S(2)}, u32[]{:S(2)}) collective-permute-start(bf16[256,384]{1,0:T(8,128)(2,1)} %get-tuple-element.406), channel_id=1, source_target_pairs={{0,2},{2,0},{4,6},{6,4},{8,10},{10,8},{12,14},{14,12},{16,18},{18,... | collective-permute-start | bytes 589832 | tf_op jit(solution)/shard_map/ppermute | solution.py:477
  187.5 11.1 %collective-permute-start.29 = (bf16[256,384]{1,0:T(8,128)(2,1)}, bf16[256,384]{1,0:T(8,128)(2,1)S(1)}, u32[]{:S(2)}, u32[]{:S(2)}) collective-permute-start(bf16[256,384]{1,0:T(8,128)(2,1)} %get-tuple-element.407), channel_id=1, source_target_pairs={{0,4},{2,6},{4,0},{6,2},{8,12},{10,14},{12,8},{14,10},{16,20},{18,... | collective-permute-start | bytes 589832 | tf_op jit(solution)/shard_map/ppermute | solution.py:477
  188.7 9.9 %collective-permute-start.30 = (bf16[256,384]{1,0:T(8,128)(2,1)}, bf16[256,384]{1,0:T(8,128)(2,1)S(1)}, u32[]{:S(2)}, u32[]{:S(2)}) collective-permute-start(bf16[256,384]{1,0:T(8,128)(2,1)} %get-tuple-element.408), channel_id=1, source_target_pairs={{0,6},{2,4},{4,2},{6,0},{8,14},{10,12},{12,10},{14,8},{16,22},{18,... | collective-permute-start | bytes 589832 | tf_op jit(solution)/shard_map/ppermute | solution.py:477
  204.6 26.3 %all-to-all-start.5 = ((bf16[16,16,1536]{2,1,0:T(8,128)(2,1)}), bf16[16,16,1536]{2,1,0:T(8,128)(2,1)S(1)}, u32[]{:S(2)}, u32[]{:S(2)}) async-start(bf16[16,16,1536]{2,1,0:T(8,128)(2,1)} %retain.10), calls=%async_computation.5 | async-start | bytes 1572864 | tf_op jit(solution)/shard_map/all_to_all | solution.py:141
  (31 other events, 357.6 us)

commit v5 on v4

--- a/solution.py
+++ b/solution.py
@@ -118,10 +118,7 @@
         got = trade(picked.reshape(self.width, self.cap, self.cols)).reshape(rows, self.cols)
         return jnp.take(got, self.holder * self.cap + self.rank % self.cap, axis=0, mode="clip")
 
-    def fetch(self, asked=None, found=None):
-        heard = trade(self.table)
-        if asked is not None:
-            heard = after(heard, asked)
+    def fetch(self, heard, found=None):
         place_of = heard[:, self.cap]
         rounds = jnp.max(heard[:, self.cap + 1])
         first = self.rows_for(heard[:, : self.cap], found)
@@ -484,15 +481,17 @@
 
     plane_b, plane_a = swaps(1), swaps(0)
     one_b, three_b = up(plane_b), down(plane_b)
-    first, finish, place_of = tokens.fetch(asked=(plane_b,), found=(one_b, three_b))
+    heard = after(trade(tokens.table), plane_b)
+    two_b = up(after(one_b, heard))
+    first, finish, place_of = tokens.fetch(heard, found=(three_b, two_b))
     first, plane_a = fence(first, plane_a)
     half = finish(first)
 
-    two_b, one_a = up(after(one_b, half)), up(after(plane_a, half))
+    one_a = up(after(plane_a, half))
     three_a = down(after(plane_a, half))
     other = lax.ppermute(half, "head", [(0, 1), (1, 0)])
     half_x = side(half, 2)
-    half, other, half_x, two_b = fence(half, other, half_x, two_b)
+    half, other, half_x = fence(half, other, half_x)
     other_x = side(other, 2)
     plane_c = swaps(2)
     other_x, one_a, plane_c = fence(other_x, one_a, plane_c)
@@ -533,7 +532,8 @@
         lax.all_gather(table, "req", axis=0, tiled=True)
         for table in (w_query, w_key, w_value, w_gate)
     ]
-    half, finish, place_of = Asked(draft_ids, worker_slot, embedding).fetch()
+    asked = Asked(draft_ids, worker_slot, embedding)
+    half, finish, place_of = asked.fetch(trade(asked.table))
     half = finish(half)
     tokens = lax.all_gather(half, "head", axis=1, tiled=True)
     normed = layer_norm(tokens.astype(jnp.float32)).astype(jnp.bfloat16)

time: 236 us -> 225 us (0.953)
  blocking collectives: 19.7 us -> 0 us
  starting transfers between devices: 48.9 us -> 57.4 us
    all_to_all x1 -> x0, blocking collectives: 19.7 us -> none  [trade(): return lax.all_to_all(table, 'req', split_axis=0, concat_axis=0, tiled=True)]
    all_to_all x3 -> x4, starting transfers between devices: 17.2 us -> 27.1 us  [trade(): return lax.all_to_all(table, 'req', split_axis=0, concat_axis=0, tiled=True)]
    ppermute x6, waiting for transfers between devices: 16.2 us -> 7.61 us  [up(): return lax.ppermute(piece, 'req', ring_perm(group, 1))]
    ppermute x1, waiting for transfers between devices: 1.41 us -> 9.81 us  [fast_device(): other = lax.ppermute(half, 'head', [(0, 1), (1, 0)])]
    ppermute x3, waiting for transfers between devices: 7.66 us -> 0.01 us  [down(): return lax.ppermute(piece, 'req', ring_perm(group, -1))]
    all_to_all x3 -> x4, waiting for transfers between devices: 7.85 us -> 14.4 us  [trade(): return lax.all_to_all(table, 'req', split_axis=0, concat_axis=0, tiled=True)]
    ppermute x6, starting transfers between devices: 12 us -> 9.22 us  [up(): return lax.ppermute(piece, 'req', ring_perm(group, 1))]
    unnamed x61 -> x71, local copies, waits for them, and re-layouts: 7.02 us -> 7.84 us
  transfers between devices with their start and end apart: 34 -> 35, of which waited for: 16 -> 15; matrix products, arithmetic and copies ran while one was open for 4% -> 5% of each run, Pallas kernels for 26% -> 27%
where the time goes in v5:
time: 225 us; the launch traced here: 224 us
  waiting for transfers between devices  76.5 us (34%)
  Pallas kernels  65.4 us (29%)
  starting transfers between devices  57.4 us (26%)
  local copies, waits for them, and re-layouts  18.2 us (8%)
  other arithmetic  4.16 us (2%)
    ppermute x21, waiting for transfers between devices, side(): return lax.ppermute(rows, 'req', swap_perm(group, k))  44.7 us
    pallas_call x7, Pallas kernels, retain(): pl.pallas_call(lambda *refs: retain_kernel(head, key_dim, value_dim, len(...  35.9 us
    all_to_all x4, starting transfers between devices, trade(): return lax.all_to_all(table, 'req', split_axis=0, concat_axis=0, tiled=True)  27.1 us
    pallas_call x3, Pallas kernels, project(): pl.pallas_call(lambda *refs: project_kernel(len(pieces), *refs), out_shap...  19.1 us
    ppermute x21, starting transfers between devices, side(): return lax.ppermute(rows, 'req', swap_perm(group, k))  16.9 us
    all_to_all x4, waiting for transfers between devices, trade(): return lax.all_to_all(table, 'req', split_axis=0, concat_axis=0, tiled=True)  14.4 us
    ppermute x1, waiting for transfers between devices, fast_device(): other = lax.ppermute(half, 'head', [(0, 1), (1, 0)])  9.81 us
    ppermute x6, starting transfers between devices, up(): return lax.ppermute(piece, 'req', ring_perm(group, 1))  9.22 us
  transfers between devices with their start and end apart: 35, of which 15 were waited for; matrix products, arithmetic and copies ran while one was open for 5% of the time, Pallas kernels for 27%

profile of v5, /device:TPU:9, one launch (start us, length us, event | category | flops | bytes accessed | tf_op | source)
XLA Modules:
  0.0 224.2 jit_solution(13167223817024775381)
XLA Ops:
  5.1 2.6 %pack.1 = (bf16[128,768]{1,0:T(8,128)(2,1)}, bf16[128,768]{1,0:T(8,128)(2,1)}, bf16[128,768]{1,0:T(8,128)(2,1)}, bf16[128,768]{1,0:T(8,128)(2,1)}, bf16[128,384]...) custom-call(s32[1]{0:T(128)} %bitcast.10.refs_0_.member_ref.refs_3_,, ...), custom_call_target="tpu_custom_call" | custom-call | flops 1 | bytes 1 | tf_op jit(solution)/shard_map/pack/pallas_call | solution.py:168
  11.0 1.9 collective-permute-done.1
  13.0 2.2 %collective-permute-done.2 = bf16[128,384]{1,0:T(8,128)(2,1)S(1)} collective-permute-done((bf16[128,384]{1,0:T(8,128)(2,1)}, bf16[128,384]{1,0:T(8,128)(2,1)S(1)}, u32[]{:S(2)}, u32[]{:S(2)}) %collective-permute-start.2) | collective-permute-done | bytes 98336 | tf_op jit(solution)/shard_map/ppermute | solution.py:474
  16.6 5.4 %all-to-all-start.2 = ((s32[16,1,128]{2,1,0:T(1,128)}), s32[16,1,128]{2,1,0:T(1,128)S(1)}, u32[]{:S(2)}, u32[]{:S(2)}) async-start(s32[16,1,128]{2,1,0:T(1,128)} %bitcast.8), calls=%async_computation.2 | async-start | bytes 16384 | tf_op jit(solution)/shard_map/all_to_all | solution.py:138
  22.1 6.5 %all-to-all-done.2 = s32[16,1,128]{2,1,0:T(1,128)S(1)} async-done(((s32[16,1,128]{2,1,0:T(1,128)}), s32[16,1,128]{2,1,0:T(1,128)S(1)}, u32[]{:S(2)}, u32[]{:S(2)}) %all-to-all-start.2) | async-done | bytes 8224 | tf_op jit(solution)/shard_map/all_to_all | solution.py:138
  28.6 7.7 %collective-permute-start.5 = (bf16[512,384]{1,0:T(8,128)(2,1)S(1)}, bf16[512,384]{1,0:T(8,128)(2,1)S(1)}, u32[]{:S(2)}, u32[]{:S(2)}) collective-permute-start(bf16[512,384]{1,0:T(8,128)(2,1)S(1)} %collective-permute-done.4.refs_4_), channel_id=1, source_target_pairs={{0,8},{2,10},{4,12},{6,14},{8,16},{10,18},{12,20},{14,22},{16,24},... | collective-permute-start | bytes 1179656 | tf_op jit(solution)/shard_map/ppermute | solution.py:468
  36.4 7.8 %gather_fusion.2 = bf16[512,1024]{1,0:T(8,128)(2,1)} fusion(bf16[4000,1024]{1,0:T(8,128)(2,1)} %param.14, s32[1024]{0:T(1024)S(1)} %pad_clamp_fusion.3), kind=kCustom, calls=%fused_computation.2 | custom fusion | bytes 2099200 | tf_op jit(solution)/shard_map/jit(_take)/gather | solution.py:115
  45.2 7.8 %all-to-all-start.3 = ((bf16[16,32,1024]{2,1,0:T(8,128)(2,1)}), bf16[16,32,1024]{2,1,0:T(8,128)(2,1)S(1)}, u32[]{:S(2)}, u32[]{:S(2)}) async-start(bf16[16,32,1024]{2,1,0:T(8,128)(2,1)} %bitcast.13), calls=%async_computation.3 | async-start | bytes 2097152 | tf_op jit(solution)/shard_map/all_to_all | solution.py:138
  56.3 10.7 %collective-permute-done.8 = bf16[128,768]{1,0:T(8,128)(2,1)S(1)} collective-permute-done((bf16[128,768]{1,0:T(8,128)(2,1)S(1)}, bf16[128,768]{1,0:T(8,128)(2,1)S(1)}, u32[]{:S(2)}, u32[]{:S(2)}) %collective-permute-start.8) | collective-permute-done | bytes 196640 | tf_op jit(solution)/shard_map/ppermute | solution.py:474
  67.0 6.5 %collective-permute-done.7 = bf16[128,768]{1,0:T(8,128)(2,1)S(1)} collective-permute-done((bf16[128,768]{1,0:T(8,128)(2,1)S(1)}, bf16[128,768]{1,0:T(8,128)(2,1)S(1)}, u32[]{:S(2)}, u32[]{:S(2)}) %collective-permute-start.7) | collective-permute-done | bytes 196640 | tf_op jit(solution)/shard_map/ppermute | solution.py:474
  73.6 4.4 %all-to-all-done.3 = bf16[16,32,1024]{2,1,0:T(8,128)(2,1)S(1)} async-done(((bf16[16,32,1024]{2,1,0:T(8,128)(2,1)}), bf16[16,32,1024]{2,1,0:T(8,128)(2,1)S(1)}, u32[]{:S(2)}, u32[]{:S(2)}) %all-to-all-start.3) | async-done | bytes 1048608 | tf_op jit(solution)/shard_map/all_to_all | solution.py:138
  83.8 9.8 %collective-permute-done.9.own_far_ref = bf16[256,1024]{1,0:T(8,128)(2,1)S(1)} collective-permute-done((bf16[256,1024]{1,0:T(8,128)(2,1)S(1)}, bf16[256,1024]{1,0:T(8,128)(2,1)S(1)}, u32[]{:S(2)}, u32[]{:S(2)}) %collective-permute-start.9) | collective-permute-done | bytes 524320 | tf_op jit(solution)/shard_map/ppermute | solution.py:492
  99.1 13.6 %collective-permute-done.15 = bf16[128,384]{1,0:T(8,128)(2,1)S(1)} collective-permute-done((bf16[128,384]{1,0:T(8,128)(2,1)S(1)}, bf16[128,384]{1,0:T(8,128)(2,1)S(1)}, u32[]{:S(2)}, u32[]{:S(2)}) %collective-permute-start.15) | collective-permute-done | bytes 98336 | tf_op jit(solution)/shard_map/ppermute | solution.py:474
  114.1 4.9 %norm.1.refs_1_ = bf16[2,256,2048]{2,1,0:T(8,128)(2,1)} custom-call(s32[1]{0:T(128)} %bitcast.12.low_ref, s32[1]{0:T(128)} %bitcast.10.refs_0_.member_ref.refs_3_, bf16[256,1024]{1,0:T(8,128)(2,1)S(1)} %get-tuple-element.352.own_ref, bf16[256,1024]{1,0:T(8,128)(2,1)} %copy-done.14, bf16[256,1024]{1,0:T(8,128)(2,1)} %copy-done.15, ...), custom_call_target="tpu_custom_call" | custom-call | flops 1 | bytes 1 | tf_op jit(solution)/shard_map/norm/pallas_call | solution.py:218
  119.3 4.1 %collective-permute-done.17.refs_2_ = bf16[2,256,2048]{2,1,0:T(8,128)(2,1)S(1)} collective-permute-done((bf16[2,256,2048]{2,1,0:T(8,128)(2,1)}, bf16[2,256,2048]{2,1,0:T(8,128)(2,1)S(1)}, u32[]{:S(2)}, u32[]{:S(2)}) %collective-permute-start.17) | collective-permute-done | bytes 2097184 | tf_op jit(solution)/shard_map/ppermute | solution.py:474
  124.8 5.7 %project.3 = (bf16[256,384]{1,0:T(8,128)(2,1)}, bf16[256,384]{1,0:T(8,128)(2,1)}, bf16[256,384]{1,0:T(8,128)(2,1)}, bf16[256,384]{1,0:T(8,128)(2,1)}) custom-call(s32[1]{0:T(128)} %bitcast.11.refs_0_, bf16[2,256,2048]{2,1,0:T(8,128)(2,1)} %norm.1.refs_1_, bf16[2,256,2048]{2,1,0:T(8,128)(2,1)} %copy-done, bf16[512,384]{1,0:T(8,128)(2,1)} %copy-done.13, ...), custom_call_target="tpu_custom_call" | custom-call | flops 1 | bytes 1 | tf_op jit(solution)/shard_map/project/pallas_call | solution.py:273
  132.6 5.7 %collective-permute-done.21.refs_5_ = bf16[512,768]{1,0:T(8,128)(2,1)S(1)} collective-permute-done((bf16[512,768]{1,0:T(8,128)(2,1)}, bf16[512,768]{1,0:T(8,128)(2,1)S(1)}, u32[]{:S(2)}, u32[]{:S(2)}) %collective-permute-start.21) | collective-permute-done | bytes 786464 | tf_op jit(solution)/shard_map/ppermute | solution.py:468
  138.4 3.3 %collective-permute-done.20.refs_7_ = bf16[256,384]{1,0:T(8,128)(2,1)S(1)} collective-permute-done((bf16[256,384]{1,0:T(8,128)(2,1)}, bf16[256,384]{1,0:T(8,128)(2,1)S(1)}, u32[]{:S(2)}, u32[]{:S(2)}) %collective-permute-start.20) | collective-permute-done | bytes 196640 | tf_op jit(solution)/shard_map/ppermute | solution.py:474
  143.9 7.6 %project.4 = (bf16[256,768]{1,0:T(8,128)(2,1)}, bf16[256,768]{1,0:T(8,128)(2,1)}, bf16[256,768]{1,0:T(8,128)(2,1)}, bf16[256,768]{1,0:T(8,128)(2,1)}) custom-call(s32[1]{0:T(128)} %bitcast.11.refs_0_, bf16[2,256,2048]{2,1,0:T(8,128)(2,1)} %norm.1.refs_1_, bf16[2,256,2048]{2,1,0:T(8,128)(2,1)} %copy-done, bf16[512,768]{1,0:T(8,128)(2,1)} %copy-done.5, ...), custom_call_target="tpu_custom_call" | custom-call | flops 1 | bytes 1 | tf_op jit(solution)/shard_map/project/pallas_call | solution.py:273
  151.5 1.9 collective-permute-done.22.refs_4_
  156.8 6.0 %retain.7 = (bf16[16,16,512]{2,1,0:T(8,128)(2,1)}, bf16[16,4,256,512]{3,2,1,0:T(8,128)(2,1)}) custom-call(s32[16]{0:T(128)} %copy-done.27, s32[16]{0:T(128)} %refs_1_.15, f32[4]{0:T(128)} %negate_log-plus-one_fusion.refs_2_, s32[1]{0:T(128)} %bitcast.10.refs_0_.member_ref.refs_3_, bf16[256,384]{1,0:T(8,128)(2,1)} %get-tuple-element.381.refs_4_, ...), custom_call_target="tpu_custom_call" | custom-call | flops 1 | bytes 1 | tf_op jit(solution)/shard_map/retain/pallas_call | solution.py:368
  162.8 7.8 %all-to-all-start.4 = ((bf16[16,16,512]{2,1,0:T(8,128)(2,1)}), bf16[16,16,512]{2,1,0:T(8,128)(2,1)S(1)}, u32[]{:S(2)}, u32[]{:S(2)}) async-start(bf16[16,16,512]{2,1,0:T(8,128)(2,1)} %get-tuple-element.385), calls=%async_computation.4 | async-start | bytes 524288 | tf_op jit(solution)/shard_map/all_to_all | solution.py:138
  171.4 5.8 %project.5 = (bf16[256,384]{1,0:T(8,128)(2,1)}, bf16[256,384]{1,0:T(8,128)(2,1)}, bf16[256,384]{1,0:T(8,128)(2,1)}, bf16[256,384]{1,0:T(8,128)(2,1)}) custom-call(s32[1]{0:T(128)} %bitcast.11.refs_0_, bf16[2,256,2048]{2,1,0:T(8,128)(2,1)} %norm.1.refs_1_, bf16[2,256,2048]{2,1,0:T(8,128)(2,1)} %copy-done, bf16[512,384]{1,0:T(8,128)(2,1)} %copy-done.6, ...), custom_call_target="tpu_custom_call" | custom-call | flops 1 | bytes 1 | tf_op jit(solution)/shard_map/project/pallas_call | solution.py:273
  179.4 4.6 %retain.8.refs_9_ = bf16[16,16,1536]{2,1,0:T(8,128)(2,1)} custom-call(s32[16]{0:T(128)} %copy-done.27, s32[16]{0:T(128)} %refs_1_.15, f32[4]{0:T(128)} %negate_log-plus-one_fusion.refs_2_, s32[1]{0:T(128)} %bitcast.10.refs_0_.member_ref.refs_3_, bf16[256,768]{1,0:T(8,128)(2,1)} %get-tuple-element.417.refs_4_, bf16[256,768]{1,0:T(8,128)(2,1)} %copy-done.1, ...), custom_call_target="tpu_custom_call" | custom-call | flops 1 | bytes 1 | tf_op jit(solution)/shard_map/retain/pallas_call | solution.py:368
  184.0 4.6 %retain.9.refs_9_ = bf16[16,16,1536]{2,1,0:T(8,128)(2,1)} custom-call(s32[16]{0:T(128)} %copy-done.27, s32[16]{0:T(128)} %refs_1_.15, f32[4]{0:T(128)} %negate_log-plus-one_fusion.refs_2_, s32[1]{0:T(128)} %bitcast.10.refs_0_.member_ref.refs_3_, bf16[256,768]{1,0:T(8,128)(2,1)} %get-tuple-element.417.refs_4_, ...), custom_call_target="tpu_custom_call", output_to_operand_aliasing={{}: (9, {})} | custom-call | flops 1 | bytes 1 | tf_op jit(solution)/shard_map/retain/pallas_call | solution.py:368
  190.1 4.6 %retain.10 = bf16[16,16,1536]{2,1,0:T(8,128)(2,1)} custom-call(s32[16]{0:T(128)} %copy-done.27, s32[16]{0:T(128)} %refs_1_.15, f32[4]{0:T(128)} %negate_log-plus-one_fusion.refs_2_, s32[1]{0:T(128)} %bitcast.10.refs_0_.member_ref.refs_3_, bf16[256,384]{1,0:T(8,128)(2,1)} %get-tuple-element.413.refs_4_, ...), custom_call_target="tpu_custom_call", output_to_operand_aliasing={{}: (9, {})} | custom-call | flops 1 | bytes 1 | tf_op jit(solution)/shard_map/retain/pallas_call | solution.py:368
  194.7 6.1 %all-to-all-start.5 = ((bf16[16,16,1536]{2,1,0:T(8,128)(2,1)}), bf16[16,16,1536]{2,1,0:T(8,128)(2,1)S(1)}, u32[]{:S(2)}, u32[]{:S(2)}) async-start(bf16[16,16,1536]{2,1,0:T(8,128)(2,1)} %retain.10), calls=%async_computation.5 | async-start | bytes 1572864 | tf_op jit(solution)/shard_map/all_to_all | solution.py:138
  200.8 5.4 %retain.11.refs_9_ = bf16[16,4,256,512]{3,2,1,0:T(8,128)(2,1)} custom-call(s32[16]{0:T(128)} %copy-done.27, s32[16]{0:T(128)} %refs_1_.15, f32[4]{0:T(128)} %negate_log-plus-one_fusion.refs_2_, s32[1]{0:T(128)} %bitcast.10.refs_0_.member_ref.refs_3_, bf16[256,768]{1,0:T(8,128)(2,1)} %get-tuple-element.417.refs_4_, ...), custom_call_target="tpu_custom_call", output_to_operand_aliasing={{}: (9, {})} | custom-call | flops 1 | bytes 1 | tf_op jit(solution)/shard_map/retain/pallas_call | solution.py:368
  206.1 5.4 %retain.12.refs_9_ = bf16[16,4,256,512]{3,2,1,0:T(8,128)(2,1)} custom-call(s32[16]{0:T(128)} %copy-done.27, s32[16]{0:T(128)} %refs_1_.15, f32[4]{0:T(128)} %negate_log-plus-one_fusion.refs_2_, s32[1]{0:T(128)} %bitcast.10.refs_0_.member_ref.refs_3_, bf16[256,768]{1,0:T(8,128)(2,1)} %get-tuple-element.417.refs_4_, ...), custom_call_target="tpu_custom_call", output_to_operand_aliasing={{}: (9, {})} | custom-call | flops 1 | bytes 1 | tf_op jit(solution)/shard_map/retain/pallas_call | solution.py:368
  211.5 5.4 %retain.13 = bf16[16,4,256,512]{3,2,1,0:T(8,128)(2,1)} custom-call(s32[16]{0:T(128)} %copy-done.27, s32[16]{0:T(128)} %refs_1_.15, f32[4]{0:T(128)} %negate_log-plus-one_fusion.refs_2_, s32[1]{0:T(128)} %bitcast.10.refs_0_.member_ref.refs_3_, bf16[256,384]{1,0:T(8,128)(2,1)} %get-tuple-element.413.refs_4_, ...), custom_call_target="tpu_custom_call", output_to_operand_aliasing={{}: (9, {})} | custom-call | flops 1 | bytes 1 | tf_op jit(solution)/shard_map/retain/pallas_call | solution.py:368
  216.8 3.5 %all-to-all-done.5.refs_2_ = bf16[16,16,1536]{2,1,0:T(8,128)(2,1)S(1)} async-done(((bf16[16,16,1536]{2,1,0:T(8,128)(2,1)}), bf16[16,16,1536]{2,1,0:T(8,128)(2,1)S(1)}, u32[]{:S(2)}, u32[]{:S(2)}) %all-to-all-start.5) | async-done | bytes 786464 | tf_op jit(solution)/shard_map/all_to_all | solution.py:138
  221.3 2.9 %settle.1 = bf16[16,16,2048]{2,1,0:T(8,128)(2,1)} custom-call(s32[16]{0:T(128)} %get-tuple-element.423.refs_0_, bf16[16,16,512]{2,1,0:T(8,128)(2,1)} %copy-done.7, bf16[16,16,1536]{2,1,0:T(8,128)(2,1)} %copy-done.4), custom_call_target="tpu_custom_call" | custom-call | flops 1 | bytes 1 | tf_op jit(solution)/shard_map/settle/pallas_call | solution.py:404
  (154 shorter events, 40.3 us)
Async XLA Ops:
  8.4 4.6 %collective-permute-start.1 = (bf16[128,384]{1,0:T(8,128)(2,1)}, bf16[128,384]{1,0:T(8,128)(2,1)S(1)}, u32[]{:S(2)}, u32[]{:S(2)}) collective-permute-start(bf16[128,384]{1,0:T(8,128)(2,1)} %get-tuple-element.341), channel_id=1, source_target_pairs={{0,4},{2,6},{4,0},{6,2},{8,12},{10,14},{12,8},{14,10},{16,20},{18,... | collective-permute-start | bytes 294920 | tf_op jit(solution)/shard_map/ppermute | solution.py:474
  9.6 5.6 %collective-permute-start.2 = (bf16[128,384]{1,0:T(8,128)(2,1)}, bf16[128,384]{1,0:T(8,128)(2,1)S(1)}, u32[]{:S(2)}, u32[]{:S(2)}) collective-permute-start(bf16[128,384]{1,0:T(8,128)(2,1)} %get-tuple-element.342), channel_id=1, source_target_pairs={{0,6},{2,4},{4,2},{6,0},{8,14},{10,12},{12,10},{14,8},{16,22},{18,... | collective-permute-start | bytes 294920 | tf_op jit(solution)/shard_map/ppermute | solution.py:474
  15.3 13.3 %collective-permute-start.4 = (bf16[512,384]{1,0:T(8,128)(2,1)S(1)}, bf16[512,384]{1,0:T(8,128)(2,1)S(1)}, u32[]{:S(2)}, u32[]{:S(2)}) collective-permute-start(bf16[512,384]{1,0:T(8,128)(2,1)S(1)} %constant_dynamic-update-slice_fusion.refs_3_), channel_id=1, source_target_pairs={{0,8},{2,10},{4,12},{6,14},{8,16},{10,18},{12,20},{14,22},{16,24},... | collective-permute-start | bytes 1179656 | tf_op jit(solution)/shard_map/ppermute | solution.py:468
  16.6 12.0 %all-to-all-start.2 = ((s32[16,1,128]{2,1,0:T(1,128)}), s32[16,1,128]{2,1,0:T(1,128)S(1)}, u32[]{:S(2)}, u32[]{:S(2)}) async-start(s32[16,1,128]{2,1,0:T(1,128)} %bitcast.8), calls=%async_computation.2 | async-start | bytes 16384 | tf_op jit(solution)/shard_map/all_to_all | solution.py:138
  22.0 22.3 %collective-permute-start.3 = (bf16[512,384]{1,0:T(8,128)(2,1)S(1)}, bf16[512,384]{1,0:T(8,128)(2,1)S(1)}, u32[]{:S(2)}, u32[]{:S(2)}) collective-permute-start(bf16[512,384]{1,0:T(8,128)(2,1)S(1)} %constant_dynamic-update-slice_fusion.refs_3_), channel_id=1, source_target_pairs={{0,24},{2,26},{4,28},{6,30},{8,0},{10,2},{12,4},{14,6},{16,8},{18,... | collective-permute-start | bytes 1179656 | tf_op jit(solution)/shard_map/ppermute | solution.py:471
  28.6 15.7 %collective-permute-start.5 = (bf16[512,384]{1,0:T(8,128)(2,1)S(1)}, bf16[512,384]{1,0:T(8,128)(2,1)S(1)}, u32[]{:S(2)}, u32[]{:S(2)}) collective-permute-start(bf16[512,384]{1,0:T(8,128)(2,1)S(1)} %collective-permute-done.4.refs_4_), channel_id=1, source_target_pairs={{0,8},{2,10},{4,12},{6,14},{8,16},{10,18},{12,20},{14,22},{16,24},... | collective-permute-start | bytes 1179656 | tf_op jit(solution)/shard_map/ppermute | solution.py:468
  45.2 32.7 %all-to-all-start.3 = ((bf16[16,32,1024]{2,1,0:T(8,128)(2,1)}), bf16[16,32,1024]{2,1,0:T(8,128)(2,1)S(1)}, u32[]{:S(2)}, u32[]{:S(2)}) async-start(bf16[16,32,1024]{2,1,0:T(8,128)(2,1)} %bitcast.13), calls=%async_computation.3 | async-start | bytes 2097152 | tf_op jit(solution)/shard_map/all_to_all | solution.py:138
  53.1 13.9 %collective-permute-start.8 = (bf16[128,768]{1,0:T(8,128)(2,1)S(1)}, bf16[128,768]{1,0:T(8,128)(2,1)S(1)}, u32[]{:S(2)}, u32[]{:S(2)}) collective-permute-start(bf16[128,768]{1,0:T(8,128)(2,1)S(1)} %copy-done.30), channel_id=1, source_target_pairs={{0,6},{2,4},{4,2},{6,0},{8,14},{10,12},{12,10},{14,8},{16,22},{18,... | collective-permute-start | bytes 589832 | tf_op jit(solution)/shard_map/ppermute | solution.py:474
  54.6 18.9 %collective-permute-start.7 = (bf16[128,768]{1,0:T(8,128)(2,1)S(1)}, bf16[128,768]{1,0:T(8,128)(2,1)S(1)}, u32[]{:S(2)}, u32[]{:S(2)}) collective-permute-start(bf16[128,768]{1,0:T(8,128)(2,1)S(1)} %copy-done.29), channel_id=1, source_target_pairs={{0,4},{2,6},{4,0},{6,2},{8,12},{10,14},{12,8},{14,10},{16,20},{18,... | collective-permute-start | bytes 589832 | tf_op jit(solution)/shard_map/ppermute | solution.py:474
  54.8 18.6 %collective-permute-start.6 = (bf16[128,768]{1,0:T(8,128)(2,1)S(1)}, bf16[128,768]{1,0:T(8,128)(2,1)S(1)}, u32[]{:S(2)}, u32[]{:S(2)}) collective-permute-start(bf16[128,768]{1,0:T(8,128)(2,1)S(1)} %copy-done.28), channel_id=1, source_target_pairs={{0,2},{2,0},{4,6},{6,4},{8,10},{10,8},{12,14},{14,12},{16,18},{18,... | collective-permute-start | bytes 589832 | tf_op jit(solution)/shard_map/ppermute | solution.py:474
  79.8 13.8 %collective-permute-start.9 = (bf16[256,1024]{1,0:T(8,128)(2,1)S(1)}, bf16[256,1024]{1,0:T(8,128)(2,1)S(1)}, u32[]{:S(2)}, u32[]{:S(2)}) collective-permute-start(bf16[256,1024]{1,0:T(8,128)(2,1)S(1)} %get-tuple-element.352.own_ref), channel_id=1, source_target_pairs={{0,1},{1,0},{2,3},{3,2},{4,5},{5,4},{6,7},{7,6},{8,9},{9,8},{10,11... | collective-permute-start | bytes 1572872 | tf_op jit(solution)/shard_map/ppermute | solution.py:492
  81.1 13.5 %collective-permute-start.10 = (bf16[256,1024]{1,0:T(8,128)(2,1)S(1)}, bf16[256,1024]{1,0:T(8,128)(2,1)S(1)}, u32[]{:S(2)}, u32[]{:S(2)}) collective-permute-start(bf16[256,1024]{1,0:T(8,128)(2,1)S(1)} %get-tuple-element.352.own_ref), channel_id=1, source_target_pairs={{0,4},{2,6},{4,0},{6,2},{8,12},{10,14},{12,8},{14,10},{16,20},{18,... | collective-permute-start | bytes 1572872 | tf_op jit(solution)/shard_map/ppermute | solution.py:474
  82.4 31.7 %collective-permute-start.12 = (bf16[512,768]{1,0:T(8,128)(2,1)S(1)}, bf16[512,768]{1,0:T(8,128)(2,1)S(1)}, u32[]{:S(2)}, u32[]{:S(2)}) collective-permute-start(bf16[512,768]{1,0:T(8,128)(2,1)S(1)} %pad_maximum_fusion.refs_3_), channel_id=1, source_target_pairs={{0,8},{2,10},{4,12},{6,14},{8,16},{10,18},{12,20},{14,22},{16,24},... | collective-permute-start | bytes 2359304 | tf_op jit(solution)/shard_map/ppermute | solution.py:468
  82.4 36.6 %collective-permute-start.16 = (bf16[512,768]{1,0:T(8,128)(2,1)S(1)}, bf16[512,768]{1,0:T(8,128)(2,1)}, u32[]{:S(2)}, u32[]{:S(2)}) collective-permute-start(bf16[512,768]{1,0:T(8,128)(2,1)S(1)} %pad_maximum_fusion.refs_3_), channel_id=1, source_target_pairs={{0,24},{2,26},{4,28},{6,30},{8,0},{10,2},{12,4},{14,6},{16,8},{18,... | collective-permute-start | bytes 2359304 | tf_op jit(solution)/shard_map/ppermute | solution.py:471
  95.5 18.6 %collective-permute-start.11 = (bf16[256,1024]{1,0:T(8,128)(2,1)S(1)}, bf16[256,1024]{1,0:T(8,128)(2,1)}, u32[]{:S(2)}, u32[]{:S(2)}) collective-permute-start(bf16[256,1024]{1,0:T(8,128)(2,1)S(1)} %collective-permute-done.9.own_far_ref), channel_id=1, source_target_pairs={{0,4},{2,6},{4,0},{6,2},{8,12},{10,14},{12,8},{14,10},{16,20},{18,... | collective-permute-start | bytes 1572872 | tf_op jit(solution)/shard_map/ppermute | solution.py:474
  96.2 16.5 %collective-permute-start.15 = (bf16[128,384]{1,0:T(8,128)(2,1)S(1)}, bf16[128,384]{1,0:T(8,128)(2,1)S(1)}, u32[]{:S(2)}, u32[]{:S(2)}) collective-permute-start(bf16[128,384]{1,0:T(8,128)(2,1)S(1)} %copy-done.33), channel_id=1, source_target_pairs={{0,6},{2,4},{4,2},{6,0},{8,14},{10,12},{12,10},{14,8},{16,22},{18,... | collective-permute-start | bytes 294920 | tf_op jit(solution)/shard_map/ppermute | solution.py:474
  97.9 14.8 %collective-permute-start.14 = (bf16[128,384]{1,0:T(8,128)(2,1)S(1)}, bf16[128,384]{1,0:T(8,128)(2,1)S(1)}, u32[]{:S(2)}, u32[]{:S(2)}) collective-permute-start(bf16[128,384]{1,0:T(8,128)(2,1)S(1)} %copy-done.32), channel_id=1, source_target_pairs={{0,4},{2,6},{4,0},{6,2},{8,12},{10,14},{12,8},{14,10},{16,20},{18,... | collective-permute-start | bytes 294920 | tf_op jit(solution)/shard_map/ppermute | solution.py:474
  119.2 19.2 %collective-permute-start.21 = (bf16[512,768]{1,0:T(8,128)(2,1)}, bf16[512,768]{1,0:T(8,128)(2,1)S(1)}, u32[]{:S(2)}, u32[]{:S(2)}) collective-permute-start(bf16[512,768]{1,0:T(8,128)(2,1)} %copy-done.11), channel_id=1, source_target_pairs={{0,8},{2,10},{4,12},{6,14},{8,16},{10,18},{12,20},{14,22},{16,24},... | collective-permute-start | bytes 2359304 | tf_op jit(solution)/shard_map/ppermute | solution.py:468
  130.5 7.9 %collective-permute-start.18 = (bf16[256,384]{1,0:T(8,128)(2,1)}, bf16[256,384]{1,0:T(8,128)(2,1)S(1)}, u32[]{:S(2)}, u32[]{:S(2)}) collective-permute-start(bf16[256,384]{1,0:T(8,128)(2,1)} %get-tuple-element.365), channel_id=1, source_target_pairs={{0,2},{2,0},{4,6},{6,4},{8,10},{10,8},{12,14},{14,12},{16,18},{18,... | collective-permute-start | bytes 589832 | tf_op jit(solution)/shard_map/ppermute | solution.py:474
  130.7 7.7 %collective-permute-start.19 = (bf16[256,384]{1,0:T(8,128)(2,1)}, bf16[256,384]{1,0:T(8,128)(2,1)S(1)}, u32[]{:S(2)}, u32[]{:S(2)}) collective-permute-start(bf16[256,384]{1,0:T(8,128)(2,1)} %get-tuple-element.366), channel_id=1, source_target_pairs={{0,4},{2,6},{4,0},{6,2},{8,12},{10,14},{12,8},{14,10},{16,20},{18,... | collective-permute-start | bytes 589832 | tf_op jit(solution)/shard_map/ppermute | solution.py:474
  131.3 10.4 %collective-permute-start.20 = (bf16[256,384]{1,0:T(8,128)(2,1)}, bf16[256,384]{1,0:T(8,128)(2,1)S(1)}, u32[]{:S(2)}, u32[]{:S(2)}) collective-permute-start(bf16[256,384]{1,0:T(8,128)(2,1)} %get-tuple-element.367), channel_id=1, source_target_pairs={{0,6},{2,4},{4,2},{6,0},{8,14},{10,12},{12,10},{14,8},{16,22},{18,... | collective-permute-start | bytes 589832 | tf_op jit(solution)/shard_map/ppermute | solution.py:474
  142.4 11.0 %collective-permute-start.22 = (bf16[512,384]{1,0:T(8,128)(2,1)S(1)}, bf16[512,384]{1,0:T(8,128)(2,1)S(1)}, u32[]{:S(2)}, u32[]{:S(2)}) collective-permute-start(bf16[512,384]{1,0:T(8,128)(2,1)S(1)} %pad_maximum_fusion.1.refs_3_), channel_id=1, source_target_pairs={{0,8},{2,10},{4,12},{6,14},{8,16},{10,18},{12,20},{14,22},{16,24},... | collective-permute-start | bytes 1179656 | tf_op jit(solution)/shard_map/ppermute | solution.py:468
  142.5 28.0 %collective-permute-start.25 = (bf16[512,384]{1,0:T(8,128)(2,1)S(1)}, bf16[512,384]{1,0:T(8,128)(2,1)}, u32[]{:S(2)}, u32[]{:S(2)}) collective-permute-start(bf16[512,384]{1,0:T(8,128)(2,1)S(1)} %pad_maximum_fusion.1.refs_3_), channel_id=1, source_target_pairs={{0,24},{2,26},{4,28},{6,30},{8,0},{10,2},{12,4},{14,6},{16,8},{18,... | collective-permute-start | bytes 1179656 | tf_op jit(solution)/shard_map/ppermute | solution.py:471
  153.4 23.8 %collective-permute-start.23 = (bf16[256,768]{1,0:T(8,128)(2,1)}, bf16[256,768]{1,0:T(8,128)(2,1)S(1)}, u32[]{:S(2)}, u32[]{:S(2)}) collective-permute-start(bf16[256,768]{1,0:T(8,128)(2,1)} %get-tuple-element.387), channel_id=1, source_target_pairs={{0,2},{2,0},{4,6},{6,4},{8,10},{10,8},{12,14},{14,12},{16,18},{18,... | collective-permute-start | bytes 1179656 | tf_op jit(solution)/shard_map/ppermute | solution.py:474
  154.2 16.3 %collective-permute-start.24 = (bf16[256,768]{1,0:T(8,128)(2,1)}, bf16[256,768]{1,0:T(8,128)(2,1)S(1)}, u32[]{:S(2)}, u32[]{:S(2)}) collective-permute-start(bf16[256,768]{1,0:T(8,128)(2,1)} %get-tuple-element.389), channel_id=1, source_target_pairs={{0,4},{2,6},{4,0},{6,2},{8,12},{10,14},{12,8},{14,10},{16,20},{18,... | collective-permute-start | bytes 1179656 | tf_op jit(solution)/shard_map/ppermute | solution.py:474
  154.9 15.7 %collective-permute-start.26 = (bf16[512,384]{1,0:T(8,128)(2,1)S(1)}, bf16[512,384]{1,0:T(8,128)(2,1)S(1)}, u32[]{:S(2)}, u32[]{:S(2)}) collective-permute-start(bf16[512,384]{1,0:T(8,128)(2,1)S(1)} %collective-permute-done.22.refs_4_), channel_id=1, source_target_pairs={{0,8},{2,10},{4,12},{6,14},{8,16},{10,18},{12,20},{14,22},{16,24},... | collective-permute-start | bytes 1179656 | tf_op jit(solution)/shard_map/ppermute | solution.py:468
  154.9 22.3 %collective-permute-start.27 = (bf16[256,768]{1,0:T(8,128)(2,1)}, bf16[256,768]{1,0:T(8,128)(2,1)S(1)}, u32[]{:S(2)}, u32[]{:S(2)}) collective-permute-start(bf16[256,768]{1,0:T(8,128)(2,1)} %get-tuple-element.392), channel_id=1, source_target_pairs={{0,6},{2,4},{4,2},{6,0},{8,14},{10,12},{12,10},{14,8},{16,22},{18,... | collective-permute-start | bytes 1179656 | tf_op jit(solution)/shard_map/ppermute | solution.py:474
  162.8 31.9 %all-to-all-start.4 = ((bf16[16,16,512]{2,1,0:T(8,128)(2,1)}), bf16[16,16,512]{2,1,0:T(8,128)(2,1)S(1)}, u32[]{:S(2)}, u32[]{:S(2)}) async-start(bf16[16,16,512]{2,1,0:T(8,128)(2,1)} %get-tuple-element.385), calls=%async_computation.4 | async-start | bytes 524288 | tf_op jit(solution)/shard_map/all_to_all | solution.py:138
  177.2 11.5 %collective-permute-start.28 = (bf16[256,384]{1,0:T(8,128)(2,1)}, bf16[256,384]{1,0:T(8,128)(2,1)S(1)}, u32[]{:S(2)}, u32[]{:S(2)}) collective-permute-start(bf16[256,384]{1,0:T(8,128)(2,1)} %get-tuple-element.404), channel_id=1, source_target_pairs={{0,2},{2,0},{4,6},{6,4},{8,10},{10,8},{12,14},{14,12},{16,18},{18,... | collective-permute-start | bytes 589832 | tf_op jit(solution)/shard_map/ppermute | solution.py:474
  177.6 11.0 %collective-permute-start.29 = (bf16[256,384]{1,0:T(8,128)(2,1)}, bf16[256,384]{1,0:T(8,128)(2,1)S(1)}, u32[]{:S(2)}, u32[]{:S(2)}) collective-permute-start(bf16[256,384]{1,0:T(8,128)(2,1)} %get-tuple-element.405), channel_id=1, source_target_pairs={{0,4},{2,6},{4,0},{6,2},{8,12},{10,14},{12,8},{14,10},{16,20},{18,... | collective-permute-start | bytes 589832 | tf_op jit(solution)/shard_map/ppermute | solution.py:474
  178.8 9.9 %collective-permute-start.30 = (bf16[256,384]{1,0:T(8,128)(2,1)}, bf16[256,384]{1,0:T(8,128)(2,1)S(1)}, u32[]{:S(2)}, u32[]{:S(2)}) collective-permute-start(bf16[256,384]{1,0:T(8,128)(2,1)} %get-tuple-element.406), channel_id=1, source_target_pairs={{0,6},{2,4},{4,2},{6,0},{8,14},{10,12},{12,10},{14,8},{16,22},{18,... | collective-permute-start | bytes 589832 | tf_op jit(solution)/shard_map/ppermute | solution.py:474
  194.7 25.7 %all-to-all-start.5 = ((bf16[16,16,1536]{2,1,0:T(8,128)(2,1)}), bf16[16,16,1536]{2,1,0:T(8,128)(2,1)S(1)}, u32[]{:S(2)}, u32[]{:S(2)}) async-start(bf16[16,16,1536]{2,1,0:T(8,128)(2,1)} %retain.10), calls=%async_computation.5 | async-start | bytes 1572864 | tf_op jit(solution)/shard_map/all_to_all | solution.py:138
  (37 other events, 402.7 us)

commit v6 on v5

--- a/solution.py
+++ b/solution.py
@@ -458,7 +458,7 @@
 
     chunks = ((0, 1), (2,), (3,))
     tokens = Asked(draft_ids, worker_slot, embedding)
-    packed = pack(heads, chunks, group, after(me, tokens.table), (w_query, w_key, w_value, w_gate))
+    packed = pack(heads, chunks, group, me, (w_query, w_key, w_value, w_gate))
 
     def swaps(c):
         parts = [part if k == 0 else side(part, k) for k, part in enumerate(packed[c])]

time: 225 us -> 220 us (0.978)
  starting transfers between devices: 57.4 us -> 49.1 us
  waiting for transfers between devices: 76.5 us -> 80.2 us
    ppermute x6, waiting for transfers between devices: 7.61 us -> 15.3 us  [up(): return lax.ppermute(piece, 'req', ring_perm(group, 1))]
    ppermute x6, starting transfers between devices: 9.22 us -> 1.92 us  [up(): return lax.ppermute(piece, 'req', ring_perm(group, 1))]
  transfers between devices with their start and end apart: 35 -> 35, of which waited for: 15 -> 15; matrix products, arithmetic and copies ran while one was open for 5% -> 7% of each run, Pallas kernels for 27% -> 27%
where the time goes in v6:
time: 220 us; the launch traced here: 219 us
  waiting for transfers between devices  80.2 us (36%)
  Pallas kernels  65.4 us (30%)
  starting transfers between devices  49.1 us (22%)
  local copies, waits for them, and re-layouts  18.1 us (8%)
  other arithmetic  4.16 us (2%)
    ppermute x21, waiting for transfers between devices, side(): return lax.ppermute(rows, 'req', swap_perm(group, k))  42.7 us
    pallas_call x7, Pallas kernels, retain(): pl.pallas_call(lambda *refs: retain_kernel(head, key_dim, value_dim, len(...  35.9 us
    all_to_all x4, starting transfers between devices, trade(): return lax.all_to_all(table, 'req', split_axis=0, concat_axis=0, tiled=True)  26.1 us
    pallas_call x3, Pallas kernels, project(): pl.pallas_call(lambda *refs: project_kernel(len(pieces), *refs), out_shap...  19.1 us
    ppermute x21, starting transfers between devices, side(): return lax.ppermute(rows, 'req', swap_perm(group, k))  16.9 us
    ppermute x6, waiting for transfers between devices, up(): return lax.ppermute(piece, 'req', ring_perm(group, 1))  15.3 us
    all_to_all x4, waiting for transfers between devices, trade(): return lax.all_to_all(table, 'req', split_axis=0, concat_axis=0, tiled=True)  12.4 us
    ppermute x1, waiting for transfers between devices, fast_device(): other = lax.ppermute(half, 'head', [(0, 1), (1, 0)])  9.81 us
  transfers between devices with their start and end apart: 35, of which 15 were waited for; matrix products, arithmetic and copies ran while one was open for 7% of the time, Pallas kernels for 27%

profile of v6, /device:TPU:9, one launch (start us, length us, event | category | flops | bytes accessed | tf_op | source)
XLA Modules:
  0.0 219.4 jit_solution(15288765007926151376)
XLA Ops:
  0.6 2.6 %pack.1 = (bf16[128,768]{1,0:T(8,128)(2,1)}, bf16[128,768]{1,0:T(8,128)(2,1)}, bf16[128,768]{1,0:T(8,128)(2,1)}, bf16[128,768]{1,0:T(8,128)(2,1)}, bf16[128,384]...) custom-call(s32[1]{0:T(128)} %bitcast.10.refs_0_.member_ref.refs_3_,, ...), custom_call_target="tpu_custom_call" | custom-call | flops 1 | bytes 1 | tf_op jit(solution)/shard_map/pack/pallas_call | solution.py:168
  8.5 2.2 %collective-permute-done.2 = bf16[128,384]{1,0:T(8,128)(2,1)S(1)} collective-permute-done((bf16[128,384]{1,0:T(8,128)(2,1)}, bf16[128,384]{1,0:T(8,128)(2,1)S(1)}, u32[]{:S(2)}, u32[]{:S(2)}) %collective-permute-start.2) | collective-permute-done | bytes 98336 | tf_op jit(solution)/shard_map/ppermute | solution.py:474
  14.7 5.4 %all-to-all-start.2 = ((s32[16,1,128]{2,1,0:T(1,128)}), s32[16,1,128]{2,1,0:T(1,128)S(1)}, u32[]{:S(2)}, u32[]{:S(2)}) async-start(s32[16,1,128]{2,1,0:T(1,128)} %bitcast.8), calls=%async_computation.2 | async-start | bytes 16384 | tf_op jit(solution)/shard_map/all_to_all | solution.py:138
  20.2 4.5 %all-to-all-done.2 = s32[16,1,128]{2,1,0:T(1,128)S(1)} async-done(((s32[16,1,128]{2,1,0:T(1,128)}), s32[16,1,128]{2,1,0:T(1,128)S(1)}, u32[]{:S(2)}, u32[]{:S(2)}) %all-to-all-start.2) | async-done | bytes 8224 | tf_op jit(solution)/shard_map/all_to_all | solution.py:138
  25.1 7.8 %gather_fusion.2 = bf16[512,1024]{1,0:T(8,128)(2,1)} fusion(bf16[4000,1024]{1,0:T(8,128)(2,1)} %param.14, s32[1024]{0:T(1024)S(1)} %pad_clamp_fusion.3), kind=kCustom, calls=%fused_computation.2 | custom fusion | bytes 2099200 | tf_op jit(solution)/shard_map/jit(_take)/gather | solution.py:115
  33.1 7.7 %collective-permute-done.5.refs_5_ = bf16[512,384]{1,0:T(8,128)(2,1)S(1)} collective-permute-done((bf16[512,384]{1,0:T(8,128)(2,1)S(1)}, bf16[512,384]{1,0:T(8,128)(2,1)S(1)}, u32[]{:S(2)}, u32[]{:S(2)}) %collective-permute-start.5) | collective-permute-done | bytes 393248 | tf_op jit(solution)/shard_map/ppermute | solution.py:468
  41.5 6.8 %all-to-all-start.3 = ((bf16[16,32,1024]{2,1,0:T(8,128)(2,1)}), bf16[16,32,1024]{2,1,0:T(8,128)(2,1)S(1)}, u32[]{:S(2)}, u32[]{:S(2)}) async-start(bf16[16,32,1024]{2,1,0:T(8,128)(2,1)} %bitcast.13), calls=%async_computation.3 | async-start | bytes 2097152 | tf_op jit(solution)/shard_map/all_to_all | solution.py:138
  51.5 10.7 %collective-permute-done.8 = bf16[128,768]{1,0:T(8,128)(2,1)S(1)} collective-permute-done((bf16[128,768]{1,0:T(8,128)(2,1)S(1)}, bf16[128,768]{1,0:T(8,128)(2,1)S(1)}, u32[]{:S(2)}, u32[]{:S(2)}) %collective-permute-start.8) | collective-permute-done | bytes 196640 | tf_op jit(solution)/shard_map/ppermute | solution.py:474
  62.2 6.5 %collective-permute-done.7 = bf16[128,768]{1,0:T(8,128)(2,1)S(1)} collective-permute-done((bf16[128,768]{1,0:T(8,128)(2,1)S(1)}, bf16[128,768]{1,0:T(8,128)(2,1)S(1)}, u32[]{:S(2)}, u32[]{:S(2)}) %collective-permute-start.7) | collective-permute-done | bytes 196640 | tf_op jit(solution)/shard_map/ppermute | solution.py:474
  68.8 4.4 %all-to-all-done.3 = bf16[16,32,1024]{2,1,0:T(8,128)(2,1)S(1)} async-done(((bf16[16,32,1024]{2,1,0:T(8,128)(2,1)}), bf16[16,32,1024]{2,1,0:T(8,128)(2,1)S(1)}, u32[]{:S(2)}, u32[]{:S(2)}) %all-to-all-start.3) | async-done | bytes 1048608 | tf_op jit(solution)/shard_map/all_to_all | solution.py:138
  79.0 9.8 %collective-permute-done.9.own_far_ref = bf16[256,1024]{1,0:T(8,128)(2,1)S(1)} collective-permute-done((bf16[256,1024]{1,0:T(8,128)(2,1)S(1)}, bf16[256,1024]{1,0:T(8,128)(2,1)S(1)}, u32[]{:S(2)}, u32[]{:S(2)}) %collective-permute-start.9) | collective-permute-done | bytes 524320 | tf_op jit(solution)/shard_map/ppermute | solution.py:492
  91.4 1.8 collective-permute-start.15
  94.3 13.6 %collective-permute-done.15 = bf16[128,384]{1,0:T(8,128)(2,1)S(1)} collective-permute-done((bf16[128,384]{1,0:T(8,128)(2,1)S(1)}, bf16[128,384]{1,0:T(8,128)(2,1)S(1)}, u32[]{:S(2)}, u32[]{:S(2)}) %collective-permute-start.15) | collective-permute-done | bytes 98336 | tf_op jit(solution)/shard_map/ppermute | solution.py:474
  109.3 4.9 %norm.1.refs_1_ = bf16[2,256,2048]{2,1,0:T(8,128)(2,1)} custom-call(s32[1]{0:T(128)} %bitcast.12.low_ref, s32[1]{0:T(128)} %bitcast.10.refs_0_.member_ref.refs_3_, bf16[256,1024]{1,0:T(8,128)(2,1)S(1)} %get-tuple-element.350.own_ref, bf16[256,1024]{1,0:T(8,128)(2,1)} %copy-done.14, bf16[256,1024]{1,0:T(8,128)(2,1)} %copy-done.15, ...), custom_call_target="tpu_custom_call" | custom-call | flops 1 | bytes 1 | tf_op jit(solution)/shard_map/norm/pallas_call | solution.py:218
  114.5 4.1 %collective-permute-done.17.refs_2_ = bf16[2,256,2048]{2,1,0:T(8,128)(2,1)S(1)} collective-permute-done((bf16[2,256,2048]{2,1,0:T(8,128)(2,1)}, bf16[2,256,2048]{2,1,0:T(8,128)(2,1)S(1)}, u32[]{:S(2)}, u32[]{:S(2)}) %collective-permute-start.17) | collective-permute-done | bytes 2097184 | tf_op jit(solution)/shard_map/ppermute | solution.py:474
  120.0 5.7 %project.3 = (bf16[256,384]{1,0:T(8,128)(2,1)}, bf16[256,384]{1,0:T(8,128)(2,1)}, bf16[256,384]{1,0:T(8,128)(2,1)}, bf16[256,384]{1,0:T(8,128)(2,1)}) custom-call(s32[1]{0:T(128)} %bitcast.11.refs_0_, bf16[2,256,2048]{2,1,0:T(8,128)(2,1)} %norm.1.refs_1_, bf16[2,256,2048]{2,1,0:T(8,128)(2,1)} %copy-done, bf16[512,384]{1,0:T(8,128)(2,1)} %copy-done.13, ...), custom_call_target="tpu_custom_call" | custom-call | flops 1 | bytes 1 | tf_op jit(solution)/shard_map/project/pallas_call | solution.py:273
  127.9 5.7 %collective-permute-done.21.refs_5_ = bf16[512,768]{1,0:T(8,128)(2,1)S(1)} collective-permute-done((bf16[512,768]{1,0:T(8,128)(2,1)}, bf16[512,768]{1,0:T(8,128)(2,1)S(1)}, u32[]{:S(2)}, u32[]{:S(2)}) %collective-permute-start.21) | collective-permute-done | bytes 786464 | tf_op jit(solution)/shard_map/ppermute | solution.py:468
  133.6 3.3 %collective-permute-done.20.refs_7_ = bf16[256,384]{1,0:T(8,128)(2,1)S(1)} collective-permute-done((bf16[256,384]{1,0:T(8,128)(2,1)}, bf16[256,384]{1,0:T(8,128)(2,1)S(1)}, u32[]{:S(2)}, u32[]{:S(2)}) %collective-permute-start.20) | collective-permute-done | bytes 196640 | tf_op jit(solution)/shard_map/ppermute | solution.py:474
  139.1 7.6 %project.4 = (bf16[256,768]{1,0:T(8,128)(2,1)}, bf16[256,768]{1,0:T(8,128)(2,1)}, bf16[256,768]{1,0:T(8,128)(2,1)}, bf16[256,768]{1,0:T(8,128)(2,1)}) custom-call(s32[1]{0:T(128)} %bitcast.11.refs_0_, bf16[2,256,2048]{2,1,0:T(8,128)(2,1)} %norm.1.refs_1_, bf16[2,256,2048]{2,1,0:T(8,128)(2,1)} %copy-done, bf16[512,768]{1,0:T(8,128)(2,1)} %copy-done.5, ...), custom_call_target="tpu_custom_call" | custom-call | flops 1 | bytes 1 | tf_op jit(solution)/shard_map/project/pallas_call | solution.py:273
  146.7 1.9 collective-permute-done.22.refs_4_
  152.0 6.0 %retain.7 = (bf16[16,16,512]{2,1,0:T(8,128)(2,1)}, bf16[16,4,256,512]{3,2,1,0:T(8,128)(2,1)}) custom-call(s32[16]{0:T(128)} %copy-done.27, s32[16]{0:T(128)} %refs_1_.15, f32[4]{0:T(128)} %negate_log-plus-one_fusion.refs_2_, s32[1]{0:T(128)} %bitcast.10.refs_0_.member_ref.refs_3_, bf16[256,384]{1,0:T(8,128)(2,1)} %get-tuple-element.379.refs_4_, ...), custom_call_target="tpu_custom_call" | custom-call | flops 1 | bytes 1 | tf_op jit(solution)/shard_map/retain/pallas_call | solution.py:368
  158.0 7.8 %all-to-all-start.4 = ((bf16[16,16,512]{2,1,0:T(8,128)(2,1)}), bf16[16,16,512]{2,1,0:T(8,128)(2,1)S(1)}, u32[]{:S(2)}, u32[]{:S(2)}) async-start(bf16[16,16,512]{2,1,0:T(8,128)(2,1)} %get-tuple-element.383), calls=%async_computation.4 | async-start | bytes 524288 | tf_op jit(solution)/shard_map/all_to_all | solution.py:138
  166.6 5.8 %project.5 = (bf16[256,384]{1,0:T(8,128)(2,1)}, bf16[256,384]{1,0:T(8,128)(2,1)}, bf16[256,384]{1,0:T(8,128)(2,1)}, bf16[256,384]{1,0:T(8,128)(2,1)}) custom-call(s32[1]{0:T(128)} %bitcast.11.refs_0_, bf16[2,256,2048]{2,1,0:T(8,128)(2,1)} %norm.1.refs_1_, bf16[2,256,2048]{2,1,0:T(8,128)(2,1)} %copy-done, bf16[512,384]{1,0:T(8,128)(2,1)} %copy-done.6, ...), custom_call_target="tpu_custom_call" | custom-call | flops 1 | bytes 1 | tf_op jit(solution)/shard_map/project/pallas_call | solution.py:273
  174.7 4.6 %retain.8.refs_9_ = bf16[16,16,1536]{2,1,0:T(8,128)(2,1)} custom-call(s32[16]{0:T(128)} %copy-done.27, s32[16]{0:T(128)} %refs_1_.15, f32[4]{0:T(128)} %negate_log-plus-one_fusion.refs_2_, s32[1]{0:T(128)} %bitcast.10.refs_0_.member_ref.refs_3_, bf16[256,768]{1,0:T(8,128)(2,1)} %get-tuple-element.415.refs_4_, bf16[256,768]{1,0:T(8,128)(2,1)} %copy-done.1, ...), custom_call_target="tpu_custom_call" | custom-call | flops 1 | bytes 1 | tf_op jit(solution)/shard_map/retain/pallas_call | solution.py:368
  179.3 4.6 %retain.9.refs_9_ = bf16[16,16,1536]{2,1,0:T(8,128)(2,1)} custom-call(s32[16]{0:T(128)} %copy-done.27, s32[16]{0:T(128)} %refs_1_.15, f32[4]{0:T(128)} %negate_log-plus-one_fusion.refs_2_, s32[1]{0:T(128)} %bitcast.10.refs_0_.member_ref.refs_3_, bf16[256,768]{1,0:T(8,128)(2,1)} %get-tuple-element.415.refs_4_, ...), custom_call_target="tpu_custom_call", output_to_operand_aliasing={{}: (9, {})} | custom-call | flops 1 | bytes 1 | tf_op jit(solution)/shard_map/retain/pallas_call | solution.py:368
  185.3 4.6 %retain.10 = bf16[16,16,1536]{2,1,0:T(8,128)(2,1)} custom-call(s32[16]{0:T(128)} %copy-done.27, s32[16]{0:T(128)} %refs_1_.15, f32[4]{0:T(128)} %negate_log-plus-one_fusion.refs_2_, s32[1]{0:T(128)} %bitcast.10.refs_0_.member_ref.refs_3_, bf16[256,384]{1,0:T(8,128)(2,1)} %get-tuple-element.411.refs_4_, ...), custom_call_target="tpu_custom_call", output_to_operand_aliasing={{}: (9, {})} | custom-call | flops 1 | bytes 1 | tf_op jit(solution)/shard_map/retain/pallas_call | solution.py:368
  190.0 6.1 %all-to-all-start.5 = ((bf16[16,16,1536]{2,1,0:T(8,128)(2,1)}), bf16[16,16,1536]{2,1,0:T(8,128)(2,1)S(1)}, u32[]{:S(2)}, u32[]{:S(2)}) async-start(bf16[16,16,1536]{2,1,0:T(8,128)(2,1)} %retain.10), calls=%async_computation.5 | async-start | bytes 1572864 | tf_op jit(solution)/shard_map/all_to_all | solution.py:138
  196.0 5.4 %retain.11.refs_9_ = bf16[16,4,256,512]{3,2,1,0:T(8,128)(2,1)} custom-call(s32[16]{0:T(128)} %copy-done.27, s32[16]{0:T(128)} %refs_1_.15, f32[4]{0:T(128)} %negate_log-plus-one_fusion.refs_2_, s32[1]{0:T(128)} %bitcast.10.refs_0_.member_ref.refs_3_, bf16[256,768]{1,0:T(8,128)(2,1)} %get-tuple-element.415.refs_4_, ...), custom_call_target="tpu_custom_call", output_to_operand_aliasing={{}: (9, {})} | custom-call | flops 1 | bytes 1 | tf_op jit(solution)/shard_map/retain/pallas_call | solution.py:368
  201.4 5.4 %retain.12.refs_9_ = bf16[16,4,256,512]{3,2,1,0:T(8,128)(2,1)} custom-call(s32[16]{0:T(128)} %copy-done.27, s32[16]{0:T(128)} %refs_1_.15, f32[4]{0:T(128)} %negate_log-plus-one_fusion.refs_2_, s32[1]{0:T(128)} %bitcast.10.refs_0_.member_ref.refs_3_, bf16[256,768]{1,0:T(8,128)(2,1)} %get-tuple-element.415.refs_4_, ...), custom_call_target="tpu_custom_call", output_to_operand_aliasing={{}: (9, {})} | custom-call | flops 1 | bytes 1 | tf_op jit(solution)/shard_map/retain/pallas_call | solution.py:368
  206.8 5.4 %retain.13 = bf16[16,4,256,512]{3,2,1,0:T(8,128)(2,1)} custom-call(s32[16]{0:T(128)} %copy-done.27, s32[16]{0:T(128)} %refs_1_.15, f32[4]{0:T(128)} %negate_log-plus-one_fusion.refs_2_, s32[1]{0:T(128)} %bitcast.10.refs_0_.member_ref.refs_3_, bf16[256,384]{1,0:T(8,128)(2,1)} %get-tuple-element.411.refs_4_, ...), custom_call_target="tpu_custom_call", output_to_operand_aliasing={{}: (9, {})} | custom-call | flops 1 | bytes 1 | tf_op jit(solution)/shard_map/retain/pallas_call | solution.py:368
  212.1 3.5 %all-to-all-done.5.refs_2_ = bf16[16,16,1536]{2,1,0:T(8,128)(2,1)S(1)} async-done(((bf16[16,16,1536]{2,1,0:T(8,128)(2,1)}), bf16[16,16,1536]{2,1,0:T(8,128)(2,1)S(1)}, u32[]{:S(2)}, u32[]{:S(2)}) %all-to-all-start.5) | async-done | bytes 786464 | tf_op jit(solution)/shard_map/all_to_all | solution.py:138
  216.5 2.9 %settle.1 = bf16[16,16,2048]{2,1,0:T(8,128)(2,1)} custom-call(s32[16]{0:T(128)} %get-tuple-element.421.refs_0_, bf16[16,16,512]{2,1,0:T(8,128)(2,1)} %copy-done.7, bf16[16,16,1536]{2,1,0:T(8,128)(2,1)} %copy-done.4), custom_call_target="tpu_custom_call" | custom-call | flops 1 | bytes 1 | tf_op jit(solution)/shard_map/settle/pallas_call | solution.py:404
  (154 shorter events, 38.7 us)
Async XLA Ops:
  3.3 5.2 %collective-permute-start = (bf16[128,384]{1,0:T(8,128)(2,1)}, bf16[128,384]{1,0:T(8,128)(2,1)S(1)}, u32[]{:S(2)}, u32[]{:S(2)}) collective-permute-start(bf16[128,384]{1,0:T(8,128)(2,1)} %get-tuple-element.338), channel_id=1, source_target_pairs={{0,2},{2,0},{4,6},{6,4},{8,10},{10,8},{12,14},{14,12},{16,18},{18,... | collective-permute-start | bytes 294920 | tf_op jit(solution)/shard_map/ppermute | solution.py:474
  5.1 5.6 %collective-permute-start.2 = (bf16[128,384]{1,0:T(8,128)(2,1)}, bf16[128,384]{1,0:T(8,128)(2,1)S(1)}, u32[]{:S(2)}, u32[]{:S(2)}) collective-permute-start(bf16[128,384]{1,0:T(8,128)(2,1)} %get-tuple-element.340), channel_id=1, source_target_pairs={{0,6},{2,4},{4,2},{6,0},{8,14},{10,12},{12,10},{14,8},{16,22},{18,... | collective-permute-start | bytes 294920 | tf_op jit(solution)/shard_map/ppermute | solution.py:474
  10.8 13.9 %collective-permute-start.4 = (bf16[512,384]{1,0:T(8,128)(2,1)S(1)}, bf16[512,384]{1,0:T(8,128)(2,1)S(1)}, u32[]{:S(2)}, u32[]{:S(2)}) collective-permute-start(bf16[512,384]{1,0:T(8,128)(2,1)S(1)} %constant_dynamic-update-slice_fusion.refs_3_), channel_id=1, source_target_pairs={{0,8},{2,10},{4,12},{6,14},{8,16},{10,18},{12,20},{14,22},{16,24},... | collective-permute-start | bytes 1179656 | tf_op jit(solution)/shard_map/ppermute | solution.py:468
  14.7 10.0 %all-to-all-start.2 = ((s32[16,1,128]{2,1,0:T(1,128)}), s32[16,1,128]{2,1,0:T(1,128)S(1)}, u32[]{:S(2)}, u32[]{:S(2)}) async-start(s32[16,1,128]{2,1,0:T(1,128)} %bitcast.8), calls=%async_computation.2 | async-start | bytes 16384 | tf_op jit(solution)/shard_map/all_to_all | solution.py:138
  20.1 12.9 %collective-permute-start.3 = (bf16[512,384]{1,0:T(8,128)(2,1)S(1)}, bf16[512,384]{1,0:T(8,128)(2,1)S(1)}, u32[]{:S(2)}, u32[]{:S(2)}) collective-permute-start(bf16[512,384]{1,0:T(8,128)(2,1)S(1)} %constant_dynamic-update-slice_fusion.refs_3_), channel_id=1, source_target_pairs={{0,24},{2,26},{4,28},{6,30},{8,0},{10,2},{12,4},{14,6},{16,8},{18,... | collective-permute-start | bytes 1179656 | tf_op jit(solution)/shard_map/ppermute | solution.py:471
  24.7 16.0 %collective-permute-start.5 = (bf16[512,384]{1,0:T(8,128)(2,1)S(1)}, bf16[512,384]{1,0:T(8,128)(2,1)S(1)}, u32[]{:S(2)}, u32[]{:S(2)}) collective-permute-start(bf16[512,384]{1,0:T(8,128)(2,1)S(1)} %collective-permute-done.4.refs_4_), channel_id=1, source_target_pairs={{0,8},{2,10},{4,12},{6,14},{8,16},{10,18},{12,20},{14,22},{16,24},... | collective-permute-start | bytes 1179656 | tf_op jit(solution)/shard_map/ppermute | solution.py:468
  41.5 31.6 %all-to-all-start.3 = ((bf16[16,32,1024]{2,1,0:T(8,128)(2,1)}), bf16[16,32,1024]{2,1,0:T(8,128)(2,1)S(1)}, u32[]{:S(2)}, u32[]{:S(2)}) async-start(bf16[16,32,1024]{2,1,0:T(8,128)(2,1)} %bitcast.13), calls=%async_computation.3 | async-start | bytes 2097152 | tf_op jit(solution)/shard_map/all_to_all | solution.py:138
  48.3 13.9 %collective-permute-start.8 = (bf16[128,768]{1,0:T(8,128)(2,1)S(1)}, bf16[128,768]{1,0:T(8,128)(2,1)S(1)}, u32[]{:S(2)}, u32[]{:S(2)}) collective-permute-start(bf16[128,768]{1,0:T(8,128)(2,1)S(1)} %copy-done.30), channel_id=1, source_target_pairs={{0,6},{2,4},{4,2},{6,0},{8,14},{10,12},{12,10},{14,8},{16,22},{18,... | collective-permute-start | bytes 589832 | tf_op jit(solution)/shard_map/ppermute | solution.py:474
  49.8 18.9 %collective-permute-start.7 = (bf16[128,768]{1,0:T(8,128)(2,1)S(1)}, bf16[128,768]{1,0:T(8,128)(2,1)S(1)}, u32[]{:S(2)}, u32[]{:S(2)}) collective-permute-start(bf16[128,768]{1,0:T(8,128)(2,1)S(1)} %copy-done.29), channel_id=1, source_target_pairs={{0,4},{2,6},{4,0},{6,2},{8,12},{10,14},{12,8},{14,10},{16,20},{18,... | collective-permute-start | bytes 589832 | tf_op jit(solution)/shard_map/ppermute | solution.py:474
  50.1 18.6 %collective-permute-start.6 = (bf16[128,768]{1,0:T(8,128)(2,1)S(1)}, bf16[128,768]{1,0:T(8,128)(2,1)S(1)}, u32[]{:S(2)}, u32[]{:S(2)}) collective-permute-start(bf16[128,768]{1,0:T(8,128)(2,1)S(1)} %copy-done.28), channel_id=1, source_target_pairs={{0,2},{2,0},{4,6},{6,4},{8,10},{10,8},{12,14},{14,12},{16,18},{18,... | collective-permute-start | bytes 589832 | tf_op jit(solution)/shard_map/ppermute | solution.py:474
  75.0 13.8 %collective-permute-start.9 = (bf16[256,1024]{1,0:T(8,128)(2,1)S(1)}, bf16[256,1024]{1,0:T(8,128)(2,1)S(1)}, u32[]{:S(2)}, u32[]{:S(2)}) collective-permute-start(bf16[256,1024]{1,0:T(8,128)(2,1)S(1)} %get-tuple-element.350.own_ref), channel_id=1, source_target_pairs={{0,1},{1,0},{2,3},{3,2},{4,5},{5,4},{6,7},{7,6},{8,9},{9,8},{10,11... | collective-permute-start | bytes 1572872 | tf_op jit(solution)/shard_map/ppermute | solution.py:492
  76.4 13.5 %collective-permute-start.10 = (bf16[256,1024]{1,0:T(8,128)(2,1)S(1)}, bf16[256,1024]{1,0:T(8,128)(2,1)S(1)}, u32[]{:S(2)}, u32[]{:S(2)}) collective-permute-start(bf16[256,1024]{1,0:T(8,128)(2,1)S(1)} %get-tuple-element.350.own_ref), channel_id=1, source_target_pairs={{0,4},{2,6},{4,0},{6,2},{8,12},{10,14},{12,8},{14,10},{16,20},{18,... | collective-permute-start | bytes 1572872 | tf_op jit(solution)/shard_map/ppermute | solution.py:474
  77.6 31.7 %collective-permute-start.12 = (bf16[512,768]{1,0:T(8,128)(2,1)S(1)}, bf16[512,768]{1,0:T(8,128)(2,1)S(1)}, u32[]{:S(2)}, u32[]{:S(2)}) collective-permute-start(bf16[512,768]{1,0:T(8,128)(2,1)S(1)} %pad_maximum_fusion.refs_3_), channel_id=1, source_target_pairs={{0,8},{2,10},{4,12},{6,14},{8,16},{10,18},{12,20},{14,22},{16,24},... | collective-permute-start | bytes 2359304 | tf_op jit(solution)/shard_map/ppermute | solution.py:468
  77.6 36.6 %collective-permute-start.16 = (bf16[512,768]{1,0:T(8,128)(2,1)S(1)}, bf16[512,768]{1,0:T(8,128)(2,1)}, u32[]{:S(2)}, u32[]{:S(2)}) collective-permute-start(bf16[512,768]{1,0:T(8,128)(2,1)S(1)} %pad_maximum_fusion.refs_3_), channel_id=1, source_target_pairs={{0,24},{2,26},{4,28},{6,30},{8,0},{10,2},{12,4},{14,6},{16,8},{18,... | collective-permute-start | bytes 2359304 | tf_op jit(solution)/shard_map/ppermute | solution.py:471
  90.7 18.6 %collective-permute-start.11 = (bf16[256,1024]{1,0:T(8,128)(2,1)S(1)}, bf16[256,1024]{1,0:T(8,128)(2,1)}, u32[]{:S(2)}, u32[]{:S(2)}) collective-permute-start(bf16[256,1024]{1,0:T(8,128)(2,1)S(1)} %collective-permute-done.9.own_far_ref), channel_id=1, source_target_pairs={{0,4},{2,6},{4,0},{6,2},{8,12},{10,14},{12,8},{14,10},{16,20},{18,... | collective-permute-start | bytes 1572872 | tf_op jit(solution)/shard_map/ppermute | solution.py:474
  91.4 16.5 %collective-permute-start.15 = (bf16[128,384]{1,0:T(8,128)(2,1)S(1)}, bf16[128,384]{1,0:T(8,128)(2,1)S(1)}, u32[]{:S(2)}, u32[]{:S(2)}) collective-permute-start(bf16[128,384]{1,0:T(8,128)(2,1)S(1)} %copy-done.33), channel_id=1, source_target_pairs={{0,6},{2,4},{4,2},{6,0},{8,14},{10,12},{12,10},{14,8},{16,22},{18,... | collective-permute-start | bytes 294920 | tf_op jit(solution)/shard_map/ppermute | solution.py:474
  93.2 14.8 %collective-permute-start.14 = (bf16[128,384]{1,0:T(8,128)(2,1)S(1)}, bf16[128,384]{1,0:T(8,128)(2,1)S(1)}, u32[]{:S(2)}, u32[]{:S(2)}) collective-permute-start(bf16[128,384]{1,0:T(8,128)(2,1)S(1)} %copy-done.32), channel_id=1, source_target_pairs={{0,4},{2,6},{4,0},{6,2},{8,12},{10,14},{12,8},{14,10},{16,20},{18,... | collective-permute-start | bytes 294920 | tf_op jit(solution)/shard_map/ppermute | solution.py:474
  114.4 19.2 %collective-permute-start.21 = (bf16[512,768]{1,0:T(8,128)(2,1)}, bf16[512,768]{1,0:T(8,128)(2,1)S(1)}, u32[]{:S(2)}, u32[]{:S(2)}) collective-permute-start(bf16[512,768]{1,0:T(8,128)(2,1)} %copy-done.11), channel_id=1, source_target_pairs={{0,8},{2,10},{4,12},{6,14},{8,16},{10,18},{12,20},{14,22},{16,24},... | collective-permute-start | bytes 2359304 | tf_op jit(solution)/shard_map/ppermute | solution.py:468
  125.7 7.9 %collective-permute-start.18 = (bf16[256,384]{1,0:T(8,128)(2,1)}, bf16[256,384]{1,0:T(8,128)(2,1)S(1)}, u32[]{:S(2)}, u32[]{:S(2)}) collective-permute-start(bf16[256,384]{1,0:T(8,128)(2,1)} %get-tuple-element.363), channel_id=1, source_target_pairs={{0,2},{2,0},{4,6},{6,4},{8,10},{10,8},{12,14},{14,12},{16,18},{18,... | collective-permute-start | bytes 589832 | tf_op jit(solution)/shard_map/ppermute | solution.py:474
  125.9 7.7 %collective-permute-start.19 = (bf16[256,384]{1,0:T(8,128)(2,1)}, bf16[256,384]{1,0:T(8,128)(2,1)S(1)}, u32[]{:S(2)}, u32[]{:S(2)}) collective-permute-start(bf16[256,384]{1,0:T(8,128)(2,1)} %get-tuple-element.364), channel_id=1, source_target_pairs={{0,4},{2,6},{4,0},{6,2},{8,12},{10,14},{12,8},{14,10},{16,20},{18,... | collective-permute-start | bytes 589832 | tf_op jit(solution)/shard_map/ppermute | solution.py:474
  126.5 10.4 %collective-permute-start.20 = (bf16[256,384]{1,0:T(8,128)(2,1)}, bf16[256,384]{1,0:T(8,128)(2,1)S(1)}, u32[]{:S(2)}, u32[]{:S(2)}) collective-permute-start(bf16[256,384]{1,0:T(8,128)(2,1)} %get-tuple-element.365), channel_id=1, source_target_pairs={{0,6},{2,4},{4,2},{6,0},{8,14},{10,12},{12,10},{14,8},{16,22},{18,... | collective-permute-start | bytes 589832 | tf_op jit(solution)/shard_map/ppermute | solution.py:474
  137.6 11.0 %collective-permute-start.22 = (bf16[512,384]{1,0:T(8,128)(2,1)S(1)}, bf16[512,384]{1,0:T(8,128)(2,1)S(1)}, u32[]{:S(2)}, u32[]{:S(2)}) collective-permute-start(bf16[512,384]{1,0:T(8,128)(2,1)S(1)} %pad_maximum_fusion.1.refs_3_), channel_id=1, source_target_pairs={{0,8},{2,10},{4,12},{6,14},{8,16},{10,18},{12,20},{14,22},{16,24},... | collective-permute-start | bytes 1179656 | tf_op jit(solution)/shard_map/ppermute | solution.py:468
  137.7 28.0 %collective-permute-start.25 = (bf16[512,384]{1,0:T(8,128)(2,1)S(1)}, bf16[512,384]{1,0:T(8,128)(2,1)}, u32[]{:S(2)}, u32[]{:S(2)}) collective-permute-start(bf16[512,384]{1,0:T(8,128)(2,1)S(1)} %pad_maximum_fusion.1.refs_3_), channel_id=1, source_target_pairs={{0,24},{2,26},{4,28},{6,30},{8,0},{10,2},{12,4},{14,6},{16,8},{18,... | collective-permute-start | bytes 1179656 | tf_op jit(solution)/shard_map/ppermute | solution.py:471
  148.6 23.8 %collective-permute-start.23 = (bf16[256,768]{1,0:T(8,128)(2,1)}, bf16[256,768]{1,0:T(8,128)(2,1)S(1)}, u32[]{:S(2)}, u32[]{:S(2)}) collective-permute-start(bf16[256,768]{1,0:T(8,128)(2,1)} %get-tuple-element.385), channel_id=1, source_target_pairs={{0,2},{2,0},{4,6},{6,4},{8,10},{10,8},{12,14},{14,12},{16,18},{18,... | collective-permute-start | bytes 1179656 | tf_op jit(solution)/shard_map/ppermute | solution.py:474
  149.4 16.4 %collective-permute-start.24 = (bf16[256,768]{1,0:T(8,128)(2,1)}, bf16[256,768]{1,0:T(8,128)(2,1)S(1)}, u32[]{:S(2)}, u32[]{:S(2)}) collective-permute-start(bf16[256,768]{1,0:T(8,128)(2,1)} %get-tuple-element.387), channel_id=1, source_target_pairs={{0,4},{2,6},{4,0},{6,2},{8,12},{10,14},{12,8},{14,10},{16,20},{18,... | collective-permute-start | bytes 1179656 | tf_op jit(solution)/shard_map/ppermute | solution.py:474
  150.1 15.7 %collective-permute-start.26 = (bf16[512,384]{1,0:T(8,128)(2,1)S(1)}, bf16[512,384]{1,0:T(8,128)(2,1)S(1)}, u32[]{:S(2)}, u32[]{:S(2)}) collective-permute-start(bf16[512,384]{1,0:T(8,128)(2,1)S(1)} %collective-permute-done.22.refs_4_), channel_id=1, source_target_pairs={{0,8},{2,10},{4,12},{6,14},{8,16},{10,18},{12,20},{14,22},{16,24},... | collective-permute-start | bytes 1179656 | tf_op jit(solution)/shard_map/ppermute | solution.py:468
  150.1 22.4 %collective-permute-start.27 = (bf16[256,768]{1,0:T(8,128)(2,1)}, bf16[256,768]{1,0:T(8,128)(2,1)S(1)}, u32[]{:S(2)}, u32[]{:S(2)}) collective-permute-start(bf16[256,768]{1,0:T(8,128)(2,1)} %get-tuple-element.390), channel_id=1, source_target_pairs={{0,6},{2,4},{4,2},{6,0},{8,14},{10,12},{12,10},{14,8},{16,22},{18,... | collective-permute-start | bytes 1179656 | tf_op jit(solution)/shard_map/ppermute | solution.py:474
  158.0 32.0 %all-to-all-start.4 = ((bf16[16,16,512]{2,1,0:T(8,128)(2,1)}), bf16[16,16,512]{2,1,0:T(8,128)(2,1)S(1)}, u32[]{:S(2)}, u32[]{:S(2)}) async-start(bf16[16,16,512]{2,1,0:T(8,128)(2,1)} %get-tuple-element.383), calls=%async_computation.4 | async-start | bytes 524288 | tf_op jit(solution)/shard_map/all_to_all | solution.py:138
  172.4 11.5 %collective-permute-start.28 = (bf16[256,384]{1,0:T(8,128)(2,1)}, bf16[256,384]{1,0:T(8,128)(2,1)S(1)}, u32[]{:S(2)}, u32[]{:S(2)}) collective-permute-start(bf16[256,384]{1,0:T(8,128)(2,1)} %get-tuple-element.402), channel_id=1, source_target_pairs={{0,2},{2,0},{4,6},{6,4},{8,10},{10,8},{12,14},{14,12},{16,18},{18,... | collective-permute-start | bytes 589832 | tf_op jit(solution)/shard_map/ppermute | solution.py:474
  172.9 11.0 %collective-permute-start.29 = (bf16[256,384]{1,0:T(8,128)(2,1)}, bf16[256,384]{1,0:T(8,128)(2,1)S(1)}, u32[]{:S(2)}, u32[]{:S(2)}) collective-permute-start(bf16[256,384]{1,0:T(8,128)(2,1)} %get-tuple-element.403), channel_id=1, source_target_pairs={{0,4},{2,6},{4,0},{6,2},{8,12},{10,14},{12,8},{14,10},{16,20},{18,... | collective-permute-start | bytes 589832 | tf_op jit(solution)/shard_map/ppermute | solution.py:474
  174.1 9.9 %collective-permute-start.30 = (bf16[256,384]{1,0:T(8,128)(2,1)}, bf16[256,384]{1,0:T(8,128)(2,1)S(1)}, u32[]{:S(2)}, u32[]{:S(2)}) collective-permute-start(bf16[256,384]{1,0:T(8,128)(2,1)} %get-tuple-element.404), channel_id=1, source_target_pairs={{0,6},{2,4},{4,2},{6,0},{8,14},{10,12},{12,10},{14,8},{16,22},{18,... | collective-permute-start | bytes 589832 | tf_op jit(solution)/shard_map/ppermute | solution.py:474
  190.0 25.7 %all-to-all-start.5 = ((bf16[16,16,1536]{2,1,0:T(8,128)(2,1)}), bf16[16,16,1536]{2,1,0:T(8,128)(2,1)S(1)}, u32[]{:S(2)}, u32[]{:S(2)}) async-start(bf16[16,16,1536]{2,1,0:T(8,128)(2,1)} %retain.10), calls=%async_computation.5 | async-start | bytes 1572864 | tf_op jit(solution)/shard_map/all_to_all | solution.py:138
  (37 other events, 414.5 us)
